TPU v7x, 32 devices: a whole 2x2x4 slice. The times are simulated.
32 devices in a mesh: seq: 4 (over z), fsdp: 4 (over y, x), rep: 2 (over core).
Axes of the slice: x: 2, y: 2, z: 4, core: 2. Of those that a mesh axis runs over, the one named last changes fastest.
Arguments:
- tokens: bfloat16 [16, 1024, 2048], P(('fsdp', 'rep'), 'seq'), may hold values from -6 to 6
- cotangent: bfloat16 [16, 1024, 2048], P(('fsdp', 'rep'), 'seq'), may hold values from -6 to 6
- piece_start: int32 [16], P(('fsdp', 'rep')), may hold values from 0 to 768, as said below
- attention_gain: bfloat16 [2048], P('fsdp'), may hold values from 0.099609375 to 1.8984375
- query_weight: bfloat16 [2048, 2048], P('fsdp'), may hold values from -0.1875 to 0.1875
- key_weight: bfloat16 [2048, 2048], P('fsdp'), may hold values from -0.125 to 0.125
- value_weight: bfloat16 [2048, 2048], P('fsdp'), may hold values from -0.125 to 0.125
- output_weight: bfloat16 [2048, 2048], P('fsdp'), may hold values from -3 to 3
- feedforward_gain: bfloat16 [2048], P('fsdp'), may hold values from 0.099609375 to 1.8984375
- gate_weight: bfloat16 [2048, 8192], P('fsdp'), may hold values from -0.125 to 0.125
- up_weight: bfloat16 [2048, 8192], P('fsdp'), may hold values from -0.125 to 0.125
- down_weight: bfloat16 [8192, 2048], P('fsdp'), may hold values from -0.0625 to 0.0625
Outputs:
- layer_output: bfloat16 [16, 1024, 2048], P(('fsdp', 'rep'), 'seq')
- input_gradient: bfloat16 [16, 1024, 2048], P(('fsdp', 'rep'), 'seq')
- attention_gain_gradient: float32 [2048], P('fsdp')
- query_weight_gradient: float32 [2048, 2048], P('fsdp')
- key_weight_gradient: float32 [2048, 2048], P('fsdp')
- value_weight_gradient: float32 [2048, 2048], P('fsdp')
- output_weight_gradient: float32 [2048, 2048], P('fsdp')
- feedforward_gain_gradient: float32 [2048], P('fsdp')
- gate_weight_gradient: float32 [2048, 8192], P('fsdp')
- up_weight_gradient: float32 [2048, 8192], P('fsdp')
- down_weight_gradient: float32 [8192, 2048], P('fsdp')
Inputs may be any that keep to these rules, and one draw needn't show every extreme that they name: `piece_start`: each sequence holds one picture piece of 256 positions starting here; in every draw some sequence starts it at 0 and some at 768.
All inputs are finite; a program needn't handle non-finite values.
Results may differ from a plain program's by a relative error of at most 0.02.
Values may be sent and summed in bfloat16 or wider, within the bound.
No kernel may reach another device: no remote copies, remote signals or barrier semaphores. Data moves between devices by JAX's collectives and lax.ppermute only.
A program may use at most 576 MiB of HBM per device.

v0:
```python
import jax
import jax.numpy as jnp
from jax import lax
from jax.sharding import PartitionSpec as P

HEADS = 32
HEAD_DIM = 64
PIECE = 256
HEAD_GROUP = 8


NORM_EPS = 1e-05
ROPE_BASE = 130000.0
MASKED_SCORE = -1e30


def matmul(left_op, right_op):
    return jnp.dot(left_op, right_op, preferred_element_type=jnp.float32)


def outer_sum(left_op, right_op):
    return lax.dot_general(
        left_op, right_op, (((0,), (0,)), ((), ())), preferred_element_type=jnp.float32
    )


def against(left_op, right_op):
    return lax.dot_general(
        left_op, right_op, (((1,), (1,)), ((), ())), preferred_element_type=jnp.float32
    )


def normed(activation, gain_vec):
    scaling = lax.rsqrt(jnp.mean(activation * activation, axis=-1, keepdims=True) + NORM_EPS)
    return activation * scaling * gain_vec


def rotary(activation, offset):
    row_count = activation.shape[0]
    half_dim = HEAD_DIM // 2
    places = (offset + jnp.arange(row_count, dtype=jnp.int32)).astype(jnp.float32)
    frequency = ROPE_BASE ** (-jnp.arange(half_dim, dtype=jnp.float32) / half_dim)
    angles = places[:, None] * frequency[None, :]
    cosine = jnp.cos(angles)[:, None, :]
    sine_part = jnp.sin(angles)[:, None, :]
    per_head = activation.reshape(row_count, HEADS, HEAD_DIM)
    front_half = per_head[..., :half_dim]
    back_half = per_head[..., half_dim:]
    turned = jnp.concatenate(
        [front_half * cosine - back_half * sine_part, back_half * cosine + front_half * sine_part],
        axis=-1,
    )
    return turned.reshape(row_count, HEADS * HEAD_DIM)


def visible(query_pos, key_pos, piece_at):
    causal = key_pos[None, :] <= query_pos[:, None]
    query_in = (query_pos >= piece_at) & (query_pos < piece_at + PIECE)
    key_in = (key_pos >= piece_at) & (key_pos < piece_at + PIECE)
    return causal | query_in[:, None] & key_in[None, :]


def gated(gate_proj, up_proj):
    return jax.nn.silu(gate_proj) * up_proj


def flatten(stacked):
    return stacked.reshape(-1, stacked.shape[-1])


def local(
    tokens,
    cotangent,
    piece_start,
    attention_gain,
    query_weight,
    key_weight,
    value_weight,
    output_weight,
    feedforward_gain,
    gate_weight,
    up_weight,
    down_weight,
):
    local_len = tokens.shape[1]
    features = tokens.shape[2]
    length = local_len * lax.axis_size("seq")
    offset = lax.axis_index("seq") * local_len
    query_pos = offset + jnp.arange(local_len, dtype=jnp.int32)
    key_pos = jnp.arange(length, dtype=jnp.int32)
    groups = HEADS // HEAD_GROUP
    span = HEAD_GROUP * HEAD_DIM
    gathered = (
        lax.all_gather(attention_gain, "fsdp", axis=0, tiled=True),
        lax.all_gather(query_weight, "fsdp", axis=0, tiled=True),
        lax.all_gather(key_weight, "fsdp", axis=0, tiled=True),
        lax.all_gather(value_weight, "fsdp", axis=0, tiled=True),
        lax.all_gather(output_weight, "fsdp", axis=0, tiled=True),
        lax.all_gather(feedforward_gain, "fsdp", axis=0, tiled=True),
        lax.all_gather(gate_weight, "fsdp", axis=0, tiled=True),
        lax.all_gather(up_weight, "fsdp", axis=0, tiled=True),
        lax.all_gather(down_weight, "fsdp", axis=0, tiled=True),
    )
    (
        gain_first,
        query_full,
        key_full,
        value_full,
        output_full,
        gain_second,
        gate_full,
        up_full,
        down_full,
    ) = gathered
    gain_first_f = gain_first.astype(jnp.float32)
    gain_second_f = gain_second.astype(jnp.float32)

    def heads_of(activation, group):
        portion = lax.dynamic_slice_in_dim(activation, group * span, span, 1)
        return portion.reshape(activation.shape[0], HEAD_GROUP, HEAD_DIM)

    def joined(stacked):
        return jnp.moveaxis(stacked, 0, 1).reshape(stacked.shape[1], features)

    def one_batch(gain_sums, inputs):
        rows_in, rows_back, piece_at = inputs
        activation = rows_in.astype(jnp.float32)
        first_float, norm_back_first = jax.vjp(normed, activation, gain_first_f)
        normed_first = first_float.astype(jnp.bfloat16)
        query_lin = matmul(normed_first, query_full)
        key_lin = matmul(normed_first, key_full)
        value_lin = matmul(normed_first, value_full)
        query_turned, rotate_query = jax.vjp(lambda activ: rotary(activ, offset), query_lin)
        key_turned, rotate_key = jax.vjp(lambda activ: rotary(activ, offset), key_lin)
        queries = query_turned.astype(jnp.bfloat16)
        keys_local = key_turned.astype(jnp.bfloat16)
        values_local = value_lin.astype(jnp.bfloat16)
        keys_all, values_all = (
            lax.all_gather(keys_local, "seq", axis=0, tiled=True),
            lax.all_gather(values_local, "seq", axis=0, tiled=True),
        )
        allowed = visible(query_pos, key_pos, piece_at)

        def scored(group, keys_src):
            scores = (
                jnp.einsum(
                    "qhd,khd->hqk",
                    heads_of(queries, group),
                    heads_of(keys_src, group),
                    preferred_element_type=jnp.float32,
                )
                * 0.125
            )
            return jnp.where(allowed[None], scores, MASKED_SCORE)

        def attend_forward(group):
            scores = scored(group, keys_all)
            row_max = jnp.max(scores, axis=-1, keepdims=True)
            log_total = (
                jnp.log(jnp.sum(jnp.exp(scores - row_max), axis=-1, keepdims=True)) + row_max
            )
            weights_soft = jnp.exp(scores - log_total).astype(jnp.bfloat16)
            mixture = jnp.einsum(
                "hqk,khd->qhd",
                weights_soft,
                heads_of(values_all, group),
                preferred_element_type=jnp.float32,
            )
            return (mixture.reshape(local_len, span), log_total[..., 0])

        mixture, log_totals = lax.map(attend_forward, jnp.arange(groups))
        attended = joined(mixture).astype(jnp.bfloat16)
        residual = activation + matmul(attended, output_full)
        second_float, norm_back_second = jax.vjp(normed, residual, gain_second_f)
        normed_second = second_float.astype(jnp.bfloat16)
        gate_proj = matmul(normed_second, gate_full)
        up_proj = matmul(normed_second, up_full)
        inner_float, gated_back = jax.vjp(gated, gate_proj, up_proj)
        inner_act = inner_float.astype(jnp.bfloat16)
        layer_rows = (residual + matmul(inner_act, down_full)).astype(jnp.bfloat16)
        keys_back, values_back = (
            lax.all_gather(keys_local, "seq", axis=0, tiled=True),
            lax.all_gather(values_local, "seq", axis=0, tiled=True),
        )
        output_rows = rows_back.astype(jnp.float32)
        inner_grad = against(rows_back, down_full)
        gate_grad_f, up_grad_f = gated_back(inner_grad)
        gate_grad = gate_grad_f.astype(jnp.bfloat16)
        up_grad = up_grad_f.astype(jnp.bfloat16)
        second_grad = against(gate_grad, gate_full) + against(up_grad, up_full)
        residual_part, gain_second_term = norm_back_second(second_grad)
        residual_grad = output_rows + residual_part
        branch_grad = residual_grad.astype(jnp.bfloat16)
        attended_grad = against(branch_grad, output_full).astype(jnp.bfloat16)

        def attend_backward(pair):
            group, log_total = pair
            scores = scored(group, keys_back)
            soft = jnp.exp(scores - log_total[..., None])
            value_heads = heads_of(values_back, group)
            grad_heads = heads_of(attended_grad, group)
            soft_grad = jnp.einsum(
                "qhd,khd->hqk", grad_heads, value_heads, preferred_element_type=jnp.float32
            )
            row_delta = jnp.sum(soft * soft_grad, axis=-1, keepdims=True)
            score_grad = (soft * (soft_grad - row_delta)).astype(jnp.bfloat16)
            query_part = (
                jnp.einsum(
                    "hqk,khd->qhd",
                    score_grad,
                    heads_of(keys_back, group),
                    preferred_element_type=jnp.float32,
                )
                * 0.125
            )
            key_part = (
                jnp.einsum(
                    "hqk,qhd->khd",
                    score_grad,
                    heads_of(queries, group),
                    preferred_element_type=jnp.float32,
                )
                * 0.125
            )
            value_part = jnp.einsum(
                "hqk,qhd->khd",
                soft.astype(jnp.bfloat16),
                grad_heads,
                preferred_element_type=jnp.float32,
            )
            return (
                query_part.reshape(local_len, span),
                key_part.reshape(length, span),
                value_part.reshape(length, span),
            )

        query_parts, key_parts, value_parts = lax.map(
            attend_backward, (jnp.arange(groups), log_totals)
        )
        query_grad = joined(query_parts)
        key_terms = joined(key_parts)
        value_terms = joined(value_parts)
        key_grad, value_grad = (
            lax.psum_scatter(key_terms, "seq", scatter_dimension=0, tiled=True),
            lax.psum_scatter(value_terms, "seq", scatter_dimension=0, tiled=True),
        )
        query_lin_grad = rotate_query(query_grad)[0].astype(jnp.bfloat16)
        key_lin_grad = rotate_key(key_grad)[0].astype(jnp.bfloat16)
        value_lin_grad = value_grad.astype(jnp.bfloat16)
        first_grad = (
            against(query_lin_grad, query_full)
            + against(key_lin_grad, key_full)
            + against(value_lin_grad, value_full)
        )
        input_part, gain_first_term = norm_back_first(first_grad)
        input_rows = (residual_grad + input_part).astype(jnp.bfloat16)
        new_sums = (gain_sums[0] + gain_first_term, gain_sums[1] + gain_second_term)
        saved = (
            layer_rows,
            input_rows,
            normed_first,
            query_lin_grad,
            key_lin_grad,
            value_lin_grad,
            attended,
            branch_grad,
            normed_second,
            gate_grad,
            up_grad,
            inner_act,
        )
        return (new_sums, saved)

    gain_init = (jnp.zeros((features,), jnp.float32), jnp.zeros((features,), jnp.float32))
    gain_sums, saved = lax.scan(one_batch, gain_init, (tokens, cotangent, piece_start))
    (
        layer_output,
        input_gradient,
        normed_first,
        query_lin_grad,
        key_lin_grad,
        value_lin_grad,
        attended,
        branch_grad,
        normed_second,
        gate_grad,
        up_grad,
        inner_act,
    ) = saved
    first_rows = flatten(normed_first)
    second_rows = flatten(normed_second)
    query_term = outer_sum(first_rows, flatten(query_lin_grad))
    key_term = outer_sum(first_rows, flatten(key_lin_grad))
    value_term = outer_sum(first_rows, flatten(value_lin_grad))
    output_term = outer_sum(flatten(attended), flatten(branch_grad))
    gate_term = outer_sum(second_rows, flatten(gate_grad))
    up_term = outer_sum(second_rows, flatten(up_grad))
    down_term = outer_sum(flatten(inner_act), flatten(cotangent))
    shares = (
        lax.psum_scatter(
            gain_sums[0].astype(jnp.bfloat16), "fsdp", scatter_dimension=0, tiled=True
        ).astype(jnp.float32),
        lax.psum_scatter(
            query_term.astype(jnp.bfloat16), "fsdp", scatter_dimension=0, tiled=True
        ).astype(jnp.float32),
        lax.psum_scatter(
            key_term.astype(jnp.bfloat16), "fsdp", scatter_dimension=0, tiled=True
        ).astype(jnp.float32),
        lax.psum_scatter(
            value_term.astype(jnp.bfloat16), "fsdp", scatter_dimension=0, tiled=True
        ).astype(jnp.float32),
        lax.psum_scatter(
            output_term.astype(jnp.bfloat16), "fsdp", scatter_dimension=0, tiled=True
        ).astype(jnp.float32),
        lax.psum_scatter(
            gain_sums[1].astype(jnp.bfloat16), "fsdp", scatter_dimension=0, tiled=True
        ).astype(jnp.float32),
        lax.psum_scatter(
            gate_term.astype(jnp.bfloat16), "fsdp", scatter_dimension=0, tiled=True
        ).astype(jnp.float32),
        lax.psum_scatter(
            up_term.astype(jnp.bfloat16), "fsdp", scatter_dimension=0, tiled=True
        ).astype(jnp.float32),
        lax.psum_scatter(
            down_term.astype(jnp.bfloat16), "fsdp", scatter_dimension=0, tiled=True
        ).astype(jnp.float32),
    )
    down_share = shares[8]
    summed = (
        lax.psum(shares[0].astype(jnp.bfloat16), ("seq", "rep")).astype(jnp.float32),
        lax.psum(shares[1].astype(jnp.bfloat16), ("seq", "rep")).astype(jnp.float32),
        lax.psum(shares[2].astype(jnp.bfloat16), ("seq", "rep")).astype(jnp.float32),
        lax.psum(shares[3].astype(jnp.bfloat16), ("seq", "rep")).astype(jnp.float32),
        lax.psum(shares[4].astype(jnp.bfloat16), ("seq", "rep")).astype(jnp.float32),
        lax.psum(shares[5].astype(jnp.bfloat16), ("seq", "rep")).astype(jnp.float32),
        lax.psum(shares[6].astype(jnp.bfloat16), ("seq", "rep")).astype(jnp.float32),
        lax.psum(shares[7].astype(jnp.bfloat16), ("seq", "rep")).astype(jnp.float32),
        lax.psum(down_share.astype(jnp.bfloat16), ("seq", "rep")).astype(jnp.float32),
    )
    return (
        layer_output,
        input_gradient,
        summed[0],
        summed[1],
        summed[2],
        summed[3],
        summed[4],
        summed[5],
        summed[6],
        summed[7],
        summed[8],
    )


def solution(mesh):
    placed = (
        P(("fsdp", "rep"), "seq", None),
        P(("fsdp", "rep"), "seq", None),
        P(("fsdp", "rep")),
        P("fsdp"),
        P("fsdp", None),
        P("fsdp", None),
        P("fsdp", None),
        P("fsdp", None),
        P("fsdp"),
        P("fsdp", None),
        P("fsdp", None),
        P("fsdp", None),
    )
    return jax.shard_map(
        local,
        mesh=mesh,
        in_specs=placed,
        out_specs=(
            P(("fsdp", "rep"), "seq", None),
            P(("fsdp", "rep"), "seq", None),
            P("fsdp"),
            P("fsdp", None),
            P("fsdp", None),
            P("fsdp", None),
            P("fsdp", None),
            P("fsdp"),
            P("fsdp", None),
            P("fsdp", None),
            P("fsdp", None),
        ),
        check_vma=False,
    )
```

profile of v0, /device:TPU:9, one launch (start us, length us, event | category | flops | bytes accessed | tf_op | source)
XLA Modules:
  0.0 4657.1 jit_solution(11702652466843767081)
XLA Ops:
  32.2 67.5 %all-gather.12.cloned.1.call-done = bf16[2048,2048]{0,1:T(8,128)(2,1)} async-done(((bf16[512,2048]{0,1:T(8,128)(2,1)}), bf16[2048,2048]{0,1:T(8,128)(2,1)}) %all-gather.12.cloned.1.call-update) | async-done | bytes 8388624 | tf_op jit(solution)/shard_map/all_gather | solution.py:95
  99.8 89.8 %all-gather.14.cloned.1.call-done = bf16[2048,2048]{0,1:T(8,128)(2,1)} async-done(((bf16[512,2048]{0,1:T(8,128)(2,1)}), bf16[2048,2048]{0,1:T(8,128)(2,1)}) %all-gather.14.cloned.1.call-update) | async-done | bytes 8388624 | tf_op jit(solution)/shard_map/all_gather | solution.py:96
  189.6 89.4 %all-gather.16.cloned.1.call-done = bf16[2048,2048]{1,0:T(8,128)(2,1)} async-done(((bf16[512,2048]{1,0:T(8,128)(2,1)}), bf16[2048,2048]{1,0:T(8,128)(2,1)}) %all-gather.16.cloned.1.call-update) | async-done | bytes 8388624 | tf_op jit(solution)/shard_map/all_gather | solution.py:97
  278.9 89.2 %all-gather.20.cloned.1.call-done = bf16[2048,2048]{1,0:T(8,128)(2,1)} async-done(((bf16[512,2048]{1,0:T(8,128)(2,1)}), bf16[2048,2048]{1,0:T(8,128)(2,1)}) %all-gather.20.cloned.1.call-update) | async-done | bytes 8388624 | tf_op jit(solution)/shard_map/all_gather | solution.py:98
  368.1 298.8 %all-gather.18.cloned.1.call-done = bf16[8192,2048]{1,0:T(8,128)(2,1)} async-done(((bf16[2048,2048]{1,0:T(8,128)(2,1)}), bf16[8192,2048]{1,0:T(8,128)(2,1)}) %all-gather.18.cloned.1.call-update) | async-done | bytes 33554448 | tf_op jit(solution)/shard_map/all_gather | solution.py:102
  666.9 298.8 %all-gather.22.cloned.1.call-done = bf16[2048,8192]{1,0:T(8,128)(2,1)} async-done(((bf16[512,8192]{1,0:T(8,128)(2,1)}), bf16[2048,8192]{1,0:T(8,128)(2,1)}) %all-gather.22.cloned.1.call-update) | async-done | bytes 33554448 | tf_op jit(solution)/shard_map/all_gather | solution.py:101
  965.7 298.9 %all-gather.24.cloned.1.call-done = bf16[2048,8192]{1,0:T(8,128)(2,1)} async-done(((bf16[512,8192]{1,0:T(8,128)(2,1)}), bf16[2048,8192]{1,0:T(8,128)(2,1)}) %all-gather.24.cloned.1.call-update) | async-done | bytes 33554448 | tf_op jit(solution)/shard_map/all_gather | solution.py:100
  1264.7 1448.1 %while.83 = (s32[]{:T(128)}, f32[2048]{0:T(1024)}, f32[2048]{0:T(1024)}, bf16[2,256,2048]{2,1,0:T(8,128)(2,1)}, bf16[2,256,2048]{2,1,0:T(8,128)(2,1)}, /*index=5...) while((s32[]{:T(128)}, f32[2048]{0:T(1024)}, ...), condition=%wide.region_16.17_spmd.clone.clone.clone.clone.clone, body=%wide.region_0.16_spmd.clone.clone.clone.clone.sunk.clone | while | flops 70737084416 | bytes 924582400 | solution.py:275
  1308.6 41.9 all-gather.28.cloned.1.call-done
  1356.9 74.5 %all-gather.26.cloned.1.call-done = bf16[1024,2048]{0,1:T(8,128)(2,1)} async-done(((bf16[256,2048]{0,1:T(8,128)(2,1)}), bf16[1024,2048]{0,1:T(8,128)(2,1)}) %all-gather.26.cloned.1.call-update) | async-done | bytes 4194320 | tf_op jit(solution)/shard_map/while/body/eval_jaxpr/all_gather | solution.py:139
  1431.5 38.7 while.81
  1496.7 28.8 bitcast_dynamic-update-slice_fusion.21
  1567.8 104.7 %while.82 = (s32[]{:T(128)}, f32[4,256,512]{1,2,0:T(8,128)}, f32[4,1024,512]{1,2,0:T(8,128)}, f32[4,1024,512]{1,2,0:T(8,128)}, s32[4]{0:T(128)S(1)}, /*index=5*/...) while((s32[]{:T(128)}, f32[4,256,512]{1,2,0:T(8,128)}, ...), condition=%wide.region_10.10_spmd.clone, body=%wide.region_8.9_spmd.clone.sunk | while | flops 1375074304 | bytes 113311264 | solution.py:237
  1692.3 125.5 %reduce-scatter.30.cloned.1.call-done = f32[256,2048]{0,1:T(8,128)} async-done(((f32[1024,2048]{0,1:T(8,128)}), f32[256,2048]{0,1:T(8,128)}) %reduce-scatter.30.cloned.1.call-update) | async-done | bytes 2097168 | tf_op jit(solution)/shard_map/while/body/eval_jaxpr/reduce_scatter | solution.py:244
  1830.6 134.9 %reduce-scatter.32.cloned.1.call-done = f32[256,2048]{0,1:T(8,128)} async-done(((f32[1024,2048]{0,1:T(8,128)}), f32[256,2048]{0,1:T(8,128)}) %reduce-scatter.32.cloned.1.call-update) | async-done | bytes 2097168 | tf_op jit(solution)/shard_map/while/body/eval_jaxpr/reduce_scatter | solution.py:245
  2027.5 43.5 all-gather.28.cloned.1.call-done
  2077.3 74.5 %all-gather.26.cloned.1.call-done = bf16[1024,2048]{0,1:T(8,128)(2,1)} async-done(((bf16[256,2048]{0,1:T(8,128)(2,1)}), bf16[1024,2048]{0,1:T(8,128)(2,1)}) %all-gather.26.cloned.1.call-update) | async-done | bytes 4194320 | tf_op jit(solution)/shard_map/while/body/eval_jaxpr/all_gather | solution.py:139
  2151.9 38.7 while.81
  2217.1 28.8 bitcast_dynamic-update-slice_fusion.21
  2288.1 104.7 %while.82 = (s32[]{:T(128)}, f32[4,256,512]{1,2,0:T(8,128)}, f32[4,1024,512]{1,2,0:T(8,128)}, f32[4,1024,512]{1,2,0:T(8,128)}, s32[4]{0:T(128)S(1)}, /*index=5*/...) while((s32[]{:T(128)}, f32[4,256,512]{1,2,0:T(8,128)}, ...), condition=%wide.region_10.10_spmd.clone, body=%wide.region_8.9_spmd.clone.sunk | while | flops 1375074304 | bytes 113311264 | solution.py:237
  2412.5 125.7 %reduce-scatter.30.cloned.1.call-done = f32[256,2048]{0,1:T(8,128)} async-done(((f32[1024,2048]{0,1:T(8,128)}), f32[256,2048]{0,1:T(8,128)}) %reduce-scatter.30.cloned.1.call-update) | async-done | bytes 2097168 | tf_op jit(solution)/shard_map/while/body/eval_jaxpr/reduce_scatter | solution.py:244
  2550.9 134.7 %reduce-scatter.32.cloned.1.call-done = f32[256,2048]{0,1:T(8,128)} async-done(((f32[1024,2048]{0,1:T(8,128)}), f32[256,2048]{0,1:T(8,128)}) %reduce-scatter.32.cloned.1.call-update) | async-done | bytes 2097168 | tf_op jit(solution)/shard_map/while/body/eval_jaxpr/reduce_scatter | solution.py:245
  2753.0 25.4 bitcast_convert_fusion.1
  2778.5 25.0 bitcast_convert_fusion.2
  2805.1 25.3 bitcast_convert_fusion
  2830.5 69.1 %reduce-scatter.18.cloned.1.call-done = bf16[512,2048]{1,0:T(8,128)(2,1)} async-done(((bf16[2048,2048]{1,0:T(8,128)(2,1)}), bf16[512,2048]{1,0:T(8,128)(2,1)}) %reduce-scatter.18.cloned.1.call-update) | async-done | bytes 2097168 | tf_op jit(solution)/shard_map/reduce_scatter | solution.py:306
  2899.6 89.2 %reduce-scatter.16.cloned.1.call-done = bf16[512,2048]{1,0:T(8,128)(2,1)} async-done(((bf16[2048,2048]{1,0:T(8,128)(2,1)}), bf16[512,2048]{1,0:T(8,128)(2,1)}) %reduce-scatter.16.cloned.1.call-update) | async-done | bytes 2097168 | tf_op jit(solution)/shard_map/reduce_scatter | solution.py:303
  2988.8 89.4 %reduce-scatter.22.cloned.1.call-done = bf16[512,2048]{1,0:T(8,128)(2,1)} async-done(((bf16[2048,2048]{1,0:T(8,128)(2,1)}), bf16[512,2048]{1,0:T(8,128)(2,1)}) %reduce-scatter.22.cloned.1.call-update) | async-done | bytes 2097168 | tf_op jit(solution)/shard_map/reduce_scatter | solution.py:312
  3078.2 291.5 %reduce-scatter.26.cloned.1.call-done = bf16[512,8192]{1,0:T(8,128)(2,1)} async-done(((bf16[2048,8192]{1,0:T(8,128)(2,1)}), bf16[512,8192]{1,0:T(8,128)(2,1)}) %reduce-scatter.26.cloned.1.call-update) | async-done | bytes 8388624
  3369.7 291.7 %reduce-scatter.24.cloned.1.call-done = bf16[512,8192]{1,0:T(8,128)(2,1)} async-done(((bf16[2048,8192]{1,0:T(8,128)(2,1)}), bf16[512,8192]{1,0:T(8,128)(2,1)}) %reduce-scatter.24.cloned.1.call-update) | async-done | bytes 8388624
  3661.4 291.6 %reduce-scatter.28.cloned.1.call-done = bf16[2048,2048]{1,0:T(8,128)(2,1)} async-done(((bf16[8192,2048]{1,0:T(8,128)(2,1)}), bf16[2048,2048]{1,0:T(8,128)(2,1)}) %reduce-scatter.28.cloned.1.call-update) | async-done | bytes 8388624
  3976.6 628.3 %all-reduce.14.cloned.1.call-done = (bf16[512,2048]{1,0:T(8,128)(2,1)}, bf16[512,2048]{1,0:T(8,128)(2,1)}, bf16[512,2048]{1,0:T(8,128)(2,1)}, bf16[512,2048]{1,0...) async-done(((bf16[512,2048]{1,0:T(8,128)(2,1)}, bf16[512,2048]{1,0:T(8,128)(2,1)}, bf16[512,2048]{1,0:T(8,128)(2,1)}, ...) | async-done | bytes 33554448 | tf_op jit(solution)/shard_map/psum | solution.py:331
  (639 shorter events, 747.3 us)
Async XLA Ops:
  7.2 92.6 %all-gather.12.cloned.1.call-start = ((), (), s32[]{:S(2)}) async-start(), calls=%async_computation.9 | async-start | bytes 10485760 | tf_op jit(solution)/shard_map/all_gather | solution.py:95
  11.2 178.4 %all-gather.14.cloned.1.call-start = ((), (), s32[]{:S(2)}) async-start(), calls=%async_computation.10 | async-start | bytes 10485760 | tf_op jit(solution)/shard_map/all_gather | solution.py:96
  15.3 263.7 %all-gather.16.cloned.1.call-start = ((), (), s32[]{:S(2)}) async-start(), calls=%async_computation.11 | async-start | bytes 10485760 | tf_op jit(solution)/shard_map/all_gather | solution.py:97
  16.0 352.1 %all-gather.20.cloned.1.call-start = ((), (), s32[]{:S(2)}) async-start(), calls=%async_computation.13 | async-start | bytes 10485760 | tf_op jit(solution)/shard_map/all_gather | solution.py:98
  16.6 650.4 %all-gather.18.cloned.1.call-start = ((), (), s32[]{:S(2)}) async-start(), calls=%async_computation.12 | async-start | bytes 41943040 | tf_op jit(solution)/shard_map/all_gather | solution.py:102
  17.2 948.6 %all-gather.22.cloned.1.call-start = ((), (), s32[]{:S(2)}) async-start(), calls=%async_computation.14 | async-start | bytes 41943040 | tf_op jit(solution)/shard_map/all_gather | solution.py:101
  17.8 1246.9 %copy-start.6 = (bf16[2,256,2048]{2,1,0:T(8,128)(2,1)S(1)}, bf16[2,256,2048]{2,1,0:T(8,128)(2,1)}, u32[]{:S(2)}) copy-start(bf16[2,256,2048]{2,1,0:T(8,128)(2,1)} %param.18) | copy-start | bytes 6291460
  17.8 1246.9 %copy-start.56 = (s32[2]{0:T(128)S(1)}, s32[2]{0:T(128)}, u32[]{:S(2)}) copy-start(s32[2]{0:T(128)} %param.20) | copy-start | bytes 28
  17.8 1246.9 %all-gather.24.cloned.1.call-start = ((), (), s32[]{:S(2)}) async-start(), calls=%async_computation.15 | async-start | bytes 41943040 | tf_op jit(solution)/shard_map/all_gather | solution.py:100
  1265.0 293.9 %copy-start.23 = (f32[2048]{0:T(1024)}, f32[2048]{0:T(1024)S(1)}, u32[]{:S(2)}) copy-start(f32[2048]{0:T(1024)S(1)} %get-tuple-element.1715) | copy-start | bytes 24580 | tf_op jit(solution)/shard_map/while
  1265.0 85.6 %all-gather.28.cloned.1.call-start = ((), (), s32[]{:S(2)}) async-start(), calls=%async_computation.25 | async-start | bytes 5242880 | tf_op jit(solution)/shard_map/while/body/eval_jaxpr/all_gather | solution.py:140
  1272.1 159.3 %all-gather.26.cloned.1.call-start = ((), (), s32[]{:S(2)}) async-start(), calls=%async_computation.24 | async-start | bytes 5242880 | tf_op jit(solution)/shard_map/while/body/eval_jaxpr/all_gather | solution.py:139
  1286.7 531.2 %reduce-scatter.30.cloned.1.call-start = ((), (), s32[]{:S(2)}) async-start(), calls=%async_computation.26 | async-start | bytes 10485760 | tf_op jit(solution)/shard_map/while/body/eval_jaxpr/reduce_scatter | solution.py:244
  1672.5 293.0 %reduce-scatter.32.cloned.1.call-start = ((), (), s32[]{:S(2)}) async-start(), calls=%async_computation.27 | async-start | bytes 10485760 | tf_op jit(solution)/shard_map/while/body/eval_jaxpr/reduce_scatter | solution.py:245
  1674.1 143.8 %copy-start.13 = (f32[256,32]{0,1:T(8,128)S(1)}, f32[256,32]{0,1:T(8,128)}, u32[]{:S(2)}) copy-start(f32[256,32]{0,1:T(8,128)} %copy-done.12) | copy-start | bytes 98308 | tf_op jit(solution)/shard_map/while
  1674.1 143.8 %copy-start.15 = (f32[256,32]{0,1:T(8,128)S(1)}, f32[256,32]{0,1:T(8,128)}, u32[]{:S(2)}) copy-start(f32[256,32]{0,1:T(8,128)} %copy-done.14) | copy-start | bytes 98308 | tf_op jit(solution)/shard_map/while
  1830.6 142.8 %copy-start.25 = (f32[2048]{0:T(1024)S(1)}, f32[2048]{0:T(1024)}, u32[]{:S(2)}) copy-start(f32[2048]{0:T(1024)} %get-tuple-element.1657) | copy-start | bytes 24580 | tf_op jit(solution)/shard_map/while
  1984.4 294.7 %copy-start.23 = (f32[2048]{0:T(1024)}, f32[2048]{0:T(1024)S(1)}, u32[]{:S(2)}) copy-start(f32[2048]{0:T(1024)S(1)} %get-tuple-element.1715) | copy-start | bytes 24580 | tf_op jit(solution)/shard_map/while
  1984.5 86.5 %all-gather.28.cloned.1.call-start = ((), (), s32[]{:S(2)}) async-start(), calls=%async_computation.25 | async-start | bytes 5242880 | tf_op jit(solution)/shard_map/while/body/eval_jaxpr/all_gather | solution.py:140
  1991.6 160.3 %all-gather.26.cloned.1.call-start = ((), (), s32[]{:S(2)}) async-start(), calls=%async_computation.24 | async-start | bytes 5242880 | tf_op jit(solution)/shard_map/while/body/eval_jaxpr/all_gather | solution.py:139
  2005.8 532.4 %reduce-scatter.30.cloned.1.call-start = ((), (), s32[]{:S(2)}) async-start(), calls=%async_computation.26 | async-start | bytes 10485760 | tf_op jit(solution)/shard_map/while/body/eval_jaxpr/reduce_scatter | solution.py:244
  2392.8 292.9 %reduce-scatter.32.cloned.1.call-start = ((), (), s32[]{:S(2)}) async-start(), calls=%async_computation.27 | async-start | bytes 10485760 | tf_op jit(solution)/shard_map/while/body/eval_jaxpr/reduce_scatter | solution.py:245
  2394.5 143.7 %copy-start.13 = (f32[256,32]{0,1:T(8,128)S(1)}, f32[256,32]{0,1:T(8,128)}, u32[]{:S(2)}) copy-start(f32[256,32]{0,1:T(8,128)} %copy-done.12) | copy-start | bytes 98308 | tf_op jit(solution)/shard_map/while
  2394.5 143.7 %copy-start.15 = (f32[256,32]{0,1:T(8,128)S(1)}, f32[256,32]{0,1:T(8,128)}, u32[]{:S(2)}) copy-start(f32[256,32]{0,1:T(8,128)} %copy-done.14) | copy-start | bytes 98308 | tf_op jit(solution)/shard_map/while
  2712.8 117.7 %reduce-scatter.20.cloned.1.call-start = ((), (), s32[]{:S(2)}) async-start(), calls=%async_computation.18 | async-start | bytes 10485760 | tf_op jit(solution)/shard_map/reduce_scatter | solution.py:309
  2722.9 176.7 %reduce-scatter.18.cloned.1.call-start = ((), (), s32[]{:S(2)}) async-start(), calls=%async_computation.17 | async-start | bytes 10485760 | tf_op jit(solution)/shard_map/reduce_scatter | solution.py:306
  2732.9 255.9 %reduce-scatter.16.cloned.1.call-start = ((), (), s32[]{:S(2)}) async-start(), calls=%async_computation.16 | async-start | bytes 10485760 | tf_op jit(solution)/shard_map/reduce_scatter | solution.py:303
  2741.4 336.9 %reduce-scatter.22.cloned.1.call-start = ((), (), s32[]{:S(2)}) async-start(), calls=%async_computation.19 | async-start | bytes 10485760 | tf_op jit(solution)/shard_map/reduce_scatter | solution.py:312
  2751.5 618.3 %reduce-scatter.26.cloned.1.call-start = ((), (), s32[]{:S(2)}) async-start(), calls=%async_computation.21 | async-start | bytes 41943040
  2778.4 883.0 %reduce-scatter.24.cloned.1.call-start = ((), (), s32[]{:S(2)}) async-start(), calls=%async_computation.20 | async-start | bytes 41943040
  2803.5 1149.5 %reduce-scatter.28.cloned.1.call-start = ((), (), s32[]{:S(2)}) async-start(), calls=%async_computation.22 | async-start | bytes 41943040
  2830.5 1774.4 %all-reduce.14.cloned.1.call-start = ((), (), s32[]{:S(2)}) async-start(), calls=%async_computation.23 | async-start | bytes 67108864 | tf_op jit(solution)/shard_map/psum | solution.py:331
  (113 other events, 1807.1 us)
Sparse Core Ops, SparseCore 0:
  11.3 88.4 all-gather.11
  102.2 87.3 all-gather.13
  191.4 87.4 all-gather.15
  280.6 87.4 all-gather.19
  369.8 297.0 all-gather.17
  668.6 297.0 all-gather.21
  967.6 297.0 all-gather.23
  1272.3 78.2 all-gather.27
  1352.7 78.7 all-gather.25
  1672.6 145.2 reduce-scatter.29
  1820.2 145.2 reduce-scatter.31
  1991.7 79.1 all-gather.27
  2073.1 78.7 all-gather.25
  2392.9 145.2 reduce-scatter.29
  2540.4 145.2 reduce-scatter.31
  2723.0 87.2 reduce-scatter.19
  2813.2 86.3 reduce-scatter.17
  2902.5 86.2 reduce-scatter.15
  2991.9 86.3 reduce-scatter.21
  3081.2 288.5 reduce-scatter.25
  3372.8 288.5 reduce-scatter.23
  3664.5 288.5 reduce-scatter.27
  3956.5 648.3 all-reduce.13
where the time goes:
time: 4660 us
  waiting for transfers between devices  3740 us (80%)
  matrix products  602 us (13%)
  local copies, waits for them, and re-layouts  131 us (3%)
  other arithmetic  107 us (2%)
    unnamed x18, waiting for transfers between devices  878 us
    psum x1, waiting for transfers between devices, local(): lax.psum(shares[1].astype(jnp.bfloat16), ('seq', 'rep')).astype(jnp.float32)  628 us
    all_gather x1, waiting for transfers between devices, local(): lax.all_gather(gate_weight, 'fsdp', axis=0, tiled=True)  299 us
    all_gather x1, waiting for transfers between devices, local(): lax.all_gather(up_weight, 'fsdp', axis=0, tiled=True)  299 us
    all_gather x1, waiting for transfers between devices, local(): lax.all_gather(down_weight, 'fsdp', axis=0, tiled=True)  299 us
    reduce_scatter x2, waiting for transfers between devices, one_batch(): lax.psum_scatter(value_terms, 'seq', scatter_dimension=0, tiled=True)  270 us
    reduce_scatter x2, waiting for transfers between devices, one_batch(): lax.psum_scatter(key_terms, 'seq', scatter_dimension=0, tiled=True)  251 us
    dot_general x14, matrix products, matmul(): return jnp.dot(left_op, right_op, preferred_element_type=jnp.float32)  182 us
  transfers between devices with their start and end apart: 23, of which 22 were waited for; matrix products, arithmetic and copies ran while one was open for 5% of the time, Pallas kernels for 0%

commit v1 on v0

v1 whole, which is shorter than its diff:
```python
import functools
import math

import jax
import jax.numpy as jnp
from jax import lax
from jax.experimental import pallas as pl
from jax.experimental.pallas import tpu as pltpu
from jax.sharding import PartitionSpec as P

HEADS = 32
HEAD_DIM = 64
PIECE = 256
BLOCK = 256
LANES = 128

NORM_EPS = 1e-05
ROPE_BASE = 130000.0
MASKED_SCORE = -1e30
SCALE = 0.125 * math.log2(math.e)

bf16 = jnp.bfloat16
f32 = jnp.float32


def matmul(left_op, right_op, out=f32):
    return jnp.dot(left_op, right_op, preferred_element_type=f32).astype(out)


def outer_sum(left_op, right_op, out=f32):
    return lax.dot_general(
        left_op, right_op, (((0,), (0,)), ((), ())), preferred_element_type=f32
    ).astype(out)


def against(left_op, right_op, out=f32):
    return lax.dot_general(
        left_op, right_op, (((1,), (1,)), ((), ())), preferred_element_type=f32
    ).astype(out)


def dot_nt(left_op, right_op):
    return lax.dot_general(
        left_op, right_op, (((1,), (1,)), ((), ())), preferred_element_type=f32
    )


def dot_nn(left_op, right_op):
    return lax.dot_general(
        left_op, right_op, (((1,), (0,)), ((), ())), preferred_element_type=f32
    )


def lane_index(rows):
    return lax.broadcasted_iota(jnp.int32, (rows, LANES), 1)


def turned(value, cosine, sine):
    front = lax.rem(lane_index(value.shape[0]), HEAD_DIM) < HEAD_DIM // 2
    swapped = jnp.where(
        front,
        pltpu.roll(value, LANES - HEAD_DIM // 2, 1),
        pltpu.roll(value, HEAD_DIM // 2, 1),
    )
    return value * cosine + swapped * sine


def per_head_rows(value):
    first = lane_index(value.shape[0]) < HEAD_DIM
    zero = jnp.zeros_like(value)
    return jnp.concatenate([jnp.where(first, value, zero), jnp.where(first, zero, value)], axis=0)


def from_head_columns(value):
    rows = value.shape[1] // 2
    first = lax.broadcasted_iota(jnp.int32, (LANES, rows), 0) < HEAD_DIM
    return jnp.where(first, value[:, :rows], value[:, rows:]).T


def seen(key_block, query_block, start):
    key_pos = key_block * BLOCK + lax.broadcasted_iota(jnp.int32, (BLOCK, 2 * BLOCK), 0)
    query_pos = query_block * BLOCK + lax.rem(
        lax.broadcasted_iota(jnp.int32, (BLOCK, 2 * BLOCK), 1), BLOCK
    )
    key_in = (key_pos >= start) & (key_pos < start + PIECE)
    query_in = (query_pos >= start) & (query_pos < start + PIECE)
    return (key_pos <= query_pos) | (key_in & query_in)


def spills_over(query_block, start):
    return (start > query_block * BLOCK) & (start < (query_block + 1) * BLOCK)


def attend_forward_kernel(
    start_ref, lin_ref, cos_ref, sin_ref, out_ref, qkv_ref, lse_ref, s_ref, m_ref, l_ref, acc_ref
):
    start = start_ref[0]
    blocks = lin_ref.shape[0] // BLOCK
    for i in range(blocks):
        rows = slice(i * BLOCK, (i + 1) * BLOCK)
        cosine, sine = cos_ref[rows, :], sin_ref[rows, :]
        for part in range(2):
            columns = slice(part * LANES, (part + 1) * LANES)
            qkv_ref[rows, columns] = turned(lin_ref[rows, columns], cosine, sine).astype(bf16)
        qkv_ref[rows, 2 * LANES :] = lin_ref[rows, 2 * LANES :].astype(bf16)

    def key_rows(j):
        return qkv_ref[j * BLOCK : (j + 1) * BLOCK, LANES : 2 * LANES]

    def value_columns(j):
        return qkv_ref[j * BLOCK : (j + 1) * BLOCK, 2 * LANES :].T

    for i in range(blocks):
        rows = slice(i * BLOCK, (i + 1) * BLOCK)
        queries = per_head_rows(qkv_ref[rows, :LANES])
        over = spills_over(i, start)
        top = None
        for j in range(i + 1):
            scores = dot_nt(key_rows(j), queries)
            if j == i:
                scores = jnp.where(seen(j, i, start), scores, MASKED_SCORE)
            s_ref[j * BLOCK : (j + 1) * BLOCK, :] = scores
            best = jnp.max(scores, axis=0, keepdims=True)
            top = best if top is None else jnp.maximum(top, best)
        m_ref[...] = top

        if i + 1 < blocks:

            @pl.when(over)
            def _():
                scores = dot_nt(key_rows(i + 1), queries)
                scores = jnp.where(seen(i + 1, i, start), scores, MASKED_SCORE)
                s_ref[(i + 1) * BLOCK : (i + 2) * BLOCK, :] = scores
                m_ref[...] = jnp.maximum(m_ref[...], jnp.max(scores, axis=0, keepdims=True))

        top = m_ref[...]
        shift = top * SCALE
        total, mixed = None, None
        for j in range(i + 1):
            weights = jnp.exp2(s_ref[j * BLOCK : (j + 1) * BLOCK, :] * SCALE - shift)
            part_total = jnp.sum(weights, axis=0, keepdims=True)
            part_mixed = dot_nn(value_columns(j), weights.astype(bf16))
            total = part_total if total is None else total + part_total
            mixed = part_mixed if mixed is None else mixed + part_mixed
        l_ref[...] = total
        acc_ref[...] = mixed

        if i + 1 < blocks:

            @pl.when(over)
            def _():
                weights = jnp.exp2(s_ref[(i + 1) * BLOCK : (i + 2) * BLOCK, :] * SCALE - shift)
                l_ref[...] += jnp.sum(weights, axis=0, keepdims=True)
                acc_ref[...] += dot_nn(value_columns(i + 1), weights.astype(bf16))

        total = l_ref[...]
        out_ref[rows, :] = from_head_columns(acc_ref[...] / total).astype(bf16)
        lse_ref[0, i : i + 1, :] = shift + jnp.log2(total)


def attend_backward_kernel(
    start_ref, qkv_ref, out_ref, grad_ref, lse_ref, cos_ref, sin_ref, lin_ref, dq_ref, dk_ref, dv_ref
):
    start = start_ref[0]
    blocks = qkv_ref.shape[0] // BLOCK
    dk_ref[...] = jnp.zeros_like(dk_ref)
    dv_ref[...] = jnp.zeros_like(dv_ref)
    for i in range(blocks):
        rows = slice(i * BLOCK, (i + 1) * BLOCK)
        queries = per_head_rows(qkv_ref[rows, :LANES])
        grads_in = grad_ref[rows, :]
        grads = per_head_rows(grads_in)
        both = (grads_in.astype(f32) * out_ref[rows, :].astype(f32)).T
        delta = jnp.concatenate(
            [
                jnp.sum(both[:HEAD_DIM], axis=0, keepdims=True),
                jnp.sum(both[HEAD_DIM:], axis=0, keepdims=True),
            ],
            axis=1,
        )
        lse = lse_ref[0, i : i + 1, :]

        def one(j, masked):
            keys_at = slice(j * BLOCK, (j + 1) * BLOCK)
            keys = qkv_ref[keys_at, LANES : 2 * LANES]
            scores = dot_nt(keys, queries)
            weights = jnp.exp2(scores * SCALE - lse)
            if masked:
                weights = jnp.where(seen(j, i, start), weights, 0.0)
            weight_grads = dot_nt(qkv_ref[keys_at, 2 * LANES :], grads)
            score_grads = (weights * (weight_grads - delta)).astype(bf16)
            dv_ref[keys_at, :] += dot_nn(weights.astype(bf16), grads)
            dk_ref[keys_at, :] += dot_nn(score_grads, queries)
            return dot_nn(keys.T, score_grads)

        query_grads = None
        for j in range(i + 1):
            part = one(j, j == i)
            query_grads = part if query_grads is None else query_grads + part
        dq_ref[...] = query_grads

        if i + 1 < blocks:

            @pl.when(spills_over(i, start))
            def _():
                dq_ref[...] += one(i + 1, True)

        lin_ref[rows, :LANES] = turned(
            from_head_columns(dq_ref[...]) * 0.125, cos_ref[rows, :], -sin_ref[rows, :]
        ).astype(bf16)
    for i in range(blocks):
        rows = slice(i * BLOCK, (i + 1) * BLOCK)
        lin_ref[rows, LANES : 2 * LANES] = turned(
            dk_ref[rows, :] * 0.125, cos_ref[rows, :], -sin_ref[rows, :]
        ).astype(bf16)
        lin_ref[rows, 2 * LANES :] = dv_ref[rows, :].astype(bf16)


def column_block(length, width):
    return pl.BlockSpec((length, width), lambda p, s: (0, p))


def whole_block(shape):
    return pl.BlockSpec(shape, lambda p, s: (0,) * len(shape))


def attend_forward(start, lin, cosine, sine):
    length, width = lin.shape
    pairs = width // (3 * LANES)
    blocks = length // BLOCK
    flops = pairs * 2 * 2 * 2 * length * length * LANES
    return pl.pallas_call(
        attend_forward_kernel,
        grid_spec=pltpu.PrefetchScalarGridSpec(
            num_scalar_prefetch=1,
            grid=(pairs,),
            in_specs=[
                column_block(length, 3 * LANES),
                whole_block((length, LANES)),
                whole_block((length, LANES)),
            ],
            out_specs=[
                column_block(length, LANES),
                column_block(length, 3 * LANES),
                pl.BlockSpec((1, blocks, 2 * BLOCK), lambda p, s: (p, 0, 0)),
            ],
            scratch_shapes=[
                pltpu.VMEM((length, 2 * BLOCK), f32),
                pltpu.VMEM((1, 2 * BLOCK), f32),
                pltpu.VMEM((1, 2 * BLOCK), f32),
                pltpu.VMEM((LANES, 2 * BLOCK), f32),
            ],
        ),
        out_shape=[
            jax.ShapeDtypeStruct((length, pairs * LANES), bf16),
            jax.ShapeDtypeStruct((length, width), bf16),
            jax.ShapeDtypeStruct((pairs, blocks, 2 * BLOCK), f32),
        ],
        cost_estimate=pl.CostEstimate(
            flops=flops,
            bytes_accessed=length * width * 6 + length * pairs * LANES * 2,
            transcendentals=pairs * 2 * length * length // 2,
        ),
        name="attend_forward",
    )(start, lin, cosine, sine)


def attend_backward(start, qkv, out, grad, lse, cosine, sine):
    length, width = qkv.shape
    pairs = width // (3 * LANES)
    blocks = length // BLOCK
    flops = pairs * 2 * 5 * 2 * length * length * LANES
    return pl.pallas_call(
        attend_backward_kernel,
        grid_spec=pltpu.PrefetchScalarGridSpec(
            num_scalar_prefetch=1,
            grid=(pairs,),
            in_specs=[
                column_block(length, 3 * LANES),
                column_block(length, LANES),
                column_block(length, LANES),
                pl.BlockSpec((1, blocks, 2 * BLOCK), lambda p, s: (p, 0, 0)),
                whole_block((length, LANES)),
                whole_block((length, LANES)),
            ],
            out_specs=column_block(length, 3 * LANES),
            scratch_shapes=[
                pltpu.VMEM((LANES, 2 * BLOCK), f32),
                pltpu.VMEM((length, LANES), f32),
                pltpu.VMEM((length, LANES), f32),
            ],
        ),
        out_shape=jax.ShapeDtypeStruct((length, width), bf16),
        cost_estimate=pl.CostEstimate(
            flops=flops,
            bytes_accessed=length * width * 4 + length * pairs * LANES * 4,
            transcendentals=pairs * 2 * length * length // 2,
        ),
        name="attend_backward",
    )(start, qkv, out, grad, lse, cosine, sine)


def swap(value, axis, size, distance):
    return lax.ppermute(value, axis, [(i, i ^ distance) for i in range(size)])


def bit_orders(size):
    bits = [1 << b for b in range(size.bit_length() - 1)]
    return bits, bits[::-1]


def gather_rows(value, axis, size):
    half = value.shape[0] // 2
    parts = []
    for part, order in zip((value[:half], value[half:]), bit_orders(size)):
        held = {0: part}
        for bit in order:
            for d in list(held):
                held[d ^ bit] = swap(held[d], axis, size, bit)
        parts.append(held)
    return jnp.concatenate([parts[h][d] for d in range(size) for h in range(2)], axis=0)


def scatter_rows(block_of, axis, size):
    blocks = {d: block_of(d) for d in range(size)}
    half = blocks[0].shape[0] // 2
    sums = []
    for h, order in enumerate(bit_orders(size)):
        held = {d: b[h * half : (h + 1) * half] for d, b in blocks.items()}
        for bit in order:
            for d in [d for d in held if d & bit]:
                came = swap(held.pop(d).astype(bf16), axis, size, bit)
                held[d ^ bit] = held[d ^ bit].astype(f32) + came.astype(f32)
        sums.append(held[0])
    return jnp.concatenate(sums, axis=0)


def local(
    tokens,
    cotangent,
    piece_start,
    attention_gain,
    query_weight,
    key_weight,
    value_weight,
    output_weight,
    feedforward_gain,
    gate_weight,
    up_weight,
    down_weight,
):
    lengths, shards, copies = (lax.axis_size(name) for name in ("seq", "fsdp", "rep"))
    batch, span, features = tokens.shape
    hidden = gate_weight.shape[1]
    team = lengths // batch
    members = lengths * copies
    everyone = ("seq", "rep")
    own_rows = batch * span
    length = lengths * span
    part = hidden // shards
    rows = features // shards
    heads_width = features // (shards * team)
    width = features // team
    z, f, r = (lax.axis_index(name) for name in ("seq", "fsdp", "rep"))
    line = z * copies + r
    mine = lax.rem(line, team)
    local_seq = lax.rem(line // team, batch)

    def perm_in(k):
        pairs = []
        for zz in range(lengths):
            for rr in range(copies):
                j = (zz + k) % batch
                pairs.append((zz * copies + rr, (rr * batch + j) * team + zz // batch))
        return pairs

    def take_sequence(value):
        came = [
            lax.ppermute(
                lax.dynamic_index_in_dim(value, lax.rem(z + k, batch), 0, False),
                everyone,
                perm_in(k),
            )
            for k in range(batch)
        ]
        return jnp.concatenate(
            [lax.select_n(lax.rem(local_seq + batch - b, batch), *came) for b in range(batch)],
            axis=0,
        )

    def give_back(value):
        blocks = value.reshape(batch, span, features)
        came = [
            lax.ppermute(
                lax.dynamic_index_in_dim(blocks, lax.rem(local_seq + batch - k, batch), 0, False),
                everyone,
                [(b, a) for a, b in perm_in(k)],
            )
            for k in range(batch)
        ]
        return jnp.stack(
            [lax.select_n(lax.rem(j + batch * lengths - z, batch), *came) for j in range(batch)]
        )

    def team_gather(value):
        came = [value] + [swap(value, everyone, members, d) for d in range(1, team)]
        return jnp.concatenate([lax.select_n(mine ^ u, *came) for u in range(team)], axis=0)

    def team_scatter(value):
        def block(d):
            return lax.dynamic_slice_in_dim(value, (mine ^ d) * own_rows, own_rows, 0)

        total = block(0).astype(f32)
        for d in range(1, team):
            total = total + swap(block(d), everyone, members, d).astype(f32)
        return total

    def shard_gather_small(value):
        out = jnp.zeros((shards,) + value.shape, value.dtype)
        for d in range(shards):
            came = swap(value, "fsdp", shards, d) if d else value
            out = lax.dynamic_update_index_in_dim(out, came, f ^ d, 0)
        return out

    def head_columns(weight):
        split = weight.reshape(weight.shape[0], shards, team, heads_width)
        return lax.dynamic_index_in_dim(split, mine, 2, False).reshape(weight.shape[0], width)

    tokens_own = take_sequence(tokens)
    start = lax.ppermute(
        lax.dynamic_index_in_dim(piece_start, lax.rem(z, batch), 0), everyone, perm_in(0)
    )

    pairs = width // LANES
    wqkv_rows = jnp.stack(
        [
            head_columns(w).reshape(rows, pairs, LANES)
            for w in (query_weight, key_weight, value_weight)
        ],
        axis=2,
    ).reshape(rows, 3 * width)
    wqkv = lax.all_gather(wqkv_rows, "fsdp", axis=0, tiled=True)
    wo_rows = lax.dynamic_slice_in_dim(output_weight, mine * heads_width, heads_width, 0)
    wo = lax.all_gather(wo_rows, "fsdp", axis=0, tiled=True)

    gains = shard_gather_small(jnp.stack([attention_gain, feedforward_gain]))
    gain_first = gains[:, 0].reshape(features).astype(f32)
    gain_second = gains[:, 1].reshape(features).astype(f32)

    half_dim = HEAD_DIM // 2
    places = jnp.arange(length, dtype=jnp.int32).astype(f32)
    frequency = ROPE_BASE ** (-jnp.arange(half_dim, dtype=f32) / half_dim)
    angles = places[:, None] * frequency[None, :]
    cos_half, sin_half = jnp.cos(angles), jnp.sin(angles)
    cosine = jnp.concatenate([cos_half] * 4, axis=1)
    sine = jnp.concatenate([-sin_half, sin_half] * 2, axis=1)

    activation = tokens_own.astype(f32)
    scale_first = lax.rsqrt(jnp.mean(activation * activation, axis=-1, keepdims=True) + NORM_EPS)
    first_own = (activation * scale_first * gain_first).astype(bf16)
    first = team_gather(first_own)
    lin = matmul(first, wqkv)
    attended, qkv, lse = attend_forward(start, lin, cosine, sine)
    residual = activation + team_scatter(matmul(attended, wo, bf16))
    scale_second = lax.rsqrt(jnp.mean(residual * residual, axis=-1, keepdims=True) + NORM_EPS)
    second_own = (residual * scale_second * gain_second).astype(bf16)

    slab = part // copies

    def hidden_columns(weight):
        out = jnp.zeros((shards, rows, slab), bf16)
        for d in range(shards):
            piece = lax.dynamic_slice_in_dim(weight, (f ^ d) * part + r * slab, slab, 1)
            came = swap(piece, "fsdp", shards, d) if d else piece
            out = lax.dynamic_update_index_in_dim(out, came, f ^ d, 0)
        out = out.reshape(features, slab)
        came = [out] + [swap(out, "rep", copies, d) for d in range(1, copies)]
        return jnp.concatenate([lax.select_n(r ^ u, *came) for u in range(copies)], axis=1)

    gate_w = hidden_columns(gate_weight)
    up_w = hidden_columns(up_weight)

    cotangent_own = take_sequence(cotangent)
    cot = gather_rows(cotangent_own, "fsdp", shards)
    second = gather_rows(second_own, "fsdp", shards)

    gate = matmul(second, gate_w)
    up = matmul(second, up_w)
    inner_grad = against(cot, down_weight)
    sig = jax.nn.sigmoid(gate)
    silu = gate * sig
    inner = (silu * up).astype(bf16)
    gate_grad = (inner_grad * up * (sig * (1.0 + gate * (1.0 - sig)))).astype(bf16)
    up_grad = (inner_grad * silu).astype(bf16)

    second_grad_part = (against(gate_grad, gate_w) + against(up_grad, up_w)).astype(bf16)
    second_grad = scatter_rows(
        lambda d: second_grad_part[d * own_rows : (d + 1) * own_rows], "fsdp", shards
    )
    down_part = matmul(inner, down_weight, bf16)
    layer_rows = residual + scatter_rows(
        lambda d: down_part[d * own_rows : (d + 1) * own_rows], "fsdp", shards
    )
    layer_output = give_back(layer_rows.astype(bf16))

    down_term = outer_sum(inner, cot, bf16)
    down_grad = lax.psum(down_term, everyone).astype(f32)

    tiny = rows // members

    def reorder(term):
        return term.reshape(shards, members, tiny, part).transpose(1, 0, 2, 3)

    gate_up_term = jnp.stack(
        [reorder(outer_sum(second, gate_grad, bf16)), reorder(outer_sum(second, up_grad, bf16))],
        axis=1,
    )
    gate_up_piece = lax.psum_scatter(gate_up_term, everyone, scatter_dimension=0, tiled=False)
    spread = jnp.zeros_like(gate_up_piece)
    for d in range(shards):
        piece = lax.dynamic_index_in_dim(gate_up_piece, f ^ d, 1, False)
        came = swap(piece, "fsdp", shards, d) if d else piece
        spread = lax.dynamic_update_index_in_dim(spread, came, f ^ d, 1)
    gate_up_all = lax.all_gather(spread, everyone, axis=0, tiled=False)
    gate_grad_w, up_grad_w = (
        gate_up_all[:, i].transpose(0, 2, 1, 3).reshape(rows, hidden).astype(f32) for i in range(2)
    )

    output_rows = cotangent_own.astype(f32)
    scaled = second_grad * gain_second
    residual_grad = (
        output_rows
        + scale_second * scaled
        - residual
        * (scale_second * scale_second * scale_second)
        * jnp.mean(scaled * residual, axis=-1, keepdims=True)
    )
    gain_second_term = jnp.sum(second_grad * residual * scale_second, axis=0)
    branch_own = residual_grad.astype(bf16)
    branch = team_gather(branch_own)

    attended_grad = against(branch, wo, bf16)
    wo_term = outer_sum(attended, branch, bf16)
    lin_grad = attend_backward(start, qkv, attended, attended_grad, lse, cosine, sine)
    first_grad = team_scatter(against(lin_grad, wqkv, bf16))
    wqkv_term = outer_sum(first, lin_grad, bf16)

    scaled = first_grad * gain_first
    input_rows = (
        residual_grad
        + scale_first * scaled
        - activation
        * (scale_first * scale_first * scale_first)
        * jnp.mean(scaled * activation, axis=-1, keepdims=True)
    )
    gain_first_term = jnp.sum(first_grad * activation * scale_first, axis=0)
    input_gradient = give_back(input_rows.astype(bf16))

    def weight_rows(term):
        size = term.shape[0] // shards

        def block(d):
            return lax.dynamic_slice_in_dim(term, (f ^ d) * size, size, 0)

        return scatter_rows(block, "fsdp", shards).astype(bf16)

    stride = team // copies
    if stride == 1:
        same_heads = None
    else:
        same_heads = [list(range(i, lengths, stride)) for i in range(stride)]
    wqkv_sum, wo_sum = (
        lax.psum(weight_rows(term), "seq", axis_index_groups=same_heads)
        for term in (wqkv_term, wo_term)
    )

    def team_stack(value):
        came = [value] + [swap(value, everyone, members, d) for d in range(1, team)]
        return [lax.select_n(mine ^ u, *came) for u in range(team)]

    wqkv_all = [v.reshape(rows, pairs, 3, LANES) for v in team_stack(wqkv_sum)]
    output_grad_w = jnp.concatenate(team_stack(wo_sum), axis=0).astype(f32)

    def head_gradient(i):
        split = [v[:, :, i].reshape(rows, shards, heads_width) for v in wqkv_all]
        return jnp.stack(split, axis=2).reshape(rows, features).astype(f32)

    gain_terms = lax.psum(jnp.stack([gain_first_term, gain_second_term]), ("seq", "fsdp", "rep"))
    gain_grads = lax.dynamic_slice_in_dim(gain_terms, f * rows, rows, 1)
    return (
        layer_output,
        input_gradient,
        gain_grads[0],
        head_gradient(0),
        head_gradient(1),
        head_gradient(2),
        output_grad_w,
        gain_grads[1],
        gate_grad_w,
        up_grad_w,
        down_grad,
    )


def solution(mesh):
    placed = (
        P(("fsdp", "rep"), "seq", None),
        P(("fsdp", "rep"), "seq", None),
        P(("fsdp", "rep")),
        P("fsdp"),
        P("fsdp", None),
        P("fsdp", None),
        P("fsdp", None),
        P("fsdp", None),
        P("fsdp"),
        P("fsdp", None),
        P("fsdp", None),
        P("fsdp", None),
    )
    return jax.shard_map(
        local,
        mesh=mesh,
        in_specs=placed,
        out_specs=(
            P(("fsdp", "rep"), "seq", None),
            P(("fsdp", "rep"), "seq", None),
            P("fsdp"),
            P("fsdp", None),
            P("fsdp", None),
            P("fsdp", None),
            P("fsdp", None),
            P("fsdp"),
            P("fsdp", None),
            P("fsdp", None),
            P("fsdp", None),
        ),
        check_vma=False,
    )
```

time: 4660 us -> 1800 us (0.39)
  waiting for transfers between devices: 3740 us -> 789 us
  matrix products: 602 us -> 297 us
  blocking collectives: 33.8 us -> 157 us
  local copies, waits for them, and re-layouts: 131 us -> 224 us
  starting transfers between devices: 1.71 us -> 88.1 us
  Pallas kernels: 0 us -> 79.8 us
    all_gather x11 -> x3, waiting for transfers between devices: 1470 us -> 83.2 us  [the longest x1 61.6 us: local(): wqkv = lax.all_gather(wqkv_rows, 'fsdp', axis=0, tiled=True)]
    reduce_scatter x8 -> x0, waiting for transfers between devices: 769 us -> none  [the longest x2 270 us: one_batch(): lax.psum_scatter(value_terms, 'seq', scatter_dimension=0, tiled=True)]
    unnamed x18 -> x6, waiting for transfers between devices: 878 us -> 247 us
    psum x1, waiting for transfers between devices: 628 us -> 123 us  [local(): lax.psum(weight_rows(term), 'seq', axis_index_groups=same_heads)]
    ppermute x0 -> x65, waiting for transfers between devices: none -> 336 us  [the longest x56 310 us: swap(): return lax.ppermute(value, axis, [(i, i ^ distance) for i in range(size)])]
    dot_general x70 -> x5, matrix products: 336 us -> 105 us  [matmul(): return jnp.dot(left_op, right_op, preferred_element_type=f32).astype(out)]
    psum x1, blocking collectives: 13.2 us -> 157 us  [local(): lax.psum(jnp.stack([gain_first_term, gain_second_term]), ('seq', 'fsdp',...]
    ppermute x0 -> x65, starting transfers between devices: none -> 87.9 us  [the longest x56 64.6 us: swap(): return lax.ppermute(value, axis, [(i, i ^ distance) for i in range(size)])]
  transfers between devices with their start and end apart: 23 -> 70, of which waited for: 22 -> 27; matrix products, arithmetic and copies ran while one was open for 5% -> 24% of each run, Pallas kernels for 0% -> 4%
where the time goes in v1:
time: 1800 us; the launch traced here: 1790 us
  waiting for transfers between devices  789 us (44%)
  matrix products  297 us (16%)
  local copies, waits for them, and re-layouts  224 us (12%)
  blocking collectives  157 us (9%)
  other arithmetic  135 us (8%)
  starting transfers between devices  88.1 us (5%)
  Pallas kernels  79.8 us (4%)
    ppermute x56, waiting for transfers between devices, swap(): return lax.ppermute(value, axis, [(i, i ^ distance) for i in range(size)])  310 us
    unnamed x6, waiting for transfers between devices  247 us
    psum x1, blocking collectives, local(): lax.psum(jnp.stack([gain_first_term, gain_second_term]), ('seq', 'fsdp',...  157 us
    psum x1, waiting for transfers between devices, local(): lax.psum(weight_rows(term), 'seq', axis_index_groups=same_heads)  123 us
    dot_general x5, matrix products, matmul(): return jnp.dot(left_op, right_op, preferred_element_type=f32).astype(out)  105 us
    dot_general x5, matrix products, against(): lax.dot_general(left_op, right_op, (((1,), (1,)), ((), ())), preferred_el...  95.9 us
    dot_general x5, matrix products, outer_sum(): lax.dot_general(left_op, right_op, (((0,), (0,)), ((), ())), preferred_el...  95.5 us
    unnamed x127, local copies, waits for them, and re-layouts  88.2 us
  transfers between devices with their start and end apart: 70, of which 27 were waited for; matrix products, arithmetic and copies ran while one was open for 24% of the time, Pallas kernels for 4%

profile of v1, /device:TPU:9, one launch (start us, length us, event | category | flops | bytes accessed | tf_op | source)
XLA Modules:
  0.0 1786.4 jit_solution(15630268587432487911)
XLA Ops:
  67.6 21.2 %collective-permute-done.1 = bf16[256,2048]{1,0:T(8,128)(2,1)} collective-permute-done((bf16[256,2048]{1,0:T(8,128)(2,1)}, bf16[256,2048]{1,0:T(8,128)(2,1)}, u32[]{:S(2)}, u32[]{:S(2)}) %collective-permute-start.1) | collective-permute-done | bytes 1048608 | tf_op jit(solution)/shard_map/ppermute | solution.py:379
  122.5 22.4 %collective-permute-done.20 = bf16[512,1024]{1,0:T(8,128)(2,1)} collective-permute-done((bf16[512,1024]{1,0:T(8,128)(2,1)}, bf16[512,1024]{1,0:T(8,128)(2,1)}, u32[]{:S(2)}, u32[]{:S(2)}) %collective-permute-start.20) | collective-permute-done | bytes 1048608 | tf_op jit(solution)/shard_map/ppermute | solution.py:304
  159.3 61.6 %all-gather.4.cloned.1.call-done = bf16[2048,3072]{0,1:T(8,128)(2,1)} async-done(((bf16[512,3072]{0,1:T(8,128)(2,1)}), bf16[2048,3072]{0,1:T(8,128)(2,1)}) %all-gather.4.cloned.1.call-update) | async-done | bytes 12582928 | tf_op jit(solution)/shard_map/all_gather | solution.py:442
  220.9 19.1 %fusion.16.lin_ref = f32[1024,3072]{1,0:T(8,128)} fusion(bf16[2048,3072]{0,1:T(8,128)(2,1)} %all-gather.4.cloned.1.call-done, bf16[512,2048]{1,0:T(8,128)(2,1)} %get-tuple-element.130, bf16[512,2048]{1,0:T(8,128)(2,1)} %get-tuple-element.129), kind=kOutput, calls=%fused_computation.66 | convolution fusion | flops 12893290496 | bytes 29360128 | tf_op jit(solution)/shard_map/dot_general | solution.py:27
  241.1 36.4 %attend_forward.1 = (bf16[1024,1024]{1,0:T(8,128)(2,1)}, bf16[1024,3072]{1,0:T(8,128)(2,1)}, f32[8,4,512]{2,1,0:T(4,128)}) custom-call(s32[1]{0:T(128)} %collective-permute-done.2.start_ref, f32[1024,3072]{1,0:T(8,128)} %fusion.16.lin_ref, f32[1024,128]{1,0:T(8,128)} %get-tuple-element.168.cos_ref, f32[1024,128]{1,0:T(8,128)} %get-tuple-element.169.sin_ref), custom_call_target="tpu_custom_call" | custom-call | flops 8589934592 | bytes 20971520 | tf_op jit(solution)/shard_map/attend_forward/pallas_call | solution.py:232
  277.5 21.7 %all-gather.6.cloned.1.call-done = bf16[1024,2048]{1,0:T(8,128)(2,1)} async-done(((bf16[256,2048]{1,0:T(8,128)(2,1)}), bf16[1024,2048]{1,0:T(8,128)(2,1)}) %all-gather.6.cloned.1.call-update) | async-done | bytes 4194320 | tf_op jit(solution)/shard_map/all_gather | solution.py:444
  341.9 17.8 collective-permute-done.36
  367.5 22.4 %fusion.34 = f32[2048,2048]{1,0:T(8,128)} fusion(bf16[2048,2048]{1,0:T(8,128)(2,1)S(1)} %bitcast.192, bf16[2048,2048]{1,0:T(8,128)(2,1)} %param.23), kind=kOutput, calls=%fused_computation.197 | convolution fusion | flops 17179869184 | bytes 33554432 | tf_op jit(solution)/shard_map/dot_general | solution.py:37
  416.6 19.6 %collective-permute-done.10 = bf16[256,2048]{1,0:T(8,128)(2,1)S(1)} collective-permute-done((bf16[256,2048]{1,0:T(8,128)(2,1)S(1)}, bf16[256,2048]{1,0:T(8,128)(2,1)S(1)}, u32[]{:S(2)}, u32[]{:S(2)}) %collective-permute-start.10) | collective-permute-done | bytes 1048608 | tf_op jit(solution)/shard_map/ppermute | solution.py:304
  436.4 22.3 %collective-permute-done.12 = bf16[256,2048]{1,0:T(8,128)(2,1)S(1)} collective-permute-done((bf16[256,2048]{1,0:T(8,128)(2,1)S(1)}, bf16[256,2048]{1,0:T(8,128)(2,1)S(1)}, u32[]{:S(2)}, u32[]{:S(2)}) %collective-permute-start.12) | collective-permute-done | bytes 1048608 | tf_op jit(solution)/shard_map/ppermute | solution.py:304
  458.9 20.6 %fusion.2 = f32[2048,2048]{1,0:T(8,128)} fusion(bf16[2048,2048]{1,0:T(8,128)(2,1)S(1)} %constant_dynamic-update-slice_fusion, bf16[2048,1024]{1,0:T(8,128)(2,1)S(1)} %get-tuple-element.114, bf16[2048,1024]{1,0:T(8,128)(2,1)S(1)} %get-tuple-element.113), kind=kOutput, calls=%fused_computation.27 | convolution fusion | flops 17196646400 | bytes 33554432 | tf_op jit(solution)/shard_map/dot_general | solution.py:27
  479.6 35.6 %multiply_convert_fusion.1 = (bf16[2048,2048]{1,0:T(8,128)(2,1)}, bf16[2048,2048]{1,0:T(8,128)(2,1)}, bf16[2048,2048]{1,0:T(8,128)(2,1)}) fusion(f32[2048,2048]{1,0:T(8,128)} %fusion.34, f32[2048,2048]{1,0:T(8,128)} %fusion.2, bf16[2048,2048]{1,0:T(8,128)(2,1)} %copy-done.29, bf16[2048,1024]{1,0:T(8,128)(2,1)} %get-tuple-element.109, ...), kind=kOutput, calls=%fused_computation.5 | convolution fusion | flops 17259560960 | bytes 75497472 | tf_op jit(solution)/shard_map/dot_general | solution.py:27
  515.1 24.6 %fusion.1 = f32[2048,2048]{1,0:T(8,128)} fusion(bf16[2048,2048]{1,0:T(8,128)(2,1)} %get-tuple-element.82, bf16[2048,1024]{1,0:T(8,128)(2,1)} %copy-done.20, bf16[2048,1024]{1,0:T(8,128)(2,1)} %copy-done.19), kind=kOutput, calls=%fused_computation.26 | convolution fusion | flops 17196646400 | bytes 33554432 | tf_op jit(solution)/shard_map/dot_general | solution.py:37
  539.7 25.5 %add_convert_fusion = bf16[2048,2048]{1,0:T(8,128)(2,1)} fusion(f32[2048,2048]{1,0:T(8,128)} %fusion.1, bf16[2048,2048]{1,0:T(8,128)(2,1)} %get-tuple-element.81, bf16[2048,1024]{1,0:T(8,128)(2,1)} %get-tuple-element.109, bf16[2048,1024]{1,0:T(8,128)(2,1)} %get-tuple-element.108), kind=kOutput, calls=%fused_computation.3 | convolution fusion | flops 17205035008 | bytes 41943040 | tf_op jit(solution)/shard_map/dot_general | solution.py:37
  569.9 22.7 %convolution_convert_fusion.4 = bf16[2048,2048]{1,0:T(8,128)(2,1)S(1)} fusion(bf16[2048,2048]{1,0:T(8,128)(2,1)} %get-tuple-element.83, bf16[2048,2048]{1,0:T(8,128)(2,1)} %param.23), kind=kOutput, calls=%fused_computation.25 | convolution fusion | flops 17184063488 | bytes 25165824 | tf_op jit(solution)/shard_map/dot_general | solution.py:27
  594.9 23.7 %convolution_convert_fusion.2 = bf16[2048,2048]{1,0:T(8,128)(2,1)} fusion(bf16[2048,2048]{1,0:T(8,128)(2,1)} %copy-done.29, bf16[2048,2048]{1,0:T(8,128)(2,1)} %get-tuple-element.82), kind=kOutput, calls=%fused_computation.23 | convolution fusion | flops 17184063488 | bytes 25165824 | tf_op jit(solution)/shard_map/dot_general | solution.py:31
  640.4 23.9 %convolution_convert_fusion.3 = bf16[2048,2048]{1,0:T(8,128)(2,1)} fusion(bf16[2048,2048]{1,0:T(8,128)(2,1)} %copy-done.29, bf16[2048,2048]{1,0:T(8,128)(2,1)} %get-tuple-element.81), kind=kOutput, calls=%fused_computation.24 | convolution fusion | flops 17184063488 | bytes 25165824 | tf_op jit(solution)/shard_map/dot_general | solution.py:31
  665.6 19.5 %collective-permute-done.24 = bf16[256,2048]{1,0:T(8,128)(2,1)S(1)} collective-permute-done((bf16[256,2048]{1,0:T(8,128)(2,1)S(1)}, bf16[256,2048]{1,0:T(8,128)(2,1)S(1)}, u32[]{:S(2)}, u32[]{:S(2)}) %collective-permute-start.24) | collective-permute-done | bytes 1048608 | tf_op jit(solution)/shard_map/ppermute | solution.py:304
  719.9 21.5 %convolution_convert_fusion.1 = bf16[2048,2048]{1,0:T(8,128)(2,1)} fusion(bf16[2048,2048]{1,0:T(8,128)(2,1)} %get-tuple-element.83, bf16[2048,2048]{1,0:T(8,128)(2,1)S(1)} %bitcast.194), kind=kOutput, calls=%fused_computation.22 | convolution fusion | flops 17184063488 | bytes 25165824 | tf_op jit(solution)/shard_map/dot_general | solution.py:31
  781.5 43.4 %attend_backward.1 = bf16[1024,3072]{1,0:T(8,128)(2,1)} custom-call(s32[1]{0:T(128)} %collective-permute-done.2.start_ref, bf16[1024,3072]{1,0:T(8,128)(2,1)} %get-tuple-element.15.qkv_ref, bf16[1024,1024]{1,0:T(8,128)(2,1)} %get-tuple-element.14.out_ref, bf16[1024,1024]{1,0:T(8,128)(2,1)} %fusion.17.grad_ref, f32[8,4,512]{2,1,0:T(4,128)} %get-tuple-element.16.lse_ref, ...), custom_call_target="tpu_custom_call" | custom-call | flops 21474836480 | bytes 16777216 | tf_op jit(solution)/shard_map/attend_backward/pallas_call | solution.py:273
  825.0 19.8 %convolution_convert_fusion = bf16[2048,3072]{1,0:T(8,128)(2,1)} fusion(bf16[1024,3072]{1,0:T(8,128)(2,1)} %attend_backward.1, bf16[512,2048]{1,0:T(8,128)(2,1)} %get-tuple-element.130, bf16[512,2048]{1,0:T(8,128)(2,1)S(1)} %copy-done.22), kind=kOutput, calls=%fused_computation.9 | convolution fusion | flops 12899581952 | bytes 23068672 | tf_op jit(solution)/shard_map/dot_general | solution.py:31
  852.3 34.5 %collective-permute-done.49 = bf16[256,3072]{1,0:T(8,128)(2,1)} collective-permute-done((bf16[256,3072]{1,0:T(8,128)(2,1)}, bf16[256,3072]{1,0:T(8,128)(2,1)}, u32[]{:S(2)}, u32[]{:S(2)}) %collective-permute-start.49) | collective-permute-done | bytes 1572896 | tf_op jit(solution)/shard_map/ppermute | solution.py:304
  902.1 29.5 %collective-permute-done.56 = bf16[128,2048]{1,0:T(8,128)(2,1)S(1)} collective-permute-done((bf16[128,2048]{1,0:T(8,128)(2,1)S(1)}, bf16[128,2048]{1,0:T(8,128)(2,1)S(1)}, u32[]{:S(2)}, u32[]{:S(2)}) %collective-permute-start.56) | collective-permute-done | bytes 524320 | tf_op jit(solution)/shard_map/ppermute | solution.py:304
  945.8 24.4 %collective-permute-done.59 = bf16[128,2048]{1,0:T(8,128)(2,1)S(1)} collective-permute-done((bf16[128,2048]{1,0:T(8,128)(2,1)S(1)}, bf16[128,2048]{1,0:T(8,128)(2,1)S(1)}, u32[]{:S(2)}, u32[]{:S(2)}) %collective-permute-start.59) | collective-permute-done | bytes 524320 | tf_op jit(solution)/shard_map/ppermute | solution.py:304
  970.2 22.5 %collective-permute-done.57 = bf16[128,2048]{1,0:T(8,128)(2,1)S(1)} collective-permute-done((bf16[128,2048]{1,0:T(8,128)(2,1)S(1)}, bf16[128,2048]{1,0:T(8,128)(2,1)S(1)}, u32[]{:S(2)}, u32[]{:S(2)}) %collective-permute-start.57) | collective-permute-done | bytes 524320 | tf_op jit(solution)/shard_map/ppermute | solution.py:304
  1014.6 247.4 %all-reduce.6.cloned.1.call-done = (bf16[8,2,4,64,2048]{4,3,2,0,1:T(8,128)(2,1)}, bf16[2048,2048]{1,0:T(8,128)(2,1)}) async-done(((bf16[8,2,4,64,2048]{4,3,2,0,1:T(8,128)(2,1)}, bf16[2048,2048]{1,0:T(8,128)(2,1)}), (bf16[8,2,4,64,2048]{4,3,2,0,1:T(8,128)(2,1)}, bf16[2048,2048]{1,0:T(8,128)(2,1)})) %all-reduce.6.cloned.1.call-update) | async-done | bytes 25165840
  1290.1 17.5 convolution_convert_fusion.5
  1328.7 122.5 %all-reduce.8.cloned.1.call-done = (bf16[512,3072]{1,0:T(8,128)(2,1)}, bf16[256,2048]{1,0:T(8,128)(2,1)}) async-done(((bf16[512,3072]{1,0:T(8,128)(2,1)}, bf16[256,2048]{1,0:T(8,128)(2,1)}), (bf16[512,3072]{1,0:T(8,128)(2,1)}, bf16[256,2048]{1,0:T(8,128)(2,1)})) %all-reduce.8.cloned.1.call-update) | async-done | bytes 4194320 | tf_op jit(solution)/shard_map/psum | solution.py:573
  1471.5 157.1 %psum.28 = f32[2,2048]{1,0:T(2,128)S(1)} all-reduce(f32[2,2048]{1,0:T(2,128)S(1)} %pad_maximum_fusion.24), channel_id=1, replica_groups=mesh['seq'=4,'fsdp'=4,'rep'=2] {'seq','fsdp','rep'}, use_global_device_ids=true, to_apply=%region_6.7 | all-reduce | flops 4096 | bytes 32768 | tf_op jit(solution)/shard_map/psum | solution.py:588
  1705.4 20.9 %copy.104 = f32[8,64,4,2048]{3,2,1,0:T(4,128)} copy(f32[8,64,4,2048]{3,1,2,0:T(8,128)} %get-tuple-element.85) | data formatting | bytes 33554432 | tf_op jit(solution)/shard_map/convert_element_type | solution.py:526
  1726.3 20.5 %copy.111 = f32[64,8,4,2048]{3,1,2,0:T(8,128)} copy(f32[64,8,4,2048]{3,2,1,0:T(4,128)} %bitcast.159) | data formatting | bytes 33554432
  1759.0 20.4 %copy.112 = f32[64,8,4,2048]{3,1,2,0:T(8,128)} copy(f32[64,8,4,2048]{3,2,1,0:T(4,128)} %bitcast.160) | data formatting | bytes 33554432
  (369 shorter events, 508.0 us)
Async XLA Ops:
  7.2 213.7 %all-gather.4.cloned.1.call-start = ((), (), s32[]{:S(2)}) async-start(), calls=%async_computation | async-start | bytes 15728640 | tf_op jit(solution)/shard_map/all_gather | solution.py:442
  24.5 274.7 %all-gather.6.cloned.1.call-start = ((), (), s32[]{:S(2)}) async-start(), calls=%async_computation.1 | async-start | bytes 5242880 | tf_op jit(solution)/shard_map/all_gather | solution.py:444
  37.3 1224.7 %all-reduce.6.cloned.1.call-start = ((), (), s32[]{:S(2)}) async-start(), calls=%async_computation.3 | async-start | bytes 50331648
  56.0 91.5 %collective-permute-start.30 = (bf16[256,2048]{1,0:T(8,128)(2,1)}, bf16[256,2048]{1,0:T(8,128)(2,1)S(1)}, u32[]{:S(2)}, u32[]{:S(2)}) collective-permute-start(bf16[256,2048]{1,0:T(8,128)(2,1)} %get-tuple-element.144), channel_id=1, source_target_pairs={{0,0},{1,16},{8,8},{9,24},{16,1},{17,17},{24,9},{25,25},{2,2},{3,1... | collective-permute-start | bytes 3145736 | tf_op jit(solution)/shard_map/ppermute | solution.py:379
  60.4 87.4 %collective-permute-start.31 = (bf16[256,2048]{1,0:T(8,128)(2,1)}, bf16[256,2048]{1,0:T(8,128)(2,1)}, u32[]{:S(2)}, u32[]{:S(2)}) collective-permute-start(bf16[256,2048]{1,0:T(8,128)(2,1)} %get-tuple-element.143), channel_id=1, source_target_pairs={{0,8},{1,24},{8,0},{9,16},{16,9},{17,25},{24,1},{25,17},{2,10},{3,... | collective-permute-start | bytes 3145736 | tf_op jit(solution)/shard_map/ppermute | solution.py:379
  118.1 121.9 %collective-permute-start.2 = (s32[1]{0:T(128)}, s32[1]{0:T(128)}, u32[]{:S(2)}, u32[]{:S(2)}) collective-permute-start(s32[1]{0:T(128)} %dynamic_slice.120), channel_id=1, source_target_pairs={{0,0},{1,16},{8,8},{9,24},{16,1},{17,17},{24,9},{25,25},{2,2},{3,1... | collective-permute-start | bytes 20 | tf_op jit(solution)/shard_map/ppermute | solution.py:430
  144.9 161.9 %collective-permute-start.14 = (bf16[512,1024]{1,0:T(8,128)(2,1)}, bf16[512,1024]{1,0:T(8,128)(2,1)}, u32[]{:S(2)}, u32[]{:S(2)}) collective-permute-start(bf16[512,1024]{1,0:T(8,128)(2,1)} %get-tuple-element.111), channel_id=1, source_target_pairs={{0,2},{2,0},{4,6},{6,4},{1,3},{3,1},{5,7},{7,5},{8,10},{10,8},{12,... | collective-permute-start | bytes 3145736 | tf_op jit(solution)/shard_map/ppermute | solution.py:304
  147.5 161.9 %collective-permute-start.15 = (bf16[512,1024]{1,0:T(8,128)(2,1)}, bf16[512,1024]{1,0:T(8,128)(2,1)}, u32[]{:S(2)}, u32[]{:S(2)}) collective-permute-start(bf16[512,1024]{1,0:T(8,128)(2,1)} %get-tuple-element.112), channel_id=1, source_target_pairs={{0,4},{2,6},{4,0},{6,2},{1,5},{3,7},{5,1},{7,3},{8,12},{10,14},{12... | collective-permute-start | bytes 3145736 | tf_op jit(solution)/shard_map/ppermute | solution.py:304
  148.5 164.0 %collective-permute-start.16 = (bf16[512,1024]{1,0:T(8,128)(2,1)}, bf16[512,1024]{1,0:T(8,128)(2,1)}, u32[]{:S(2)}, u32[]{:S(2)}) collective-permute-start(bf16[512,1024]{1,0:T(8,128)(2,1)} %get-tuple-element.110), channel_id=1, source_target_pairs={{0,6},{2,4},{4,2},{6,0},{1,7},{3,5},{5,3},{7,1},{8,14},{10,12},{12... | collective-permute-start | bytes 3145736 | tf_op jit(solution)/shard_map/ppermute | solution.py:304
  154.5 160.5 %collective-permute-start.32 = (bf16[256,2048]{1,0:T(8,128)(2,1)S(1)}, bf16[256,2048]{1,0:T(8,128)(2,1)}, u32[]{:S(2)}, u32[]{:S(2)}) collective-permute-start(bf16[256,2048]{1,0:T(8,128)(2,1)S(1)} %get-tuple-element.74), channel_id=1, source_target_pairs={{0,2},{2,0},{4,6},{6,4},{1,3},{3,1},{5,7},{7,5},{8,10},{10,8},{12,... | collective-permute-start | bytes 3145736 | tf_op jit(solution)/shard_map/ppermute | solution.py:304
  240.0 78.5 %collective-permute-start.35 = (bf16[256,2048]{1,0:T(8,128)(2,1)}, bf16[256,2048]{1,0:T(8,128)(2,1)}, u32[]{:S(2)}, u32[]{:S(2)}) collective-permute-start(bf16[256,2048]{1,0:T(8,128)(2,1)} %get-tuple-element.72), channel_id=1, source_target_pairs={{0,4},{2,6},{4,0},{6,2},{1,5},{3,7},{5,1},{7,3},{8,12},{10,14},{12... | collective-permute-start | bytes 3145736 | tf_op jit(solution)/shard_map/ppermute | solution.py:304
  332.6 57.6 %collective-permute-start.21 = (bf16[2048,1024]{1,0:T(8,128)(2,1)}, bf16[2048,1024]{1,0:T(8,128)(2,1)S(1)}, u32[]{:S(2)}, u32[]{:S(2)}) collective-permute-start(bf16[2048,1024]{1,0:T(8,128)(2,1)} %bitcast.24), channel_id=1, source_target_pairs={{0,1},{1,0},{2,3},{3,2},{4,5},{5,4},{6,7},{7,6},{8,9},{9,8},{10,11... | collective-permute-start | bytes 12582920 | tf_op jit(solution)/shard_map/ppermute | solution.py:304
  337.2 57.3 %collective-permute-start.17 = (bf16[2048,1024]{1,0:T(8,128)(2,1)}, bf16[2048,1024]{1,0:T(8,128)(2,1)S(1)}, u32[]{:S(2)}, u32[]{:S(2)}) collective-permute-start(bf16[2048,1024]{1,0:T(8,128)(2,1)} %bitcast.19), channel_id=1, source_target_pairs={{0,1},{1,0},{2,3},{3,2},{4,5},{5,4},{6,7},{7,6},{8,9},{9,8},{10,11... | collective-permute-start | bytes 12582920 | tf_op jit(solution)/shard_map/ppermute | solution.py:304
  394.3 64.5 %collective-permute-start.12 = (bf16[256,2048]{1,0:T(8,128)(2,1)S(1)}, bf16[256,2048]{1,0:T(8,128)(2,1)S(1)}, u32[]{:S(2)}, u32[]{:S(2)}) collective-permute-start(bf16[256,2048]{1,0:T(8,128)(2,1)S(1)} %collective-permute-done.8), channel_id=1, source_target_pairs={{0,4},{2,6},{4,0},{6,2},{1,5},{3,7},{5,1},{7,3},{8,12},{10,14},{12... | collective-permute-start | bytes 3145736 | tf_op jit(solution)/shard_map/ppermute | solution.py:304
  568.1 68.3 %collective-permute-start.38 = (bf16[256,2048]{1,0:T(8,128)(2,1)S(1)}, bf16[256,2048]{1,0:T(8,128)(2,1)S(1)}, u32[]{:S(2)}, u32[]{:S(2)}) collective-permute-start(bf16[256,2048]{1,0:T(8,128)(2,1)S(1)} %get-tuple-element.98), channel_id=1, source_target_pairs={{0,2},{2,0},{4,6},{6,4},{1,3},{3,1},{5,7},{7,5},{8,10},{10,8},{12,... | collective-permute-start | bytes 3145736 | tf_op jit(solution)/shard_map/ppermute | solution.py:304
  569.6 67.2 %collective-permute-start.42 = (bf16[256,2048]{1,0:T(8,128)(2,1)S(1)}, bf16[256,2048]{1,0:T(8,128)(2,1)S(1)}, u32[]{:S(2)}, u32[]{:S(2)}) collective-permute-start(bf16[256,2048]{1,0:T(8,128)(2,1)S(1)} %get-tuple-element.99), channel_id=1, source_target_pairs={{0,4},{2,6},{4,0},{6,2},{1,5},{3,7},{5,1},{7,3},{8,12},{10,14},{12... | collective-permute-start | bytes 3145736 | tf_op jit(solution)/shard_map/ppermute | solution.py:304
  618.6 71.0 %collective-permute-start.41 = (bf16[256,2048]{1,0:T(8,128)(2,1)S(1)}, bf16[256,2048]{1,0:T(8,128)(2,1)S(1)}, u32[]{:S(2)}, u32[]{:S(2)}) collective-permute-start(bf16[256,2048]{1,0:T(8,128)(2,1)S(1)} %get-tuple-element.100), channel_id=1, source_target_pairs={{0,4},{2,6},{4,0},{6,2},{1,5},{3,7},{5,1},{7,3},{8,12},{10,14},{12... | collective-permute-start | bytes 3145736 | tf_op jit(solution)/shard_map/ppermute | solution.py:304
  713.5 58.7 %collective-permute-start.44 = (bf16[512,2048]{1,0:T(8,128)(2,1)}, bf16[512,2048]{1,0:T(8,128)(2,1)}, u32[]{:S(2)}, u32[]{:S(2)}) collective-permute-start(bf16[512,2048]{1,0:T(8,128)(2,1)} %get-tuple-element.69), channel_id=1, source_target_pairs={{0,1},{1,0},{8,9},{9,8},{16,17},{17,16},{24,25},{25,24},{2,3},{3,2... | collective-permute-start | bytes 6291464 | tf_op jit(solution)/shard_map/ppermute | solution.py:304
  772.1 679.1 %all-reduce.8.cloned.1.call-start = ((), (), s32[]{:S(2)}) async-start(), calls=%async_computation.4 | async-start | bytes 8388608 | tf_op jit(solution)/shard_map/psum | solution.py:573
  851.9 82.3 %collective-permute-start.48 = (bf16[256,3072]{1,0:T(8,128)(2,1)}, bf16[256,3072]{1,0:T(8,128)(2,1)}, u32[]{:S(2)}, u32[]{:S(2)}) collective-permute-start(bf16[256,3072]{1,0:T(8,128)(2,1)} %get-tuple-element.92), channel_id=1, source_target_pairs={{0,2},{2,0},{4,6},{6,4},{1,3},{3,1},{5,7},{7,5},{8,10},{10,8},{12,... | collective-permute-start | bytes 4718600 | tf_op jit(solution)/shard_map/ppermute | solution.py:304
  852.0 82.6 %collective-permute-start.52 = (bf16[256,3072]{1,0:T(8,128)(2,1)}, bf16[256,3072]{1,0:T(8,128)(2,1)}, u32[]{:S(2)}, u32[]{:S(2)}) collective-permute-start(bf16[256,3072]{1,0:T(8,128)(2,1)} %get-tuple-element.94), channel_id=1, source_target_pairs={{0,4},{2,6},{4,0},{6,2},{1,5},{3,7},{5,1},{7,3},{8,12},{10,14},{12... | collective-permute-start | bytes 4718600 | tf_op jit(solution)/shard_map/ppermute | solution.py:304
  901.1 107.2 %collective-permute-start.51 = (bf16[256,3072]{1,0:T(8,128)(2,1)}, bf16[256,3072]{1,0:T(8,128)(2,1)}, u32[]{:S(2)}, u32[]{:S(2)}) collective-permute-start(bf16[256,3072]{1,0:T(8,128)(2,1)} %get-tuple-element.95), channel_id=1, source_target_pairs={{0,4},{2,6},{4,0},{6,2},{1,5},{3,7},{5,1},{7,3},{8,12},{10,14},{12... | collective-permute-start | bytes 4718600 | tf_op jit(solution)/shard_map/ppermute | solution.py:304
  934.6 61.1 %collective-permute-start.58 = (bf16[128,2048]{1,0:T(8,128)(2,1)S(1)}, bf16[128,2048]{1,0:T(8,128)(2,1)S(1)}, u32[]{:S(2)}, u32[]{:S(2)}) collective-permute-start(bf16[128,2048]{1,0:T(8,128)(2,1)S(1)} %get-tuple-element.125), channel_id=1, source_target_pairs={{0,4},{2,6},{4,0},{6,2},{1,5},{3,7},{5,1},{7,3},{8,12},{10,14},{12... | collective-permute-start | bytes 1572872 | tf_op jit(solution)/shard_map/ppermute | solution.py:304
  935.8 56.9 %collective-permute-start.57 = (bf16[128,2048]{1,0:T(8,128)(2,1)S(1)}, bf16[128,2048]{1,0:T(8,128)(2,1)S(1)}, u32[]{:S(2)}, u32[]{:S(2)}) collective-permute-start(bf16[128,2048]{1,0:T(8,128)(2,1)S(1)} %add_convert_fusion.12), channel_id=1, source_target_pairs={{0,4},{2,6},{4,0},{6,2},{1,5},{3,7},{5,1},{7,3},{8,12},{10,14},{12... | collective-permute-start | bytes 1572872 | tf_op jit(solution)/shard_map/ppermute | solution.py:304
  944.4 63.8 %collective-permute-start.53 = (bf16[256,3072]{1,0:T(8,128)(2,1)}, bf16[256,3072]{1,0:T(8,128)(2,1)}, u32[]{:S(2)}, u32[]{:S(2)}) collective-permute-start(bf16[256,3072]{1,0:T(8,128)(2,1)} %get-tuple-element.91), channel_id=1, source_target_pairs={{0,2},{2,0},{4,6},{6,4},{1,3},{3,1},{5,7},{7,5},{8,10},{10,8},{12,... | collective-permute-start | bytes 4718600 | tf_op jit(solution)/shard_map/ppermute | solution.py:304
  1013.3 679.7 %all-gather.8.cloned.1.call-start = ((), (), s32[]{:S(2)}) async-start(), calls=%async_computation.2 | async-start | bytes 18874368 | tf_op jit(solution)/shard_map/all_gather | solution.py:524
  1316.5 145.2 %collective-permute-start.28 = (bf16[256,2048]{1,0:T(8,128)(2,1)}, bf16[256,2048]{1,0:T(8,128)(2,1)}, u32[]{:S(2)}, u32[]{:S(2)}) collective-permute-start(bf16[256,2048]{1,0:T(8,128)(2,1)} %get-tuple-element.148), channel_id=1, source_target_pairs={{0,0},{16,1},{8,8},{24,9},{1,16},{17,17},{9,24},{25,25},{2,2},{18,... | collective-permute-start | bytes 3145736 | tf_op jit(solution)/shard_map/ppermute | solution.py:394
  1320.4 141.4 %collective-permute-start.29 = (bf16[256,2048]{1,0:T(8,128)(2,1)}, bf16[256,2048]{1,0:T(8,128)(2,1)}, u32[]{:S(2)}, u32[]{:S(2)}) collective-permute-start(bf16[256,2048]{1,0:T(8,128)(2,1)} %get-tuple-element.147), channel_id=1, source_target_pairs={{8,0},{24,1},{0,8},{16,9},{9,16},{25,17},{1,24},{17,25},{10,2},{26... | collective-permute-start | bytes 3145736 | tf_op jit(solution)/shard_map/ppermute | solution.py:394
  1451.2 196.8 %collective-permute-start.54 = (bf16[512,3072]{1,0:T(8,128)(2,1)}, bf16[512,3072]{1,0:T(8,128)(2,1)}, u32[]{:S(2)}, u32[]{:S(2)}) collective-permute-start(bf16[512,3072]{1,0:T(8,128)(2,1)} %get-tuple-element.67), channel_id=1, source_target_pairs={{0,1},{1,0},{8,9},{9,8},{16,17},{17,16},{24,25},{25,24},{2,3},{3,2... | collective-permute-start | bytes 9437192 | tf_op jit(solution)/shard_map/ppermute | solution.py:304
  1454.7 174.5 %collective-permute-start.46 = (bf16[256,2048]{1,0:T(8,128)(2,1)}, bf16[256,2048]{1,0:T(8,128)(2,1)}, u32[]{:S(2)}, u32[]{:S(2)}) collective-permute-start(bf16[256,2048]{1,0:T(8,128)(2,1)} %get-tuple-element.142), channel_id=1, source_target_pairs={{0,0},{16,1},{8,8},{24,9},{1,16},{17,17},{9,24},{25,25},{2,2},{18,... | collective-permute-start | bytes 3145736 | tf_op jit(solution)/shard_map/ppermute | solution.py:394
  1459.9 169.4 %collective-permute-start.47 = (bf16[256,2048]{1,0:T(8,128)(2,1)}, bf16[256,2048]{1,0:T(8,128)(2,1)}, u32[]{:S(2)}, u32[]{:S(2)}) collective-permute-start(bf16[256,2048]{1,0:T(8,128)(2,1)} %get-tuple-element.141), channel_id=1, source_target_pairs={{8,0},{24,1},{0,8},{16,9},{9,16},{25,17},{1,24},{17,25},{10,2},{26... | collective-permute-start | bytes 3145736 | tf_op jit(solution)/shard_map/ppermute | solution.py:394
  1465.2 178.9 %collective-permute-start.61 = (bf16[256,2048]{1,0:T(8,128)(2,1)S(1)}, bf16[256,2048]{1,0:T(8,128)(2,1)}, u32[]{:S(2)}, u32[]{:S(2)}) collective-permute-start(bf16[256,2048]{1,0:T(8,128)(2,1)S(1)} %copy-done.27), channel_id=1, source_target_pairs={{0,1},{1,0},{8,9},{9,8},{16,17},{17,16},{24,25},{25,24},{2,3},{3,2... | collective-permute-start | bytes 3145736 | tf_op jit(solution)/shard_map/ppermute | solution.py:304
  (92 other events, 2981.2 us)
Sparse Core Ops, SparseCore 0:
  24.6 196.1 all-gather.3
  223.3 75.8 all-gather.5
  772.2 489.7 all-reduce.5
  1264.9 186.2 all-reduce.7
  1452.6 188.7 all-gather.7

commit v2 on v1

--- a/solution.py
+++ b/solution.py
@@ -300,6 +300,128 @@
     )(start, qkv, out, grad, lse, cosine, sine)
 
 
+def widen_kernel(place_ref, mine_ref, other_ref, out_ref):
+    own = pl.program_id(0) == place_ref[0]
+
+    @pl.when(own)
+    def _():
+        out_ref[...] = mine_ref[...].astype(f32)
+
+    @pl.when(jnp.logical_not(own))
+    def _():
+        out_ref[...] = other_ref[...].astype(f32)
+
+
+def widen_halves(place, mine, other):
+    rows, width = mine.shape
+    block = rows
+    while block * width > 512 * 1024 and block % 32 == 0:
+        block //= 2
+    steps = rows // block
+    return pl.pallas_call(
+        widen_kernel,
+        grid_spec=pltpu.PrefetchScalarGridSpec(
+            num_scalar_prefetch=1,
+            grid=(2, steps),
+            in_specs=[
+                pl.BlockSpec((block, width), lambda u, i, p: (jnp.where(u == p[0], i, 0), 0)),
+                pl.BlockSpec((block, width), lambda u, i, p: (jnp.where(u == p[0], 0, i), 0)),
+            ],
+            out_specs=pl.BlockSpec((block, width), lambda u, i, p: (u * steps + i, 0)),
+        ),
+        out_shape=jax.ShapeDtypeStruct((2 * rows, width), f32),
+        cost_estimate=pl.CostEstimate(
+            flops=0, bytes_accessed=12 * rows * width, transcendentals=0
+        ),
+        name="widen_halves",
+    )(place, mine, other)
+
+
+def spread_heads_kernel(place_ref, mine_ref, other_ref, q_ref, k_ref, v_ref, *, group):
+    outs = (q_ref, k_ref, v_ref)
+    pairs = mine_ref.shape[1] // (3 * LANES)
+
+    def put(source_ref, place):
+        for p in range(pairs):
+            at = (p // group) * 2 * group * LANES + place * group * LANES + (p % group) * LANES
+            for i in range(3):
+                start = (3 * p + i) * LANES
+                outs[i][:, at : at + LANES] = source_ref[:, start : start + LANES].astype(f32)
+
+    for place in range(2):
+
+        @pl.when(place_ref[0] == place)
+        def _():
+            put(mine_ref, place)
+            put(other_ref, 1 - place)
+
+
+def spread_heads(place, mine, other, heads_width):
+    rows, width = mine.shape
+    full = 2 * width // 3
+    block = min(rows, 128)
+    return pl.pallas_call(
+        functools.partial(spread_heads_kernel, group=heads_width // LANES),
+        grid_spec=pltpu.PrefetchScalarGridSpec(
+            num_scalar_prefetch=1,
+            grid=(rows // block,),
+            in_specs=[pl.BlockSpec((block, width), lambda i, p: (i, 0))] * 2,
+            out_specs=[pl.BlockSpec((block, full), lambda i, p: (i, 0))] * 3,
+        ),
+        out_shape=[jax.ShapeDtypeStruct((rows, full), f32)] * 3,
+        cost_estimate=pl.CostEstimate(
+            flops=0, bytes_accessed=16 * rows * full, transcendentals=0
+        ),
+        name="spread_heads",
+    )(place, mine, other)
+
+
+def line_pairs(size, stride, first, last, step):
+    return [
+        (i * stride + o, (i + step) * stride + o)
+        for i in range(first, last + 1)
+        for o in range(stride)
+    ]
+
+
+def line_scatter(block_of, axis, size, stride=1):
+    count = size // stride
+    place = lax.axis_index(axis) // stride
+    total = block_of(place).astype(f32)
+    if count == 1:
+        return total
+    last = count - 1
+    up, down = block_of(last), block_of(0)
+    for s in range(last):
+        up = lax.ppermute(up, axis, line_pairs(size, stride, 0, s, 1))
+        down = lax.ppermute(down, axis, line_pairs(size, stride, last - s, last, -1))
+        if s + 1 < last:
+            here_up = block_of(jnp.minimum(last - 1 - s + place, last))
+            here_down = block_of(jnp.maximum(place - (last - 1 - s), 0))
+            up = (up.astype(f32) + here_up.astype(f32)).astype(bf16)
+            down = (down.astype(f32) + here_down.astype(f32)).astype(bf16)
+    return total + up.astype(f32) + down.astype(f32)
+
+
+def line_gather(value, axis, size, stride=1):
+    count = size // stride
+    place = lax.axis_index(axis) // stride
+    rows = value.shape[0]
+    last = count - 1
+    ups, downs = [value], [value]
+    for s in range(last):
+        ups.append(lax.ppermute(ups[-1], axis, line_pairs(size, stride, s, last - 1, 1)))
+        downs.append(lax.ppermute(downs[-1], axis, line_pairs(size, stride, 1, last - s, -1)))
+    out = jnp.zeros((count * rows,) + value.shape[1:], value.dtype)
+    out = lax.dynamic_update_slice_in_dim(out, value, place * rows, 0)
+    for s in range(last):
+        came = lax.select_n(place - 1 - s >= 0, downs[last - s], ups[s + 1])
+        out = lax.dynamic_update_slice_in_dim(
+            out, came, lax.rem(place - 1 - s + count, count) * rows, 0
+        )
+    return out
+
+
 def swap(value, axis, size, distance):
     return lax.ppermute(value, axis, [(i, i ^ distance) for i in range(size)])
 
@@ -319,6 +441,20 @@
                 held[d ^ bit] = swap(held[d], axis, size, bit)
         parts.append(held)
     return jnp.concatenate([parts[h][d] for d in range(size) for h in range(2)], axis=0)
+
+
+def gather_in_order(value, place, axis, size):
+    count = value.shape[0]
+    half = count // 2
+    out = jnp.zeros((size * count,) + value.shape[1:], value.dtype)
+    for h, (part, order) in enumerate(zip((value[:half], value[half:]), bit_orders(size))):
+        held = {0: part}
+        for bit in order:
+            for d in list(held):
+                held[d ^ bit] = swap(held[d], axis, size, bit)
+        for d, part in held.items():
+            out = lax.dynamic_update_slice_in_dim(out, part, (place ^ d) * count + h * half, 0)
+    return out
 
 
 def scatter_rows(block_of, axis, size):
@@ -439,9 +575,12 @@
         ],
         axis=2,
     ).reshape(rows, 3 * width)
-    wqkv = lax.all_gather(wqkv_rows, "fsdp", axis=0, tiled=True)
+    wqkv = gather_in_order(wqkv_rows, f, "fsdp", shards)
     wo_rows = lax.dynamic_slice_in_dim(output_weight, mine * heads_width, heads_width, 0)
-    wo = lax.all_gather(wo_rows, "fsdp", axis=0, tiled=True)
+    wqkv, wo_rows, gate_weight, up_weight, cotangent = lax.optimization_barrier(
+        (wqkv, wo_rows, gate_weight, up_weight, cotangent)
+    )
+    wo = gather_in_order(wo_rows, f, "fsdp", shards)
 
     gains = shard_gather_small(jnp.stack([attention_gain, feedforward_gain]))
     gain_first = gains[:, 0].reshape(features).astype(f32)
@@ -503,28 +642,34 @@
     )
     layer_output = give_back(layer_rows.astype(bf16))
 
-    down_term = outer_sum(inner, cot, bf16)
-    down_grad = lax.psum(down_term, everyone).astype(f32)
+    def members_scatter(value):
+        return lax.psum_scatter(value, everyone, scatter_dimension=0, tiled=True)
+
+    def members_gather(value):
+        return lax.all_gather(value, everyone, axis=0, tiled=False)
+
+    down_piece = members_scatter(outer_sum(inner, cot, bf16))
 
     tiny = rows // members
 
-    def reorder(term):
-        return term.reshape(shards, members, tiny, part).transpose(1, 0, 2, 3)
-
-    gate_up_term = jnp.stack(
-        [reorder(outer_sum(second, gate_grad, bf16)), reorder(outer_sum(second, up_grad, bf16))],
-        axis=1,
-    )
-    gate_up_piece = lax.psum_scatter(gate_up_term, everyone, scatter_dimension=0, tiled=False)
-    spread = jnp.zeros_like(gate_up_piece)
-    for d in range(shards):
-        piece = lax.dynamic_index_in_dim(gate_up_piece, f ^ d, 1, False)
-        came = swap(piece, "fsdp", shards, d) if d else piece
-        spread = lax.dynamic_update_index_in_dim(spread, came, f ^ d, 1)
-    gate_up_all = lax.all_gather(spread, everyone, axis=0, tiled=False)
-    gate_grad_w, up_grad_w = (
-        gate_up_all[:, i].transpose(0, 2, 1, 3).reshape(rows, hidden).astype(f32) for i in range(2)
-    )
+    def member_major(term):
+        blocks = term.reshape(shards, members, tiny, part)
+        return blocks.transpose(1, 0, 2, 3).reshape(features, part)
+
+    def shard_spread(piece):
+        piece = piece.reshape(shards, tiny, part)
+        out = jnp.zeros((tiny, hidden), bf16)
+        for d in range(shards):
+            came = lax.dynamic_index_in_dim(piece, f ^ d, 0, False)
+            came = swap(came, "fsdp", shards, d) if d else came
+            out = lax.dynamic_update_slice_in_dim(out, came, (f ^ d) * part, 1)
+        return out
+
+    gate_piece = members_scatter(member_major(outer_sum(second, gate_grad, bf16)))
+    up_piece = members_scatter(member_major(outer_sum(second, up_grad, bf16)))
+    down_grad = members_gather(down_piece).reshape(part, features).astype(f32)
+    gate_grad_w = members_gather(shard_spread(gate_piece)).reshape(rows, hidden).astype(f32)
+    up_grad_w = members_gather(shard_spread(up_piece)).reshape(rows, hidden).astype(f32)
 
     output_rows = cotangent_own.astype(f32)
     scaled = second_grad * gain_second
@@ -541,6 +686,7 @@
 
     attended_grad = against(branch, wo, bf16)
     wo_term = outer_sum(attended, branch, bf16)
+    attended_grad, wo_term = lax.optimization_barrier((attended_grad, wo_term))
     lin_grad = attend_backward(start, qkv, attended, attended_grad, lse, cosine, sine)
     first_grad = team_scatter(against(lin_grad, wqkv, bf16))
     wqkv_term = outer_sum(first, lin_grad, bf16)
@@ -565,35 +711,49 @@
         return scatter_rows(block, "fsdp", shards).astype(bf16)
 
     stride = team // copies
-    if stride == 1:
-        same_heads = None
-    else:
-        same_heads = [list(range(i, lengths, stride)) for i in range(stride)]
-    wqkv_sum, wo_sum = (
-        lax.psum(weight_rows(term), "seq", axis_index_groups=same_heads)
-        for term in (wqkv_term, wo_term)
-    )
+
+    def line_sum(value):
+        size = value.shape[0] * stride // lengths
+        piece = line_scatter(
+            lambda d: lax.dynamic_slice_in_dim(value, d * size, size, 0), "seq", lengths, stride
+        )
+        return line_gather(piece.astype(bf16), "seq", lengths, stride)
+
+    wo_sum = line_sum(weight_rows(wo_term))
+    wqkv_sum = line_sum(weight_rows(wqkv_term))
 
     def team_stack(value):
         came = [value] + [swap(value, everyone, members, d) for d in range(1, team)]
         return [lax.select_n(mine ^ u, *came) for u in range(team)]
 
-    wqkv_all = [v.reshape(rows, pairs, 3, LANES) for v in team_stack(wqkv_sum)]
-    output_grad_w = jnp.concatenate(team_stack(wo_sum), axis=0).astype(f32)
-
-    def head_gradient(i):
-        split = [v[:, :, i].reshape(rows, shards, heads_width) for v in wqkv_all]
-        return jnp.stack(split, axis=2).reshape(rows, features).astype(f32)
-
-    gain_terms = lax.psum(jnp.stack([gain_first_term, gain_second_term]), ("seq", "fsdp", "rep"))
+    if team == 2 and heads_width % LANES == 0:
+        place = mine.astype(jnp.int32).reshape(1)
+        output_grad_w = widen_halves(place, wo_sum, swap(wo_sum, everyone, members, 1))
+        head_gradients = spread_heads(
+            place, wqkv_sum, swap(wqkv_sum, everyone, members, 1), heads_width
+        )
+    else:
+        output_grad_w = jnp.concatenate(team_stack(wo_sum), axis=0).astype(f32)
+        wqkv_all = [v.reshape(rows, pairs, 3, LANES) for v in team_stack(wqkv_sum)]
+
+        def head_gradient(i):
+            split = [v[:, :, i].reshape(rows, shards, heads_width) for v in wqkv_all]
+            return jnp.stack(split, axis=2).reshape(rows, features).astype(f32)
+
+        head_gradients = [head_gradient(i) for i in range(3)]
+
+    gain_terms = jnp.stack([gain_first_term, gain_second_term])
+    for axis, size in (("rep", copies), ("fsdp", shards), ("seq", lengths)):
+        for bit in bit_orders(size)[0]:
+            gain_terms = gain_terms + swap(gain_terms, axis, size, bit)
     gain_grads = lax.dynamic_slice_in_dim(gain_terms, f * rows, rows, 1)
     return (
         layer_output,
         input_gradient,
         gain_grads[0],
-        head_gradient(0),
-        head_gradient(1),
-        head_gradient(2),
+        head_gradients[0],
+        head_gradients[1],
+        head_gradients[2],
         output_grad_w,
         gain_grads[1],
         gate_grad_w,

time: 1800 us -> 1490 us (0.83)
  waiting for transfers between devices: 789 us -> 620 us
  blocking collectives: 157 us -> 0 us
  starting transfers between devices: 88.1 us -> 195 us
  local copies, waits for them, and re-layouts: 224 us -> 147 us
  other arithmetic: 135 us -> 113 us
    unnamed x6, waiting for transfers between devices: 247 us -> 0.1 us
    psum x1 -> x0, blocking collectives: 157 us -> none  [local(): lax.psum(jnp.stack([gain_first_term, gain_second_term]), ('seq', 'fsdp',...]
    psum x1 -> x0, waiting for transfers between devices: 123 us -> none  [local(): lax.psum(weight_rows(term), 'seq', axis_index_groups=same_heads)]
    ppermute x56 -> x76, waiting for transfers between devices: 310 us -> 417 us  [swap(): return lax.ppermute(value, axis, [(i, i ^ distance) for i in range(size)])]
    ppermute x4, waiting for transfers between devices: 0.01 us -> 99.2 us  [give_back(): lax.ppermute(lax.dynamic_index_in_dim(blocks, lax.rem(local_seq + batch -...]
    all_gather x3, waiting for transfers between devices: 83.2 us -> 0.01 us  [members_gather(): return lax.all_gather(value, everyone, axis=0, tiled=False)]
    ppermute x0 -> x24, waiting for transfers between devices: none -> 79.8 us  [the longest x6 26.4 us: line_scatter(): lax.ppermute(down, axis, line_pairs(size, stride, last - s, last, -1))]
    ppermute x56 -> x76, starting transfers between devices: 64.6 us -> 119 us  [swap(): return lax.ppermute(value, axis, [(i, i ^ distance) for i in range(size)])]
  transfers between devices with their start and end apart: 70 -> 115, of which waited for: 27 -> 42; matrix products, arithmetic and copies ran while one was open for 24% -> 32% of each run, Pallas kernels for 4% -> 6%
where the time goes in v2:
time: 1490 us; the launch traced here: 1480 us
  waiting for transfers between devices  620 us (42%)
  matrix products  302 us (20%)
  starting transfers between devices  195 us (13%)
  local copies, waits for them, and re-layouts  147 us (10%)
  other arithmetic  113 us (8%)
  Pallas kernels  90.9 us (6%)
  between operations  15.8 us (1%)
    ppermute x76, waiting for transfers between devices, swap(): return lax.ppermute(value, axis, [(i, i ^ distance) for i in range(size)])  417 us
    ppermute x76, starting transfers between devices, swap(): return lax.ppermute(value, axis, [(i, i ^ distance) for i in range(size)])  119 us
    dot_general x5, matrix products, matmul(): return jnp.dot(left_op, right_op, preferred_element_type=f32).astype(out)  108 us
    dot_general x5, matrix products, against(): lax.dot_general(left_op, right_op, (((1,), (1,)), ((), ())), preferred_el...  99.3 us
    ppermute x4, waiting for transfers between devices, give_back(): lax.ppermute(lax.dynamic_index_in_dim(blocks, lax.rem(local_seq + batch -...  99.2 us
    dot_general x5, matrix products, outer_sum(): lax.dot_general(left_op, right_op, (((0,), (0,)), ((), ())), preferred_el...  94.3 us
    pallas_call x1, Pallas kernels, attend_backward(): pl.pallas_call(attend_backward_kernel, grid_spec=pltpu.PrefetchScalarGrid...  43.6 us
    unnamed x111, local copies, waits for them, and re-layouts  36.5 us
  transfers between devices with their start and end apart: 115, of which 42 were waited for; matrix products, arithmetic and copies ran while one was open for 32% of the time, Pallas kernels for 6%

profile of v2, /device:TPU:9, one launch (start us, length us, event | category | flops | bytes accessed | tf_op | source)
XLA Modules:
  0.0 1483.7 jit_solution(15749596829455051683)
XLA Ops:
  108.9 31.3 %collective-permute-done.10 = bf16[256,3072]{0,1:T(8,128)(2,1)} collective-permute-done((bf16[256,3072]{0,1:T(8,128)(2,1)}, bf16[256,3072]{0,1:T(8,128)(2,1)}, u32[]{:S(2)}, u32[]{:S(2)}) %collective-permute-start.10) | collective-permute-done | bytes 1572896 | tf_op jit(solution)/shard_map/ppermute | solution.py:426
  146.6 27.3 %collective-permute-done.9 = bf16[256,3072]{0,1:T(8,128)(2,1)} collective-permute-done((bf16[256,3072]{0,1:T(8,128)(2,1)}, bf16[256,3072]{0,1:T(8,128)(2,1)}, u32[]{:S(2)}, u32[]{:S(2)}) %collective-permute-start.9) | collective-permute-done | bytes 1572896 | tf_op jit(solution)/shard_map/ppermute | solution.py:426
  194.0 17.8 %fusion.16.lin_ref = f32[1024,3072]{1,0:T(8,128)} fusion(bf16[2048,3072]{0,1:T(8,128)(2,1)} %constant_dynamic-update-slice_fusion.25, bf16[512,2048]{1,0:T(8,128)(2,1)S(1)} %get-tuple-element.98, bf16[512,2048]{1,0:T(8,128)(2,1)S(1)} %get-tuple-element.97), kind=kOutput, calls=%fused_computation.68 | convolution fusion | flops 12893290496 | bytes 29360128 | tf_op jit(solution)/shard_map/dot_general | solution.py:27
  213.9 35.6 %attend_forward.1 = (bf16[1024,1024]{1,0:T(8,128)(2,1)}, bf16[1024,3072]{1,0:T(8,128)(2,1)}, f32[8,4,512]{2,1,0:T(4,128)}) custom-call(s32[1]{0:T(128)} %collective-permute-done.2.start_ref, f32[1024,3072]{1,0:T(8,128)} %fusion.16.lin_ref, f32[1024,128]{1,0:T(8,128)} %get-tuple-element.145.cos_ref, f32[1024,128]{1,0:T(8,128)} %get-tuple-element.146.sin_ref), custom_call_target="tpu_custom_call" | custom-call | flops 8589934592 | bytes 20971520 | tf_op jit(solution)/shard_map/attend_forward/pallas_call | solution.py:232
  275.1 27.1 %collective-permute-done.18 = bf16[128,2048]{1,0:T(8,128)(2,1)S(1)} collective-permute-done((bf16[128,2048]{1,0:T(8,128)(2,1)}, bf16[128,2048]{1,0:T(8,128)(2,1)S(1)}, u32[]{:S(2)}, u32[]{:S(2)}) %collective-permute-start.18) | collective-permute-done | bytes 524320 | tf_op jit(solution)/shard_map/ppermute | solution.py:426
  329.3 20.4 %collective-permute-done.26 = bf16[512,1024]{1,0:T(8,128)(2,1)S(1)} collective-permute-done((bf16[512,1024]{1,0:T(8,128)(2,1)S(1)}, bf16[512,1024]{1,0:T(8,128)(2,1)S(1)}, u32[]{:S(2)}, u32[]{:S(2)}) %collective-permute-start.26) | collective-permute-done | bytes 1048608 | tf_op jit(solution)/shard_map/ppermute | solution.py:426
  352.6 20.4 %collective-permute-done.28 = bf16[512,1024]{1,0:T(8,128)(2,1)S(1)} collective-permute-done((bf16[512,1024]{1,0:T(8,128)(2,1)S(1)}, bf16[512,1024]{1,0:T(8,128)(2,1)S(1)}, u32[]{:S(2)}, u32[]{:S(2)}) %collective-permute-start.28) | collective-permute-done | bytes 1048608 | tf_op jit(solution)/shard_map/ppermute | solution.py:426
  373.3 21.6 %collective-permute-done.44 = bf16[256,2048]{1,0:T(8,128)(2,1)} collective-permute-done((bf16[256,2048]{1,0:T(8,128)(2,1)S(1)}, bf16[256,2048]{1,0:T(8,128)(2,1)}, u32[]{:S(2)}, u32[]{:S(2)}) %collective-permute-start.44) | collective-permute-done | bytes 1048608 | tf_op jit(solution)/shard_map/ppermute | solution.py:426
  444.6 17.5 %collective-permute-done.20 = bf16[256,2048]{1,0:T(8,128)(2,1)S(1)} collective-permute-done((bf16[256,2048]{1,0:T(8,128)(2,1)S(1)}, bf16[256,2048]{1,0:T(8,128)(2,1)S(1)}, u32[]{:S(2)}, u32[]{:S(2)}) %collective-permute-start.20) | collective-permute-done | bytes 1048608 | tf_op jit(solution)/shard_map/ppermute | solution.py:426
  463.4 24.3 %fusion.46 = f32[2048,2048]{1,0:T(8,128)} fusion(bf16[2048,2048]{1,0:T(8,128)(2,1)} %constant_dynamic-update-slice_fusion.7, bf16[2048,2048]{1,0:T(8,128)(2,1)} %param.23), kind=kOutput, calls=%fused_computation.256 | convolution fusion | flops 17179869184 | bytes 33554432 | tf_op jit(solution)/shard_map/dot_general | solution.py:37
  514.0 23.5 %fusion.2 = f32[2048,2048]{1,0:T(8,128)} fusion(bf16[2048,2048]{1,0:T(8,128)(2,1)} %constant_dynamic-update-slice_fusion, bf16[2048,1024]{1,0:T(8,128)(2,1)S(1)} %get-tuple-element.84, bf16[2048,1024]{1,0:T(8,128)(2,1)S(1)} %get-tuple-element.83), kind=kOutput, calls=%fused_computation.22 | convolution fusion | flops 17196646400 | bytes 33554432 | tf_op jit(solution)/shard_map/dot_general | solution.py:27
  541.5 35.5 %multiply_convert_fusion.1 = (bf16[2048,2048]{1,0:T(8,128)(2,1)}, bf16[2048,2048]{1,0:T(8,128)(2,1)}, bf16[2048,2048]{1,0:T(8,128)(2,1)}) fusion(f32[2048,2048]{1,0:T(8,128)} %fusion.46, f32[2048,2048]{1,0:T(8,128)} %fusion.2, bf16[2048,2048]{1,0:T(8,128)(2,1)} %constant_dynamic-update-slice_fusion, bf16[2048,1024]{1,0:T(8,128)(2,1)} %get-tuple-element.79, ...), kind=kOutput, calls=%fused_computation.2 | convolution fusion | flops 17259560960 | bytes 75497472 | tf_op jit(solution)/shard_map/dot_general | solution.py:27
  577.0 23.9 %convolution_convert_fusion.1 = bf16[2048,2048]{1,0:T(8,128)(2,1)} fusion(bf16[2048,2048]{1,0:T(8,128)(2,1)} %get-tuple-element.59, bf16[2048,2048]{1,0:T(8,128)(2,1)} %constant_dynamic-update-slice_fusion.7), kind=kOutput, calls=%fused_computation.17 | convolution fusion | flops 17184063488 | bytes 25165824 | tf_op jit(solution)/shard_map/dot_general | solution.py:31
  601.0 23.7 %convolution_convert_fusion.3 = bf16[2048,2048]{1,0:T(8,128)(2,1)} fusion(bf16[2048,2048]{1,0:T(8,128)(2,1)} %constant_dynamic-update-slice_fusion, bf16[2048,2048]{1,0:T(8,128)(2,1)} %get-tuple-element.57), kind=kOutput, calls=%fused_computation.19 | convolution fusion | flops 17184063488 | bytes 25165824 | tf_op jit(solution)/shard_map/dot_general | solution.py:31
  633.1 24.0 %convolution_convert_fusion.2 = bf16[2048,2048]{1,0:T(8,128)(2,1)} fusion(bf16[2048,2048]{1,0:T(8,128)(2,1)} %constant_dynamic-update-slice_fusion, bf16[2048,2048]{1,0:T(8,128)(2,1)} %get-tuple-element.58), kind=kOutput, calls=%fused_computation.18 | convolution fusion | flops 17184063488 | bytes 25165824 | tf_op jit(solution)/shard_map/dot_general | solution.py:31
  665.7 24.5 %fusion.1 = f32[2048,2048]{1,0:T(8,128)} fusion(bf16[2048,2048]{1,0:T(8,128)(2,1)} %get-tuple-element.58, bf16[2048,1024]{1,0:T(8,128)(2,1)} %copy-done.23, bf16[2048,1024]{1,0:T(8,128)(2,1)} %copy-done.22), kind=kOutput, calls=%fused_computation.21 | convolution fusion | flops 17196646400 | bytes 33554432 | tf_op jit(solution)/shard_map/dot_general | solution.py:37
  690.2 25.5 %add_convert_fusion = bf16[2048,2048]{1,0:T(8,128)(2,1)} fusion(f32[2048,2048]{1,0:T(8,128)} %fusion.1, bf16[2048,2048]{1,0:T(8,128)(2,1)} %get-tuple-element.57, bf16[2048,1024]{1,0:T(8,128)(2,1)} %get-tuple-element.79, bf16[2048,1024]{1,0:T(8,128)(2,1)} %get-tuple-element.78), kind=kOutput, calls=%fused_computation | convolution fusion | flops 17205035008 | bytes 41943040 | tf_op jit(solution)/shard_map/dot_general | solution.py:37
  720.8 24.0 %convolution_convert_fusion.4 = bf16[2048,2048]{1,0:T(8,128)(2,1)} fusion(bf16[2048,2048]{1,0:T(8,128)(2,1)} %get-tuple-element.59, bf16[2048,2048]{1,0:T(8,128)(2,1)} %param.23), kind=kOutput, calls=%fused_computation.20 | convolution fusion | flops 17184063488 | bytes 25165824 | tf_op jit(solution)/shard_map/dot_general | solution.py:27
  752.8 19.7 %collective-permute-done.35 = bf16[256,2048]{1,0:T(8,128)(2,1)S(1)} collective-permute-done((bf16[256,2048]{1,0:T(8,128)(2,1)S(1)}, bf16[256,2048]{1,0:T(8,128)(2,1)S(1)}, u32[]{:S(2)}, u32[]{:S(2)}) %collective-permute-start.35) | collective-permute-done | bytes 1048608 | tf_op jit(solution)/shard_map/ppermute | solution.py:426
  773.0 21.9 %collective-permute-done.50 = bf16[256,2048]{1,0:T(8,128)(2,1)S(1)} collective-permute-done((bf16[256,2048]{1,0:T(8,128)(2,1)}, bf16[256,2048]{1,0:T(8,128)(2,1)S(1)}, u32[]{:S(2)}, u32[]{:S(2)}) %collective-permute-start.50) | collective-permute-done | bytes 1048608 | tf_op jit(solution)/shard_map/ppermute | solution.py:426
  799.1 18.3 %collective-permute-done.34 = bf16[256,2048]{1,0:T(8,128)(2,1)S(1)} collective-permute-done((bf16[256,2048]{1,0:T(8,128)(2,1)S(1)}, bf16[256,2048]{1,0:T(8,128)(2,1)S(1)}, u32[]{:S(2)}, u32[]{:S(2)}) %collective-permute-start.34) | collective-permute-done | bytes 1048608 | tf_op jit(solution)/shard_map/ppermute | solution.py:426
  818.5 22.5 %collective-permute-done.36 = bf16[256,2048]{1,0:T(8,128)(2,1)S(1)} collective-permute-done((bf16[256,2048]{1,0:T(8,128)(2,1)S(1)}, bf16[256,2048]{1,0:T(8,128)(2,1)S(1)}, u32[]{:S(2)}, u32[]{:S(2)}) %collective-permute-start.36) | collective-permute-done | bytes 1048608 | tf_op jit(solution)/shard_map/ppermute | solution.py:426
  842.1 21.3 %collective-permute-done.53 = bf16[256,2048]{1,0:T(8,128)(2,1)S(1)} collective-permute-done((bf16[256,2048]{1,0:T(8,128)(2,1)S(1)}, bf16[256,2048]{1,0:T(8,128)(2,1)S(1)}, u32[]{:S(2)}, u32[]{:S(2)}) %collective-permute-start.53) | collective-permute-done | bytes 1048608 | tf_op jit(solution)/shard_map/ppermute | solution.py:426
  866.3 19.6 %collective-permute-done.37 = bf16[256,2048]{1,0:T(8,128)(2,1)S(1)} collective-permute-done((bf16[256,2048]{1,0:T(8,128)(2,1)S(1)}, bf16[256,2048]{1,0:T(8,128)(2,1)S(1)}, u32[]{:S(2)}, u32[]{:S(2)}) %collective-permute-start.37) | collective-permute-done | bytes 1048608 | tf_op jit(solution)/shard_map/ppermute | solution.py:426
  916.7 43.6 %attend_backward.1 = bf16[1024,3072]{1,0:T(8,128)(2,1)} custom-call(s32[1]{0:T(128)} %collective-permute-done.2.start_ref, bf16[1024,3072]{1,0:T(8,128)(2,1)} %get-tuple-element.30.qkv_ref, bf16[1024,1024]{1,0:T(8,128)(2,1)} %get-tuple-element.25.out_ref, bf16[1024,1024]{1,0:T(8,128)(2,1)} %fusion.17.grad_ref, f32[8,4,512]{2,1,0:T(4,128)} %get-tuple-element.32.lse_ref, ...), custom_call_target="tpu_custom_call" | custom-call | flops 21474836480 | bytes 16777216 | tf_op jit(solution)/shard_map/attend_backward/pallas_call | solution.py:273
  974.3 16.7 %convolution_convert_fusion = bf16[2048,3072]{1,0:T(8,128)(2,1)S(1)} fusion(bf16[1024,3072]{1,0:T(8,128)(2,1)} %attend_backward.1, bf16[512,2048]{1,0:T(8,128)(2,1)} %copy-done.25, bf16[512,2048]{1,0:T(8,128)(2,1)} %copy-done.24), kind=kOutput, calls=%fused_computation.6 | convolution fusion | flops 12899581952 | bytes 23068672 | tf_op jit(solution)/shard_map/dot_general | solution.py:31
  1009.8 23.6 %collective-permute-done.69 = bf16[256,3072]{1,0:T(8,128)(2,1)S(1)} collective-permute-done((bf16[256,3072]{1,0:T(8,128)(2,1)}, bf16[256,3072]{1,0:T(8,128)(2,1)S(1)}, u32[]{:S(2)}, u32[]{:S(2)}) %collective-permute-start.69) | collective-permute-done | bytes 1572896 | tf_op jit(solution)/shard_map/ppermute | solution.py:426
  1036.8 45.8 %collective-permute-done.40 = bf16[256,2048]{1,0:T(8,128)(2,1)} collective-permute-done((bf16[256,2048]{1,0:T(8,128)(2,1)}, bf16[256,2048]{1,0:T(8,128)(2,1)}, u32[]{:S(2)}, u32[]{:S(2)}) %collective-permute-start.40) | collective-permute-done | bytes 1048608 | tf_op jit(solution)/shard_map/ppermute | solution.py:530
  1207.1 21.3 %collective-permute-done.73 = bf16[128,3072]{1,0:T(8,128)(2,1)S(1)} collective-permute-done((bf16[128,3072]{1,0:T(8,128)(2,1)S(1)}, bf16[128,3072]{1,0:T(8,128)(2,1)S(1)}, u32[]{:S(2)}, u32[]{:S(2)}) %collective-permute-start.73) | collective-permute-done | bytes 786464 | tf_op jit(solution)/shard_map/ppermute | solution.py:396
  1228.4 23.0 %collective-permute-done.76 = bf16[128,3072]{1,0:T(8,128)(2,1)S(1)} collective-permute-done((bf16[128,3072]{1,0:T(8,128)(2,1)S(1)}, bf16[128,3072]{1,0:T(8,128)(2,1)S(1)}, u32[]{:S(2)}, u32[]{:S(2)}) %collective-permute-start.76) | collective-permute-done | bytes 786464 | tf_op jit(solution)/shard_map/ppermute | solution.py:397
  1265.1 31.1 %collective-permute-start.60 = (f32[2,2048]{1,0:T(2,128)S(1)}, f32[2,2048]{1,0:T(2,128)S(1)}, u32[]{:S(2)}, u32[]{:S(2)}) collective-permute-start(f32[2,2048]{1,0:T(2,128)S(1)} %pad_maximum_fusion.21), channel_id=1, source_target_pairs={{0,1},{1,0},{2,3},{3,2},{4,5},{5,4},{6,7},{7,6},{8,9},{9,8},{10,11... | collective-permute-start | bytes 49160 | tf_op jit(solution)/shard_map/ppermute | solution.py:426
  1389.5 26.2 %collective-permute-done.58 = bf16[256,2048]{1,0:T(8,128)(2,1)S(1)} collective-permute-done((bf16[256,2048]{1,0:T(8,128)(2,1)S(1)}, bf16[256,2048]{1,0:T(8,128)(2,1)S(1)}, u32[]{:S(2)}, u32[]{:S(2)}) %collective-permute-start.58) | collective-permute-done | bytes 1048608 | tf_op jit(solution)/shard_map/ppermute | solution.py:530
  (475 shorter events, 665.5 us)
Async XLA Ops:
  7.2 737.6 %reduce-scatter.8.cloned.1.call-start = ((), (), s32[]{:S(2)}) async-start(), calls=%async_computation.7 | async-start | bytes 9437184 | tf_op jit(solution)/shard_map/reduce_scatter | solution.py:646
  70.7 73.3 %collective-permute-start.6 = (bf16[512,2048]{1,0:T(8,128)(2,1)}, bf16[512,2048]{1,0:T(8,128)(2,1)}, u32[]{:S(2)}, u32[]{:S(2)}) collective-permute-start(bf16[512,2048]{1,0:T(8,128)(2,1)} %fusion.6), channel_id=1, source_target_pairs={{0,1},{1,0},{8,9},{9,8},{16,17},{17,16},{24,25},{25,24},{2,3},{3,2... | collective-permute-start | bytes 6291464 | tf_op jit(solution)/shard_map/ppermute | solution.py:426
  73.2 66.9 %collective-permute-start.10 = (bf16[256,3072]{0,1:T(8,128)(2,1)}, bf16[256,3072]{0,1:T(8,128)(2,1)}, u32[]{:S(2)}, u32[]{:S(2)}) collective-permute-start(bf16[256,3072]{0,1:T(8,128)(2,1)} %bitcast.14), channel_id=1, source_target_pairs={{0,4},{2,6},{4,0},{6,2},{1,5},{3,7},{5,1},{7,3},{8,12},{10,14},{12... | collective-permute-start | bytes 4718600 | tf_op jit(solution)/shard_map/ppermute | solution.py:426
  73.5 108.4 %collective-permute-start.11 = (bf16[256,3072]{0,1:T(8,128)(2,1)}, bf16[256,3072]{0,1:T(8,128)(2,1)}, u32[]{:S(2)}, u32[]{:S(2)}) collective-permute-start(bf16[256,3072]{0,1:T(8,128)(2,1)} %bitcast.14), channel_id=1, source_target_pairs={{0,2},{2,0},{4,6},{6,4},{1,3},{3,1},{5,7},{7,5},{8,10},{10,8},{12,... | collective-permute-start | bytes 4718600 | tf_op jit(solution)/shard_map/ppermute | solution.py:426
  86.9 87.0 %collective-permute-start.9 = (bf16[256,3072]{0,1:T(8,128)(2,1)}, bf16[256,3072]{0,1:T(8,128)(2,1)}, u32[]{:S(2)}, u32[]{:S(2)}) collective-permute-start(bf16[256,3072]{0,1:T(8,128)(2,1)} %collective-permute-done.7), channel_id=1, source_target_pairs={{0,4},{2,6},{4,0},{6,2},{1,5},{3,7},{5,1},{7,3},{8,12},{10,14},{12... | collective-permute-start | bytes 4718600 | tf_op jit(solution)/shard_map/ppermute | solution.py:426
  106.5 105.3 %collective-permute-start.2 = (s32[1]{0:T(128)}, s32[1]{0:T(128)}, u32[]{:S(2)}, u32[]{:S(2)}) collective-permute-start(s32[1]{0:T(128)} %dynamic_slice.174), channel_id=1, source_target_pairs={{0,0},{1,16},{8,8},{9,24},{16,1},{17,17},{24,9},{25,25},{2,2},{3,1... | collective-permute-start | bytes 20 | tf_op jit(solution)/shard_map/ppermute | solution.py:566
  189.6 66.1 %collective-permute-start.13 = (bf16[128,2048]{1,0:T(8,128)(2,1)}, bf16[128,2048]{1,0:T(8,128)(2,1)}, u32[]{:S(2)}, u32[]{:S(2)}) collective-permute-start(bf16[128,2048]{1,0:T(8,128)(2,1)} %get-tuple-element.131), channel_id=1, source_target_pairs={{0,2},{2,0},{4,6},{6,4},{1,3},{3,1},{5,7},{7,5},{8,10},{10,8},{12,... | collective-permute-start | bytes 1572872 | tf_op jit(solution)/shard_map/ppermute | solution.py:426
  190.8 70.2 %collective-permute-start.14 = (bf16[128,2048]{1,0:T(8,128)(2,1)}, bf16[128,2048]{1,0:T(8,128)(2,1)}, u32[]{:S(2)}, u32[]{:S(2)}) collective-permute-start(bf16[128,2048]{1,0:T(8,128)(2,1)} %get-tuple-element.131), channel_id=1, source_target_pairs={{0,4},{2,6},{4,0},{6,2},{1,5},{3,7},{5,1},{7,3},{8,12},{10,14},{12... | collective-permute-start | bytes 1572872 | tf_op jit(solution)/shard_map/ppermute | solution.py:426
  192.0 76.1 %collective-permute-start.16 = (bf16[128,2048]{1,0:T(8,128)(2,1)}, bf16[128,2048]{1,0:T(8,128)(2,1)}, u32[]{:S(2)}, u32[]{:S(2)}) collective-permute-start(bf16[128,2048]{1,0:T(8,128)(2,1)} %get-tuple-element.129), channel_id=1, source_target_pairs={{0,4},{2,6},{4,0},{6,2},{1,5},{3,7},{5,1},{7,3},{8,12},{10,14},{12... | collective-permute-start | bytes 1572872 | tf_op jit(solution)/shard_map/ppermute | solution.py:426
  192.2 80.8 %collective-permute-start.17 = (bf16[128,2048]{1,0:T(8,128)(2,1)}, bf16[128,2048]{1,0:T(8,128)(2,1)}, u32[]{:S(2)}, u32[]{:S(2)}) collective-permute-start(bf16[128,2048]{1,0:T(8,128)(2,1)} %get-tuple-element.129), channel_id=1, source_target_pairs={{0,2},{2,0},{4,6},{6,4},{1,3},{3,1},{5,7},{7,5},{8,10},{10,8},{12,... | collective-permute-start | bytes 1572872 | tf_op jit(solution)/shard_map/ppermute | solution.py:426
  211.8 99.7 %collective-permute-start.42 = (bf16[256,2048]{1,0:T(8,128)(2,1)}, bf16[256,2048]{1,0:T(8,128)(2,1)S(1)}, u32[]{:S(2)}, u32[]{:S(2)}) collective-permute-start(bf16[256,2048]{1,0:T(8,128)(2,1)} %get-tuple-element.108), channel_id=1, source_target_pairs={{0,0},{1,16},{8,8},{9,24},{16,1},{17,17},{24,9},{25,25},{2,2},{3,1... | collective-permute-start | bytes 3145736 | tf_op jit(solution)/shard_map/ppermute | solution.py:515
  311.8 85.7 %collective-permute-start.19 = (bf16[512,2048]{1,0:T(8,128)(2,1)S(1)}, bf16[512,2048]{1,0:T(8,128)(2,1)S(1)}, u32[]{:S(2)}, u32[]{:S(2)}) collective-permute-start(bf16[512,2048]{1,0:T(8,128)(2,1)S(1)} %constant_dynamic-slice_fusion.17), channel_id=1, source_target_pairs={{0,1},{1,0},{8,9},{9,8},{16,17},{17,16},{24,25},{25,24},{2,3},{3,2... | collective-permute-start | bytes 6291464 | tf_op jit(solution)/shard_map/ppermute | solution.py:426
  328.0 66.9 %collective-permute-start.44 = (bf16[256,2048]{1,0:T(8,128)(2,1)S(1)}, bf16[256,2048]{1,0:T(8,128)(2,1)}, u32[]{:S(2)}, u32[]{:S(2)}) collective-permute-start(bf16[256,2048]{1,0:T(8,128)(2,1)S(1)} %get-tuple-element.50), channel_id=1, source_target_pairs={{0,2},{2,0},{4,6},{6,4},{1,3},{3,1},{5,7},{7,5},{8,10},{10,8},{12,... | collective-permute-start | bytes 3145736 | tf_op jit(solution)/shard_map/ppermute | solution.py:426
  351.2 66.1 %collective-permute-start.45 = (bf16[256,2048]{1,0:T(8,128)(2,1)S(1)}, bf16[256,2048]{1,0:T(8,128)(2,1)}, u32[]{:S(2)}, u32[]{:S(2)}) collective-permute-start(bf16[256,2048]{1,0:T(8,128)(2,1)S(1)} %get-tuple-element.48), channel_id=1, source_target_pairs={{0,2},{2,0},{4,6},{6,4},{1,3},{3,1},{5,7},{7,5},{8,10},{10,8},{12,... | collective-permute-start | bytes 3145736 | tf_op jit(solution)/shard_map/ppermute | solution.py:426
  394.8 118.3 %collective-permute-start.33 = (bf16[2048,1024]{1,0:T(8,128)(2,1)S(1)}, bf16[2048,1024]{1,0:T(8,128)(2,1)S(1)}, u32[]{:S(2)}, u32[]{:S(2)}) collective-permute-start(bf16[2048,1024]{1,0:T(8,128)(2,1)S(1)} %bitcast.136), channel_id=1, source_target_pairs={{0,1},{1,0},{2,3},{3,2},{4,5},{5,4},{6,7},{7,6},{8,9},{9,8},{10,11... | collective-permute-start | bytes 12582920 | tf_op jit(solution)/shard_map/ppermute | solution.py:426
  424.3 66.9 %collective-permute-start.22 = (bf16[256,2048]{1,0:T(8,128)(2,1)S(1)}, bf16[256,2048]{1,0:T(8,128)(2,1)S(1)}, u32[]{:S(2)}, u32[]{:S(2)}) collective-permute-start(bf16[256,2048]{1,0:T(8,128)(2,1)S(1)} %get-tuple-element.114), channel_id=1, source_target_pairs={{0,4},{2,6},{4,0},{6,2},{1,5},{3,7},{5,1},{7,3},{8,12},{10,14},{12... | collective-permute-start | bytes 3145736 | tf_op jit(solution)/shard_map/ppermute | solution.py:426
  600.9 314.1 %reduce-scatter.4.cloned.1.call-start = ((), (), s32[]{:S(2)}) async-start(), calls=%async_computation.3 | async-start | bytes 9437184 | tf_op jit(solution)/shard_map/reduce_scatter | solution.py:646
  633.1 509.9 %reduce-scatter.6.cloned.1.call-start = ((), (), s32[]{:S(2)}) async-start(), calls=%async_computation.5 | async-start | bytes 9437184 | tf_op jit(solution)/shard_map/reduce_scatter | solution.py:646
  665.6 775.7 %all-gather.9.cloned.1.call-start = ((), (), s32[]{:S(2)}) async-start(), calls=%async_computation.8 | async-start | bytes 9437184 | tf_op jit(solution)/shard_map/all_gather | solution.py:649
  744.9 708.1 %all-gather.5.cloned.1.call-start = ((), (), s32[]{:S(2)}) async-start(), calls=%async_computation.4 | async-start | bytes 9437184 | tf_op jit(solution)/shard_map/all_gather | solution.py:649
  752.5 64.9 %collective-permute-start.34 = (bf16[256,2048]{1,0:T(8,128)(2,1)S(1)}, bf16[256,2048]{1,0:T(8,128)(2,1)S(1)}, u32[]{:S(2)}, u32[]{:S(2)}) collective-permute-start(bf16[256,2048]{1,0:T(8,128)(2,1)S(1)} %get-tuple-element.74), channel_id=1, source_target_pairs={{0,2},{2,0},{4,6},{6,4},{1,3},{3,1},{5,7},{7,5},{8,10},{10,8},{12,... | collective-permute-start | bytes 3145736 | tf_op jit(solution)/shard_map/ppermute | solution.py:426
  795.1 68.3 %collective-permute-start.53 = (bf16[256,2048]{1,0:T(8,128)(2,1)S(1)}, bf16[256,2048]{1,0:T(8,128)(2,1)S(1)}, u32[]{:S(2)}, u32[]{:S(2)}) collective-permute-start(bf16[256,2048]{1,0:T(8,128)(2,1)S(1)} %get-tuple-element.70), channel_id=1, source_target_pairs={{0,4},{2,6},{4,0},{6,2},{1,5},{3,7},{5,1},{7,3},{8,12},{10,14},{12... | collective-permute-start | bytes 3145736 | tf_op jit(solution)/shard_map/ppermute | solution.py:426
  798.8 64.6 %collective-permute-start.55 = (bf16[256,2048]{1,0:T(8,128)(2,1)S(1)}, bf16[256,2048]{1,0:T(8,128)(2,1)S(1)}, u32[]{:S(2)}, u32[]{:S(2)}) collective-permute-start(bf16[256,2048]{1,0:T(8,128)(2,1)S(1)} %get-tuple-element.67), channel_id=1, source_target_pairs={{0,2},{2,0},{4,6},{6,4},{1,3},{3,1},{5,7},{7,5},{8,10},{10,8},{12,... | collective-permute-start | bytes 3145736 | tf_op jit(solution)/shard_map/ppermute | solution.py:426
  817.4 68.5 %collective-permute-start.37 = (bf16[256,2048]{1,0:T(8,128)(2,1)S(1)}, bf16[256,2048]{1,0:T(8,128)(2,1)S(1)}, u32[]{:S(2)}, u32[]{:S(2)}) collective-permute-start(bf16[256,2048]{1,0:T(8,128)(2,1)S(1)} %get-tuple-element.76), channel_id=1, source_target_pairs={{0,4},{2,6},{4,0},{6,2},{1,5},{3,7},{5,1},{7,3},{8,12},{10,14},{12... | collective-permute-start | bytes 3145736 | tf_op jit(solution)/shard_map/ppermute | solution.py:426
  974.2 490.5 %all-gather.7.cloned.1.call-start = ((), (), s32[]{:S(2)}) async-start(), calls=%async_computation.6 | async-start | bytes 9437184 | tf_op jit(solution)/shard_map/all_gather | solution.py:649
  1002.3 80.3 %collective-permute-start.40 = (bf16[256,2048]{1,0:T(8,128)(2,1)}, bf16[256,2048]{1,0:T(8,128)(2,1)}, u32[]{:S(2)}, u32[]{:S(2)}) collective-permute-start(bf16[256,2048]{1,0:T(8,128)(2,1)} %get-tuple-element.112), channel_id=1, source_target_pairs={{0,0},{16,1},{8,8},{24,9},{1,16},{17,17},{9,24},{25,25},{2,2},{18,... | collective-permute-start | bytes 3145736 | tf_op jit(solution)/shard_map/ppermute | solution.py:530
  1004.6 93.9 %collective-permute-start.41 = (bf16[256,2048]{1,0:T(8,128)(2,1)}, bf16[256,2048]{1,0:T(8,128)(2,1)}, u32[]{:S(2)}, u32[]{:S(2)}) collective-permute-start(bf16[256,2048]{1,0:T(8,128)(2,1)} %get-tuple-element.111), channel_id=1, source_target_pairs={{8,0},{24,1},{0,8},{16,9},{9,16},{25,17},{1,24},{17,25},{10,2},{26... | collective-permute-start | bytes 3145736 | tf_op jit(solution)/shard_map/ppermute | solution.py:530
  1007.7 98.0 %collective-permute-start.68 = (bf16[256,3072]{1,0:T(8,128)(2,1)}, bf16[256,3072]{1,0:T(8,128)(2,1)}, u32[]{:S(2)}, u32[]{:S(2)}) collective-permute-start(bf16[256,3072]{1,0:T(8,128)(2,1)} %get-tuple-element.62), channel_id=1, source_target_pairs={{0,4},{2,6},{4,0},{6,2},{1,5},{3,7},{5,1},{7,3},{8,12},{10,14},{12... | collective-permute-start | bytes 4718600 | tf_op jit(solution)/shard_map/ppermute | solution.py:426
  1008.0 97.7 %collective-permute-start.66 = (bf16[256,3072]{1,0:T(8,128)(2,1)}, bf16[256,3072]{1,0:T(8,128)(2,1)}, u32[]{:S(2)}, u32[]{:S(2)}) collective-permute-start(bf16[256,3072]{1,0:T(8,128)(2,1)} %get-tuple-element.63), channel_id=1, source_target_pairs={{0,2},{2,0},{4,6},{6,4},{1,3},{3,1},{5,7},{7,5},{8,10},{10,8},{12,... | collective-permute-start | bytes 4718600 | tf_op jit(solution)/shard_map/ppermute | solution.py:426
  1035.4 70.3 %collective-permute-start.70 = (bf16[256,3072]{1,0:T(8,128)(2,1)S(1)}, bf16[256,3072]{1,0:T(8,128)(2,1)}, u32[]{:S(2)}, u32[]{:S(2)}) collective-permute-start(bf16[256,3072]{1,0:T(8,128)(2,1)S(1)} %add_convert_fusion.2), channel_id=1, source_target_pairs={{0,2},{2,0},{4,6},{6,4},{1,3},{3,1},{5,7},{7,5},{8,10},{10,8},{12,... | collective-permute-start | bytes 4718600 | tf_op jit(solution)/shard_map/ppermute | solution.py:426
  1171.2 91.4 %collective-permute-start.57 = (bf16[512,2048]{1,0:T(8,128)(2,1)S(1)}, bf16[512,2048]{1,0:T(8,128)(2,1)S(1)}, u32[]{:S(2)}, u32[]{:S(2)}) collective-permute-start(bf16[512,2048]{1,0:T(8,128)(2,1)S(1)} %constant_dynamic-slice_fusion.10), channel_id=1, source_target_pairs={{0,1},{1,0},{8,9},{9,8},{16,17},{17,16},{24,25},{25,24},{2,3},{3,2... | collective-permute-start | bytes 6291464 | tf_op jit(solution)/shard_map/ppermute | solution.py:426
  1354.8 78.5 %collective-permute-start.83 = (bf16[512,3072]{1,0:T(8,128)(2,1)}, bf16[512,3072]{1,0:T(8,128)(2,1)}, u32[]{:S(2)}, u32[]{:S(2)}) collective-permute-start(bf16[512,3072]{1,0:T(8,128)(2,1)} %select_dynamic-update-slice_fusion.mine_ref), channel_id=1, source_target_pairs={{0,1},{1,0},{8,9},{9,8},{16,17},{17,16},{24,25},{25,24},{2,3},{3,2... | collective-permute-start | bytes 9437192 | tf_op jit(solution)/shard_map/ppermute | solution.py:426
  (132 other events, 4408.0 us)
Sparse Core Ops, SparseCore 0:
  601.1 87.6 reduce-scatter.7
  691.0 88.1 reduce-scatter.3
  781.5 87.9 reduce-scatter.5
  871.0 79.2 all-gather.8
  974.3 112.8 all-gather.4
  1166.8 123.0 all-gather.6

commit v3 on v2

--- a/solution.py
+++ b/solution.py
@@ -337,6 +337,32 @@
     )(place, mine, other)
 
 
+def pick_heads_kernel(place_ref, q_ref, k_ref, v_ref, out_ref):
+    for p in range(q_ref.shape[1] // LANES):
+        for i, part_ref in enumerate((q_ref, k_ref, v_ref)):
+            at = (3 * p + i) * LANES
+            out_ref[:, at : at + LANES] = part_ref[:, p * LANES : (p + 1) * LANES]
+
+
+def pick_heads(place, weights, heads_width, team):
+    rows, full = weights[0].shape
+    groups = full // (heads_width * team)
+    return pl.pallas_call(
+        pick_heads_kernel,
+        grid_spec=pltpu.PrefetchScalarGridSpec(
+            num_scalar_prefetch=1,
+            grid=(groups,),
+            in_specs=[pl.BlockSpec((rows, heads_width), lambda s, p: (0, s * team + p[0]))] * 3,
+            out_specs=pl.BlockSpec((rows, 3 * heads_width), lambda s, p: (0, s)),
+        ),
+        out_shape=jax.ShapeDtypeStruct((rows, 3 * full // team), bf16),
+        cost_estimate=pl.CostEstimate(
+            flops=0, bytes_accessed=12 * rows * full // team, transcendentals=0
+        ),
+        name="pick_heads",
+    )(place, *weights)
+
+
 def spread_heads_kernel(place_ref, mine_ref, other_ref, q_ref, k_ref, v_ref, *, group):
     outs = (q_ref, k_ref, v_ref)
     pairs = mine_ref.shape[1] // (3 * LANES)
@@ -422,6 +448,10 @@
     return out
 
 
+def together(*values):
+    return lax.optimization_barrier(values)
+
+
 def swap(value, axis, size, distance):
     return lax.ppermute(value, axis, [(i, i ^ distance) for i in range(size)])
 
@@ -431,43 +461,46 @@
     return bits, bits[::-1]
 
 
-def gather_rows(value, axis, size):
-    half = value.shape[0] // 2
-    parts = []
-    for part, order in zip((value[:half], value[half:]), bit_orders(size)):
-        held = {0: part}
-        for bit in order:
-            for d in list(held):
-                held[d ^ bit] = swap(held[d], axis, size, bit)
-        parts.append(held)
-    return jnp.concatenate([parts[h][d] for d in range(size) for h in range(2)], axis=0)
+def xor_places(order):
+    places = [0]
+    for bit in order:
+        places += [d ^ bit for d in places]
+    return places
 
 
 def gather_in_order(value, place, axis, size):
     count = value.shape[0]
     half = count // 2
     out = jnp.zeros((size * count,) + value.shape[1:], value.dtype)
-    for h, (part, order) in enumerate(zip((value[:half], value[half:]), bit_orders(size))):
-        held = {0: part}
+    for h, order in enumerate(bit_orders(size)):
+        held = value[h * half : (h + 1) * half]
         for bit in order:
-            for d in list(held):
-                held[d ^ bit] = swap(held[d], axis, size, bit)
-        for d, part in held.items():
-            out = lax.dynamic_update_slice_in_dim(out, part, (place ^ d) * count + h * half, 0)
+            held = jnp.concatenate([held, swap(held, axis, size, bit)], axis=0)
+        for i, d in enumerate(xor_places(order)):
+            out = lax.dynamic_update_slice_in_dim(
+                out, held[i * half : (i + 1) * half], (place ^ d) * count + h * half, 0
+            )
     return out
 
 
-def scatter_rows(block_of, axis, size):
-    blocks = {d: block_of(d) for d in range(size)}
-    half = blocks[0].shape[0] // 2
+def scatter_in_order(value, place, axis, size):
+    count = value.shape[0] // size
+    half = count // 2
     sums = []
     for h, order in enumerate(bit_orders(size)):
-        held = {d: b[h * half : (h + 1) * half] for d, b in blocks.items()}
-        for bit in order:
-            for d in [d for d in held if d & bit]:
-                came = swap(held.pop(d).astype(bf16), axis, size, bit)
-                held[d ^ bit] = held[d ^ bit].astype(f32) + came.astype(f32)
-        sums.append(held[0])
+        blocks = [
+            lax.dynamic_slice_in_dim(value, (place ^ d) * count + h * half, half, 0)
+            for d in xor_places(order)
+        ]
+        kept = len(blocks) // 2
+        sent = jnp.concatenate(blocks[kept:], axis=0)
+        total = jnp.concatenate(blocks[:kept], axis=0).astype(f32)
+        for step, bit in enumerate(order[::-1]):
+            if step:
+                middle = total.shape[0] // 2
+                sent, total = total[middle:].astype(bf16), total[:middle]
+            total = total + swap(sent, axis, size, bit).astype(f32)
+        sums.append(total)
     return jnp.concatenate(sums, axis=0)
 
 
@@ -568,19 +601,60 @@
     )
 
     pairs = width // LANES
-    wqkv_rows = jnp.stack(
-        [
-            head_columns(w).reshape(rows, pairs, LANES)
-            for w in (query_weight, key_weight, value_weight)
-        ],
-        axis=2,
-    ).reshape(rows, 3 * width)
+    if heads_width % LANES == 0:
+        wqkv_rows = pick_heads(
+            mine.astype(jnp.int32).reshape(1),
+            (query_weight, key_weight, value_weight),
+            heads_width,
+            team,
+        )
+    else:
+        wqkv_rows = jnp.stack(
+            [
+                head_columns(w).reshape(rows, pairs, LANES)
+                for w in (query_weight, key_weight, value_weight)
+            ],
+            axis=2,
+        ).reshape(rows, 3 * width)
     wqkv = gather_in_order(wqkv_rows, f, "fsdp", shards)
     wo_rows = lax.dynamic_slice_in_dim(output_weight, mine * heads_width, heads_width, 0)
-    wqkv, wo_rows, gate_weight, up_weight, cotangent = lax.optimization_barrier(
-        (wqkv, wo_rows, gate_weight, up_weight, cotangent)
-    )
-    wo = gather_in_order(wo_rows, f, "fsdp", shards)
+    cotangent_own = take_sequence(cotangent)
+    wqkv, wo_rows, gate_weight, up_weight, cotangent_own = together(
+        wqkv, wo_rows, gate_weight, up_weight, cotangent_own
+    )
+    wo = lax.all_gather(wo_rows, "fsdp", axis=0, tiled=True)
+    wo, cotangent_own = together(wo, cotangent_own)
+    cot = lax.all_gather(cotangent_own, "fsdp", axis=0, tiled=True)
+
+    slab = part // copies
+
+    split = rows // 2
+    z_low = lax.rem(z, 2)
+
+    def column_pieces(weight, d, row):
+        return lax.dynamic_slice(weight, (row, (f ^ d) * part + r * slab), (split, slab))
+
+    fetched = [
+        swap(
+            jnp.stack([column_pieces(w, d, z_low * split) for w in (gate_weight, up_weight)]),
+            "fsdp",
+            shards,
+            d,
+        )
+        for d in range(1, shards)
+    ]
+
+    def join_columns(i, weight, halves):
+        out = jnp.zeros((shards, rows, slab), bf16)
+        own = lax.dynamic_slice_in_dim(weight, f * part + r * slab, slab, 1)
+        out = lax.dynamic_update_index_in_dim(out, own, f, 0)
+        for low in range(2):
+            for d in range(1, shards):
+                piece = lax.select_n(z_low == low, halves[1][d - 1, i], halves[0][d - 1, i])
+                out = lax.dynamic_update_slice(out, piece[None], (f ^ d, low * split, 0))
+        out = out.reshape(features, slab)
+        came = [out] + [swap(out, "rep", copies, d) for d in range(1, copies)]
+        return jnp.concatenate([lax.select_n(r ^ u, *came) for u in range(copies)], axis=1)
 
     gains = shard_gather_small(jnp.stack([attention_gain, feedforward_gain]))
     gain_first = gains[:, 0].reshape(features).astype(f32)
@@ -600,61 +674,53 @@
     first = team_gather(first_own)
     lin = matmul(first, wqkv)
     attended, qkv, lse = attend_forward(start, lin, cosine, sine)
+    attended, *fetched = together(attended, *fetched)
+    fetched = jnp.stack(fetched)
+    exchanged = swap(fetched, "seq", lengths, 1)
     residual = activation + team_scatter(matmul(attended, wo, bf16))
     scale_second = lax.rsqrt(jnp.mean(residual * residual, axis=-1, keepdims=True) + NORM_EPS)
     second_own = (residual * scale_second * gain_second).astype(bf16)
 
-    slab = part // copies
-
-    def hidden_columns(weight):
-        out = jnp.zeros((shards, rows, slab), bf16)
-        for d in range(shards):
-            piece = lax.dynamic_slice_in_dim(weight, (f ^ d) * part + r * slab, slab, 1)
-            came = swap(piece, "fsdp", shards, d) if d else piece
-            out = lax.dynamic_update_index_in_dim(out, came, f ^ d, 0)
-        out = out.reshape(features, slab)
-        came = [out] + [swap(out, "rep", copies, d) for d in range(1, copies)]
-        return jnp.concatenate([lax.select_n(r ^ u, *came) for u in range(copies)], axis=1)
-
-    gate_w = hidden_columns(gate_weight)
-    up_w = hidden_columns(up_weight)
-
-    cotangent_own = take_sequence(cotangent)
-    cot = gather_rows(cotangent_own, "fsdp", shards)
-    second = gather_rows(second_own, "fsdp", shards)
-
+    gate_w = join_columns(0, gate_weight, (fetched, exchanged))
+    up_w = join_columns(1, up_weight, (fetched, exchanged))
+    second = gather_in_order(second_own, f, "fsdp", shards)
+
+    inner_grad = against(cot, down_weight)
+    second, inner_grad = together(second, inner_grad)
     gate = matmul(second, gate_w)
     up = matmul(second, up_w)
-    inner_grad = against(cot, down_weight)
     sig = jax.nn.sigmoid(gate)
     silu = gate * sig
     inner = (silu * up).astype(bf16)
     gate_grad = (inner_grad * up * (sig * (1.0 + gate * (1.0 - sig)))).astype(bf16)
     up_grad = (inner_grad * silu).astype(bf16)
 
-    second_grad_part = (against(gate_grad, gate_w) + against(up_grad, up_w)).astype(bf16)
-    second_grad = scatter_rows(
-        lambda d: second_grad_part[d * own_rows : (d + 1) * own_rows], "fsdp", shards
-    )
-    down_part = matmul(inner, down_weight, bf16)
-    layer_rows = residual + scatter_rows(
-        lambda d: down_part[d * own_rows : (d + 1) * own_rows], "fsdp", shards
-    )
-    layer_output = give_back(layer_rows.astype(bf16))
-
-    def members_scatter(value):
-        return lax.psum_scatter(value, everyone, scatter_dimension=0, tiled=True)
-
-    def members_gather(value):
-        return lax.all_gather(value, everyone, axis=0, tiled=False)
-
-    down_piece = members_scatter(outer_sum(inner, cot, bf16))
-
     tiny = rows // members
 
     def member_major(term):
         blocks = term.reshape(shards, members, tiny, part)
         return blocks.transpose(1, 0, 2, 3).reshape(features, part)
+
+    down_term = outer_sum(inner, cot, bf16)
+    gate_grad, up_grad, down_term = together(gate_grad, up_grad, down_term)
+    second_grad_part = (against(gate_grad, gate_w) + against(up_grad, up_w)).astype(bf16)
+    second_grad_part, gate_grad, up_grad, inner = together(
+        second_grad_part, gate_grad, up_grad, inner
+    )
+    gate_term = member_major(outer_sum(second, gate_grad, bf16))
+    up_term = member_major(outer_sum(second, up_grad, bf16))
+    down_part = matmul(inner, down_weight, bf16)
+    second_grad = scatter_in_order(second_grad_part, f, "fsdp", shards)
+
+    def members_scatter(value):
+        return lax.psum_scatter(value, everyone, scatter_dimension=0, tiled=True)
+
+    def members_gather(value):
+        return lax.all_gather(value, everyone, axis=0, tiled=False)
+
+    gate_piece = members_scatter(gate_term)
+    up_piece = members_scatter(up_term)
+    down_piece = members_scatter(down_term)
 
     def shard_spread(piece):
         piece = piece.reshape(shards, tiny, part)
@@ -665,11 +731,8 @@
             out = lax.dynamic_update_slice_in_dim(out, came, (f ^ d) * part, 1)
         return out
 
-    gate_piece = members_scatter(member_major(outer_sum(second, gate_grad, bf16)))
-    up_piece = members_scatter(member_major(outer_sum(second, up_grad, bf16)))
-    down_grad = members_gather(down_piece).reshape(part, features).astype(f32)
-    gate_grad_w = members_gather(shard_spread(gate_piece)).reshape(rows, hidden).astype(f32)
-    up_grad_w = members_gather(shard_spread(up_piece)).reshape(rows, hidden).astype(f32)
+    gate_spread = shard_spread(gate_piece)
+    up_spread = shard_spread(up_piece)
 
     output_rows = cotangent_own.astype(f32)
     scaled = second_grad * gain_second
@@ -682,14 +745,28 @@
     )
     gain_second_term = jnp.sum(second_grad * residual * scale_second, axis=0)
     branch_own = residual_grad.astype(bf16)
+    branch_own, down_part = together(branch_own, down_part)
+    layer_rows = residual + scatter_in_order(down_part, f, "fsdp", shards)
     branch = team_gather(branch_own)
 
     attended_grad = against(branch, wo, bf16)
     wo_term = outer_sum(attended, branch, bf16)
-    attended_grad, wo_term = lax.optimization_barrier((attended_grad, wo_term))
+    attended_grad, wo_term = together(attended_grad, wo_term)
+    wo_own = scatter_in_order(wo_term, f, "fsdp", shards).astype(bf16)
     lin_grad = attend_backward(start, qkv, attended, attended_grad, lse, cosine, sine)
-    first_grad = team_scatter(against(lin_grad, wqkv, bf16))
+    lin_grad, gate_spread = together(lin_grad, gate_spread)
     wqkv_term = outer_sum(first, lin_grad, bf16)
+    wqkv_term, up_spread, wo_own, layer_rows = together(
+        wqkv_term, up_spread, wo_own, layer_rows
+    )
+    layer_output = give_back(layer_rows.astype(bf16))
+    wqkv_own = scatter_in_order(wqkv_term, f, "fsdp", shards).astype(bf16)
+    wqkv_own, first_grad, layer_output = together(
+        wqkv_own, team_scatter(against(lin_grad, wqkv, bf16)), layer_output
+    )
+    down_grad = members_gather(down_piece).reshape(part, features).astype(f32)
+    gate_grad_w = members_gather(gate_spread).reshape(rows, hidden).astype(f32)
+    up_grad_w = members_gather(up_spread).reshape(rows, hidden).astype(f32)
 
     scaled = first_grad * gain_first
     input_rows = (
@@ -702,50 +779,50 @@
     gain_first_term = jnp.sum(first_grad * activation * scale_first, axis=0)
     input_gradient = give_back(input_rows.astype(bf16))
 
-    def weight_rows(term):
-        size = term.shape[0] // shards
-
-        def block(d):
-            return lax.dynamic_slice_in_dim(term, (f ^ d) * size, size, 0)
-
-        return scatter_rows(block, "fsdp", shards).astype(bf16)
-
     stride = team // copies
-
-    def line_sum(value):
-        size = value.shape[0] * stride // lengths
-        piece = line_scatter(
-            lambda d: lax.dynamic_slice_in_dim(value, d * size, size, 0), "seq", lengths, stride
-        )
-        return line_gather(piece.astype(bf16), "seq", lengths, stride)
-
-    wo_sum = line_sum(weight_rows(wo_term))
-    wqkv_sum = line_sum(weight_rows(wqkv_term))
-
-    def team_stack(value):
-        came = [value] + [swap(value, everyone, members, d) for d in range(1, team)]
-        return [lax.select_n(mine ^ u, *came) for u in range(team)]
-
-    if team == 2 and heads_width % LANES == 0:
-        place = mine.astype(jnp.int32).reshape(1)
-        output_grad_w = widen_halves(place, wo_sum, swap(wo_sum, everyone, members, 1))
-        head_gradients = spread_heads(
-            place, wqkv_sum, swap(wqkv_sum, everyone, members, 1), heads_width
-        )
-    else:
-        output_grad_w = jnp.concatenate(team_stack(wo_sum), axis=0).astype(f32)
-        wqkv_all = [v.reshape(rows, pairs, 3, LANES) for v in team_stack(wqkv_sum)]
-
-        def head_gradient(i):
-            split = [v[:, :, i].reshape(rows, shards, heads_width) for v in wqkv_all]
-            return jnp.stack(split, axis=2).reshape(rows, features).astype(f32)
-
-        head_gradients = [head_gradient(i) for i in range(3)]
-
+    line = lengths // stride
+    wo_rows = heads_width // line
+
+    wo_own = wo_own.reshape(line, wo_rows, features)
+    wo_own = jnp.concatenate([wo_own[:, :, t * width : (t + 1) * width] for t in range(team)], 1)
+    packed = jnp.concatenate([wqkv_own, wo_own.reshape(rows, width)], axis=1)
+    size = rows // line
+    packed = line_scatter(
+        lambda d: lax.dynamic_slice_in_dim(packed, d * size, size, 0), "seq", lengths, stride
+    )
     gain_terms = jnp.stack([gain_first_term, gain_second_term])
     for axis, size in (("rep", copies), ("fsdp", shards), ("seq", lengths)):
         for bit in bit_orders(size)[0]:
             gain_terms = gain_terms + swap(gain_terms, axis, size, bit)
+    packed, gain_terms = together(packed.astype(bf16), gain_terms)
+    packed = line_gather(packed, "seq", lengths, stride)
+
+    def unpack(value):
+        out = value[:, 3 * width :].reshape(line, team, wo_rows, width)
+        out = jnp.concatenate([out[:, t] for t in range(team)], axis=2)
+        return value[:, : 3 * width], out.reshape(heads_width, features)
+
+    def team_stack(value):
+        came = [value] + [swap(value, everyone, members, d) for d in range(1, team)]
+        return [lax.select_n(mine ^ u, *came) for u in range(team)]
+
+    if team == 2 and heads_width % LANES == 0:
+        place = mine.astype(jnp.int32).reshape(1)
+        wqkv_sum, wo_sum = unpack(packed)
+        wqkv_other, wo_other = unpack(swap(packed, everyone, members, 1))
+        output_grad_w = widen_halves(place, wo_sum, wo_other)
+        head_gradients = spread_heads(place, wqkv_sum, wqkv_other, heads_width)
+    else:
+        sums = [unpack(v) for v in team_stack(packed)]
+        output_grad_w = jnp.concatenate([v for _, v in sums], axis=0).astype(f32)
+        wqkv_all = [v.reshape(rows, pairs, 3, LANES) for v, _ in sums]
+
+        def head_gradient(i):
+            split = [v[:, :, i].reshape(rows, shards, heads_width) for v in wqkv_all]
+            return jnp.stack(split, axis=2).reshape(rows, features).astype(f32)
+
+        head_gradients = [head_gradient(i) for i in range(3)]
+
     gain_grads = lax.dynamic_slice_in_dim(gain_terms, f * rows, rows, 1)
     return (
         layer_output,

time: 1490 us -> 1480 us (level)
  starting transfers between devices: 195 us -> 111 us
  other arithmetic: 113 us -> 172 us
  waiting for transfers between devices: 620 us -> 642 us
  local copies, waits for them, and re-layouts: 147 us -> 132 us
    ppermute x76 -> x49, waiting for transfers between devices: 417 us -> 280 us  [swap(): return lax.ppermute(value, axis, [(i, i ^ distance) for i in range(size)])]
    ppermute x76 -> x49, starting transfers between devices: 119 us -> 48.5 us  [swap(): return lax.ppermute(value, axis, [(i, i ^ distance) for i in range(size)])]
    ppermute x4, waiting for transfers between devices: 23.6 us -> 62.1 us  [take_sequence(): lax.ppermute(lax.dynamic_index_in_dim(value, lax.rem(z + k, batch), 0, Fa...]
    ppermute x6 -> x3, waiting for transfers between devices: 16.1 us -> 54.2 us  [line_gather(): lax.ppermute(downs[-1], axis, line_pairs(size, stride, 1, last - s, -1))]
    ppermute x6 -> x3, waiting for transfers between devices: 26.4 us -> 57.8 us  [line_scatter(): lax.ppermute(down, axis, line_pairs(size, stride, last - s, last, -1))]
    unnamed x111 -> x130, local copies, waits for them, and re-layouts: 36.5 us -> 5.41 us
    ppermute x6 -> x3, waiting for transfers between devices: 22.6 us -> 49.6 us  [line_scatter(): up = lax.ppermute(up, axis, line_pairs(size, stride, 0, s, 1))]
    concatenate x0 -> x19, other arithmetic: none -> 23 us  [the longest x8 9.18 us: scatter_in_order(): sent = jnp.concatenate(blocks[kept:], axis=0)]
  transfers between devices with their start and end apart: 115 -> 78, of which waited for: 42 -> 36; matrix products, arithmetic and copies ran while one was open for 32% -> 33% of each run, Pallas kernels for 6% -> 6%
where the time goes in v3:
time: 1480 us; the launch traced here: 1470 us
  waiting for transfers between devices  642 us (43%)
  matrix products  300 us (20%)
  other arithmetic  172 us (12%)
  local copies, waits for them, and re-layouts  132 us (9%)
  starting transfers between devices  111 us (8%)
  Pallas kernels  95.8 us (6%)
  between operations  15.7 us (1%)
    ppermute x49, waiting for transfers between devices, swap(): return lax.ppermute(value, axis, [(i, i ^ distance) for i in range(size)])  280 us
    ppermute x4, waiting for transfers between devices, give_back(): lax.ppermute(lax.dynamic_index_in_dim(blocks, lax.rem(local_seq + batch -...  122 us
    dot_general x5, matrix products, matmul(): return jnp.dot(left_op, right_op, preferred_element_type=f32).astype(out)  102 us
    dot_general x5, matrix products, against(): lax.dot_general(left_op, right_op, (((1,), (1,)), ((), ())), preferred_el...  101 us
    dot_general x5, matrix products, outer_sum(): lax.dot_general(left_op, right_op, (((0,), (0,)), ((), ())), preferred_el...  96.6 us
    ppermute x4, waiting for transfers between devices, take_sequence(): lax.ppermute(lax.dynamic_index_in_dim(value, lax.rem(z + k, batch), 0, Fa...  62.1 us
    ppermute x3, waiting for transfers between devices, line_scatter(): lax.ppermute(down, axis, line_pairs(size, stride, last - s, last, -1))  57.8 us
    ppermute x3, waiting for transfers between devices, line_gather(): lax.ppermute(downs[-1], axis, line_pairs(size, stride, 1, last - s, -1))  54.2 us
  transfers between devices with their start and end apart: 78, of which 36 were waited for; matrix products, arithmetic and copies ran while one was open for 33% of the time, Pallas kernels for 6%

profile of v3, /device:TPU:9, one launch (start us, length us, event | category | flops | bytes accessed | tf_op | source)
XLA Modules:
  0.0 1467.7 jit_solution(9335581410754659157)
XLA Ops:
  44.0 39.5 %collective-permute-done.1 = bf16[256,2048]{1,0:T(8,128)(2,1)} collective-permute-done((bf16[256,2048]{1,0:T(8,128)(2,1)}, bf16[256,2048]{1,0:T(8,128)(2,1)}, u32[]{:S(2)}, u32[]{:S(2)}) %collective-permute-start.1) | collective-permute-done | bytes 1048608 | tf_op jit(solution)/shard_map/ppermute | solution.py:548
  136.0 16.1 %collective-permute-done.8 = bf16[512,3072]{1,0:T(8,128)(2,1)} collective-permute-done((bf16[512,3072]{1,0:T(8,128)(2,1)}, bf16[512,3072]{1,0:T(8,128)(2,1)}, u32[]{:S(2)}, u32[]{:S(2)}) %collective-permute-start.8) | collective-permute-done | bytes 3145760 | tf_op jit(solution)/shard_map/ppermute | solution.py:456
  161.4 37.0 %collective-permute-done.10 = bf16[512,3072]{1,0:T(8,128)(2,1)S(1)} collective-permute-done((bf16[512,3072]{1,0:T(8,128)(2,1)S(1)}, bf16[512,3072]{1,0:T(8,128)(2,1)S(1)}, u32[]{:S(2)}, u32[]{:S(2)}) %collective-permute-start.10) | collective-permute-done | bytes 3145760 | tf_op jit(solution)/shard_map/ppermute | solution.py:456
  210.3 19.0 %fusion.16.lin_ref = f32[1024,3072]{1,0:T(8,128)} fusion(bf16[2048,3072]{1,0:T(8,128)(2,1)} %slice_dynamic-update-slice_fusion, bf16[512,2048]{1,0:T(8,128)(2,1)} %get-tuple-element.167, bf16[512,2048]{1,0:T(8,128)(2,1)} %get-tuple-element.166), kind=kOutput, calls=%fused_computation.81 | convolution fusion | flops 12893290496 | bytes 29360128 | tf_op jit(solution)/shard_map/dot_general | solution.py:27
  229.3 35.6 %attend_forward.1 = (bf16[1024,1024]{1,0:T(8,128)(2,1)}, bf16[1024,3072]{1,0:T(8,128)(2,1)}, f32[8,4,512]{2,1,0:T(4,128)}) custom-call(s32[1]{0:T(128)} %collective-permute-done.6.start_ref, f32[1024,3072]{1,0:T(8,128)} %fusion.16.lin_ref, f32[1024,128]{1,0:T(8,128)} %get-tuple-element.215.cos_ref, f32[1024,128]{1,0:T(8,128)} %get-tuple-element.216.sin_ref), custom_call_target="tpu_custom_call" | custom-call | flops 8589934592 | bytes 20971520 | tf_op jit(solution)/shard_map/attend_forward/pallas_call | solution.py:232
  271.1 16.5 %all-gather.9.cloned.1.call-done = bf16[1024,2048]{1,0:T(8,128)(2,1)} async-done(((bf16[256,2048]{1,0:T(8,128)(2,1)}), bf16[1024,2048]{1,0:T(8,128)(2,1)}) %all-gather.9.cloned.1.call-update) | async-done | bytes 4194320 | tf_op jit(solution)/shard_map/all_gather | solution.py:625
  297.6 42.9 %collective-permute-done.21 = bf16[3,2,256,1024]{3,2,1,0:T(8,128)(2,1)} collective-permute-done((bf16[3,2,256,1024]{3,2,1,0:T(8,128)(2,1)}, bf16[3,2,256,1024]{3,2,1,0:T(8,128)(2,1)}, u32[]{:S(2)}, u32[]{:S(2)}) %collective-permute-start.21) | collective-permute-done | bytes 3145760 | tf_op jit(solution)/shard_map/ppermute | solution.py:456
  378.3 23.0 %collective-permute-done.17 = bf16[256,2048]{1,0:T(8,128)(2,1)S(1)} collective-permute-done((bf16[256,2048]{1,0:T(8,128)(2,1)}, bf16[256,2048]{1,0:T(8,128)(2,1)S(1)}, u32[]{:S(2)}, u32[]{:S(2)}) %collective-permute-start.17) | collective-permute-done | bytes 1048608 | tf_op jit(solution)/shard_map/ppermute | solution.py:456
  417.3 31.4 %collective-permute-done.18 = bf16[512,2048]{1,0:T(8,128)(2,1)S(1)} collective-permute-done((bf16[512,2048]{1,0:T(8,128)(2,1)S(1)}, bf16[512,2048]{1,0:T(8,128)(2,1)S(1)}, u32[]{:S(2)}, u32[]{:S(2)}) %collective-permute-start.18) | collective-permute-done | bytes 2097184 | tf_op jit(solution)/shard_map/ppermute | solution.py:456
  456.9 24.7 %fusion.44 = f32[2048,2048]{1,0:T(8,128)} fusion(bf16[2048,2048]{1,0:T(8,128)(2,1)} %all-gather.11.cloned.1.call-done, bf16[2048,2048]{1,0:T(8,128)(2,1)} %param.23), kind=kOutput, calls=%fused_computation.277 | convolution fusion | flops 17179869184 | bytes 33554432 | tf_op jit(solution)/shard_map/dot_general | solution.py:37
  481.6 21.6 %fusion.1 = f32[2048,2048]{1,0:T(8,128)} fusion(bf16[2048,2048]{1,0:T(8,128)(2,1)} %slice_dynamic-update-slice_fusion.4, bf16[2048,1024]{1,0:T(8,128)(2,1)S(1)} %copy-done.34, bf16[2048,1024]{1,0:T(8,128)(2,1)S(1)} %copy-done.33), kind=kOutput, calls=%fused_computation.28 | convolution fusion | flops 17196646400 | bytes 33554432 | tf_op jit(solution)/shard_map/dot_general | solution.py:27
  503.2 35.5 %multiply_convert_fusion = (bf16[2048,2048]{1,0:T(8,128)(2,1)}, bf16[2048,2048]{1,0:T(8,128)(2,1)}, bf16[2048,2048]{1,0:T(8,128)(2,1)}) fusion(f32[2048,2048]{1,0:T(8,128)} %fusion.1, f32[2048,2048]{1,0:T(8,128)} %fusion.44, bf16[2048,2048]{1,0:T(8,128)(2,1)} %slice_dynamic-update-slice_fusion.4, bf16[2048,1024]{1,0:T(8,128)(2,1)} %get-tuple-element.131, ...), kind=kOutput, calls=%fused_computation.1 | convolution fusion | flops 17259560960 | bytes 75497472 | tf_op jit(solution)/shard_map/dot_general | solution.py:27
  538.7 23.9 %convolution_convert_fusion.4 = bf16[2048,2048]{1,0:T(8,128)(2,1)} fusion(bf16[2048,2048]{1,0:T(8,128)(2,1)} %get-tuple-element.70, bf16[2048,2048]{1,0:T(8,128)(2,1)} %all-gather.11.cloned.1.call-done), kind=kOutput, calls=%fused_computation.25 | convolution fusion | flops 17184063488 | bytes 25165824 | tf_op jit(solution)/shard_map/dot_general | solution.py:31
  562.6 24.6 %fusion.2 = f32[2048,2048]{1,0:T(8,128)} fusion(bf16[2048,2048]{1,0:T(8,128)(2,1)} %get-tuple-element.76, bf16[2048,1024]{1,0:T(8,128)(2,1)} %get-tuple-element.131, bf16[2048,1024]{1,0:T(8,128)(2,1)} %get-tuple-element.130), kind=kOutput, calls=%fused_computation.29 | convolution fusion | flops 17196646400 | bytes 33554432 | tf_op jit(solution)/shard_map/dot_general | solution.py:37
  587.3 25.7 %add_convert_fusion = bf16[2048,2048]{1,0:T(8,128)(2,1)} fusion(f32[2048,2048]{1,0:T(8,128)} %fusion.2, bf16[2048,2048]{1,0:T(8,128)(2,1)} %get-tuple-element.74, bf16[2048,1024]{1,0:T(8,128)(2,1)} %get-tuple-element.133, bf16[2048,1024]{1,0:T(8,128)(2,1)} %get-tuple-element.132), kind=kOutput, calls=%fused_computation | convolution fusion | flops 17205035008 | bytes 41943040 | tf_op jit(solution)/shard_map/dot_general | solution.py:37
  612.9 24.0 %convolution_convert_fusion.1 = bf16[2048,2048]{1,0:T(8,128)(2,1)} fusion(bf16[2048,2048]{1,0:T(8,128)(2,1)} %slice_dynamic-update-slice_fusion.4, bf16[2048,2048]{1,0:T(8,128)(2,1)} %get-tuple-element.76), kind=kOutput, calls=%fused_computation.22 | convolution fusion | flops 17184063488 | bytes 25165824 | tf_op jit(solution)/shard_map/dot_general | solution.py:31
  645.5 23.8 %convolution_convert_fusion.2 = bf16[2048,2048]{1,0:T(8,128)(2,1)} fusion(bf16[2048,2048]{1,0:T(8,128)(2,1)} %slice_dynamic-update-slice_fusion.4, bf16[2048,2048]{1,0:T(8,128)(2,1)} %get-tuple-element.74), kind=kOutput, calls=%fused_computation.23 | convolution fusion | flops 17184063488 | bytes 25165824 | tf_op jit(solution)/shard_map/dot_general | solution.py:31
  685.5 42.1 %collective-permute-done.24 = bf16[512,2048]{1,0:T(8,128)(2,1)S(1)} collective-permute-done((bf16[512,2048]{1,0:T(8,128)(2,1)S(1)}, bf16[512,2048]{1,0:T(8,128)(2,1)S(1)}, u32[]{:S(2)}, u32[]{:S(2)}) %collective-permute-start.24) | collective-permute-done | bytes 2097184 | tf_op jit(solution)/shard_map/ppermute | solution.py:456
  732.0 21.4 %convolution_convert_fusion.3 = bf16[2048,2048]{1,0:T(8,128)(2,1)} fusion(bf16[2048,2048]{1,0:T(8,128)(2,1)} %get-tuple-element.70, bf16[2048,2048]{1,0:T(8,128)(2,1)S(1)} %bitcast.199), kind=kOutput, calls=%fused_computation.24 | convolution fusion | flops 17184063488 | bytes 25165824 | tf_op jit(solution)/shard_map/dot_general | solution.py:27
  774.6 38.1 %collective-permute-done.39 = bf16[512,2048]{1,0:T(8,128)(2,1)} collective-permute-done((bf16[512,2048]{1,0:T(8,128)(2,1)}, bf16[512,2048]{1,0:T(8,128)(2,1)}, u32[]{:S(2)}, u32[]{:S(2)}) %collective-permute-start.39) | collective-permute-done | bytes 2097184 | tf_op jit(solution)/shard_map/ppermute | solution.py:456
  846.0 44.2 %attend_backward.1 = bf16[1024,3072]{1,0:T(8,128)(2,1)} custom-call(s32[1]{0:T(128)} %collective-permute-done.6.start_ref, bf16[1024,3072]{1,0:T(8,128)(2,1)} %get-tuple-element.53.qkv_ref, bf16[1024,1024]{1,0:T(8,128)(2,1)} %get-tuple-element.57.out_ref, bf16[1024,1024]{1,0:T(8,128)(2,1)} %fusion.17.grad_ref, f32[8,4,512]{2,1,0:T(4,128)} %get-tuple-element.73.lse_ref, ...), custom_call_target="tpu_custom_call" | custom-call | flops 21474836480 | bytes 16777216 | tf_op jit(solution)/shard_map/attend_backward/pallas_call | solution.py:273
  931.7 20.0 %convolution_convert_fusion = bf16[2048,3072]{1,0:T(8,128)(2,1)} fusion(bf16[1024,3072]{1,0:T(8,128)(2,1)} %attend_backward.1, bf16[512,2048]{1,0:T(8,128)(2,1)} %get-tuple-element.167, bf16[512,2048]{1,0:T(8,128)(2,1)} %get-tuple-element.166), kind=kOutput, calls=%fused_computation.6 | convolution fusion | flops 12899581952 | bytes 23068672 | tf_op jit(solution)/shard_map/dot_general | solution.py:31
  977.1 16.3 %convolution_convert_fusion.5 = bf16[1024,2048]{1,0:T(8,128)(2,1)} fusion(bf16[1024,3072]{1,0:T(8,128)(2,1)} %attend_backward.1, bf16[2048,3072]{1,0:T(8,128)(2,1)S(1)} %bitcast.162), kind=kOutput, calls=%fused_computation.65 | convolution fusion | flops 12886999040 | bytes 23068672 | tf_op jit(solution)/shard_map/dot_general | solution.py:37
  1000.5 17.5 %collective-permute-done.48 = bf16[256,2048]{1,0:T(8,128)(2,1)} collective-permute-done((bf16[256,2048]{1,0:T(8,128)(2,1)}, bf16[256,2048]{1,0:T(8,128)(2,1)}, u32[]{:S(2)}, u32[]{:S(2)}) %collective-permute-start.48) | collective-permute-done | bytes 1048608 | tf_op jit(solution)/shard_map/ppermute | solution.py:563
  1018.0 59.3 %collective-permute-done.49 = bf16[256,2048]{1,0:T(8,128)(2,1)} collective-permute-done((bf16[256,2048]{1,0:T(8,128)(2,1)}, bf16[256,2048]{1,0:T(8,128)(2,1)}, u32[]{:S(2)}, u32[]{:S(2)}) %collective-permute-start.49) | collective-permute-done | bytes 1048608 | tf_op jit(solution)/shard_map/ppermute | solution.py:563
  1111.1 20.5 %collective-permute-done.52 = bf16[128,4096]{1,0:T(8,128)(2,1)} collective-permute-done((bf16[128,4096]{1,0:T(8,128)(2,1)}, bf16[128,4096]{1,0:T(8,128)(2,1)}, u32[]{:S(2)}, u32[]{:S(2)}) %collective-permute-start.52) | collective-permute-done | bytes 1048608 | tf_op jit(solution)/shard_map/ppermute | solution.py:422
  1136.1 29.1 %collective-permute-done.53 = bf16[128,4096]{1,0:T(8,128)(2,1)} collective-permute-done((bf16[128,4096]{1,0:T(8,128)(2,1)}, bf16[128,4096]{1,0:T(8,128)(2,1)}, u32[]{:S(2)}, u32[]{:S(2)}) %collective-permute-start.53) | collective-permute-done | bytes 1048608 | tf_op jit(solution)/shard_map/ppermute | solution.py:422
  1178.8 57.8 %collective-permute-done.56 = bf16[128,4096]{1,0:T(8,128)(2,1)} collective-permute-done((bf16[128,4096]{1,0:T(8,128)(2,1)}, bf16[128,4096]{1,0:T(8,128)(2,1)}, u32[]{:S(2)}, u32[]{:S(2)}) %collective-permute-start.56) | collective-permute-done | bytes 1048608 | tf_op jit(solution)/shard_map/ppermute | solution.py:423
  1264.8 20.3 %collective-permute-done.64 = bf16[128,4096]{1,0:T(8,128)(2,1)S(1)} collective-permute-done((bf16[128,4096]{1,0:T(8,128)(2,1)S(1)}, bf16[128,4096]{1,0:T(8,128)(2,1)S(1)}, u32[]{:S(2)}, u32[]{:S(2)}) %collective-permute-start.64) | collective-permute-done | bytes 1048608 | tf_op jit(solution)/shard_map/ppermute | solution.py:440
  1292.4 18.3 %collective-permute-done.65 = bf16[128,4096]{1,0:T(8,128)(2,1)} collective-permute-done((bf16[128,4096]{1,0:T(8,128)(2,1)S(1)}, bf16[128,4096]{1,0:T(8,128)(2,1)}, u32[]{:S(2)}, u32[]{:S(2)}) %collective-permute-start.65) | collective-permute-done | bytes 1048608 | tf_op jit(solution)/shard_map/ppermute | solution.py:440
  1353.8 17.7 %collective-permute-done.50 = bf16[256,2048]{1,0:T(8,128)(2,1)S(1)} collective-permute-done((bf16[256,2048]{1,0:T(8,128)(2,1)}, bf16[256,2048]{1,0:T(8,128)(2,1)S(1)}, u32[]{:S(2)}, u32[]{:S(2)}) %collective-permute-start.50) | collective-permute-done | bytes 1048608 | tf_op jit(solution)/shard_map/ppermute | solution.py:563
  1371.5 27.3 %collective-permute-done.51 = bf16[256,2048]{1,0:T(8,128)(2,1)S(1)} collective-permute-done((bf16[256,2048]{1,0:T(8,128)(2,1)S(1)}, bf16[256,2048]{1,0:T(8,128)(2,1)S(1)}, u32[]{:S(2)}, u32[]{:S(2)}) %collective-permute-start.51) | collective-permute-done | bytes 1048608 | tf_op jit(solution)/shard_map/ppermute | solution.py:563
  (448 shorter events, 537.3 us)
Async XLA Ops:
  7.2 280.3 %all-gather.9.cloned.1.call-start = ((), (), s32[]{:S(2)}) async-start(), calls=%async_computation.3 | async-start | bytes 5242880 | tf_op jit(solution)/shard_map/all_gather | solution.py:625
  15.3 68.2 %collective-permute-start.1 = (bf16[256,2048]{1,0:T(8,128)(2,1)}, bf16[256,2048]{1,0:T(8,128)(2,1)}, u32[]{:S(2)}, u32[]{:S(2)}) collective-permute-start(bf16[256,2048]{1,0:T(8,128)(2,1)} %get-tuple-element.184), channel_id=1, source_target_pairs={{0,8},{1,24},{8,0},{9,16},{16,9},{17,25},{24,1},{25,17},{2,10},{3,... | collective-permute-start | bytes 3145736 | tf_op jit(solution)/shard_map/ppermute | solution.py:548
  16.9 77.8 %collective-permute-start.11 = (bf16[256,2048]{1,0:T(8,128)(2,1)}, bf16[256,2048]{1,0:T(8,128)(2,1)}, u32[]{:S(2)}, u32[]{:S(2)}) collective-permute-start(bf16[256,2048]{1,0:T(8,128)(2,1)} %get-tuple-element.189), channel_id=1, source_target_pairs={{0,0},{1,16},{8,8},{9,24},{16,1},{17,17},{24,9},{25,25},{2,2},{3,1... | collective-permute-start | bytes 3145736 | tf_op jit(solution)/shard_map/ppermute | solution.py:548
  21.3 84.8 %collective-permute-start.12 = (bf16[256,2048]{1,0:T(8,128)(2,1)}, bf16[256,2048]{1,0:T(8,128)(2,1)}, u32[]{:S(2)}, u32[]{:S(2)}) collective-permute-start(bf16[256,2048]{1,0:T(8,128)(2,1)} %get-tuple-element.188), channel_id=1, source_target_pairs={{0,8},{1,24},{8,0},{9,16},{16,9},{17,25},{24,1},{25,17},{2,10},{3,... | collective-permute-start | bytes 3145736 | tf_op jit(solution)/shard_map/ppermute | solution.py:548
  42.3 68.8 %collective-permute-start.7 = (bf16[256,3072]{1,0:T(8,128)(2,1)}, bf16[256,3072]{1,0:T(8,128)(2,1)S(1)}, u32[]{:S(2)}, u32[]{:S(2)}) collective-permute-start(bf16[256,3072]{1,0:T(8,128)(2,1)} %get-tuple-element.170), channel_id=1, source_target_pairs={{0,2},{2,0},{4,6},{6,4},{1,3},{3,1},{5,7},{7,5},{8,10},{10,8},{12,... | collective-permute-start | bytes 4718600 | tf_op jit(solution)/shard_map/ppermute | solution.py:456
  42.7 84.1 %collective-permute-start.9 = (bf16[256,3072]{1,0:T(8,128)(2,1)}, bf16[256,3072]{1,0:T(8,128)(2,1)}, u32[]{:S(2)}, u32[]{:S(2)}) collective-permute-start(bf16[256,3072]{1,0:T(8,128)(2,1)} %get-tuple-element.168), channel_id=1, source_target_pairs={{0,4},{2,6},{4,0},{6,2},{1,5},{3,7},{5,1},{7,3},{8,12},{10,14},{12... | collective-permute-start | bytes 4718600 | tf_op jit(solution)/shard_map/ppermute | solution.py:456
  116.7 112.6 %collective-permute-start.6 = (s32[1]{0:T(128)}, s32[1]{0:T(128)}, u32[]{:S(2)}, u32[]{:S(2)}) collective-permute-start(s32[1]{0:T(128)} %dynamic_slice.215), channel_id=1, source_target_pairs={{0,0},{1,16},{8,8},{9,24},{16,1},{17,17},{24,9},{25,25},{2,2},{3,1... | collective-permute-start | bytes 20 | tf_op jit(solution)/shard_map/ppermute | solution.py:599
  129.0 69.4 %collective-permute-start.10 = (bf16[512,3072]{1,0:T(8,128)(2,1)S(1)}, bf16[512,3072]{1,0:T(8,128)(2,1)S(1)}, u32[]{:S(2)}, u32[]{:S(2)}) collective-permute-start(bf16[512,3072]{1,0:T(8,128)(2,1)S(1)} %pad_maximum_fusion.10), channel_id=1, source_target_pairs={{0,2},{2,0},{4,6},{6,4},{1,3},{3,1},{5,7},{7,5},{8,10},{10,8},{12,... | collective-permute-start | bytes 9437192 | tf_op jit(solution)/shard_map/ppermute | solution.py:456
  204.9 60.0 %collective-permute-start.15 = (bf16[2,256,1024]{2,1,0:T(8,128)(2,1)}, bf16[2,256,1024]{2,1,0:T(8,128)(2,1)S(1)}, u32[]{:S(2)}, u32[]{:S(2)}) collective-permute-start(bf16[2,256,1024]{2,1,0:T(8,128)(2,1)} %pad_maximum_fusion.33), channel_id=1, source_target_pairs={{0,6},{2,4},{4,2},{6,0},{1,7},{3,5},{5,3},{7,1},{8,14},{10,12},{12... | collective-permute-start | bytes 3145736 | tf_op jit(solution)/shard_map/ppermute | solution.py:456
  207.1 60.3 %collective-permute-start.14 = (bf16[2,256,1024]{2,1,0:T(8,128)(2,1)}, bf16[2,256,1024]{2,1,0:T(8,128)(2,1)S(1)}, u32[]{:S(2)}, u32[]{:S(2)}) collective-permute-start(bf16[2,256,1024]{2,1,0:T(8,128)(2,1)} %pad_maximum_fusion.32), channel_id=1, source_target_pairs={{0,4},{2,6},{4,0},{6,2},{1,5},{3,7},{5,1},{7,3},{8,12},{10,14},{12... | collective-permute-start | bytes 3145736 | tf_op jit(solution)/shard_map/ppermute | solution.py:456
  209.4 58.0 %collective-permute-start.13 = (bf16[2,256,1024]{2,1,0:T(8,128)(2,1)}, bf16[2,256,1024]{2,1,0:T(8,128)(2,1)}, u32[]{:S(2)}, u32[]{:S(2)}) collective-permute-start(bf16[2,256,1024]{2,1,0:T(8,128)(2,1)} %pad_maximum_fusion.31), channel_id=1, source_target_pairs={{0,2},{2,0},{4,6},{6,4},{1,3},{3,1},{5,7},{7,5},{8,10},{10,8},{12,... | collective-permute-start | bytes 3145736 | tf_op jit(solution)/shard_map/ppermute | solution.py:456
  209.7 247.2 %all-gather.11.cloned.1.call-start = ((), (), s32[]{:S(2)}) async-start(), calls=%async_computation.4 | async-start | bytes 10485760 | tf_op jit(solution)/shard_map/all_gather | solution.py:627
  271.1 69.4 %collective-permute-start.21 = (bf16[3,2,256,1024]{3,2,1,0:T(8,128)(2,1)}, bf16[3,2,256,1024]{3,2,1,0:T(8,128)(2,1)}, u32[]{:S(2)}, u32[]{:S(2)}) collective-permute-start(bf16[3,2,256,1024]{3,2,1,0:T(8,128)(2,1)} %pad_maximum_fusion.11), channel_id=1, source_target_pairs={{0,8},{8,0},{16,24},{24,16},{1,9},{9,1},{17,25},{25,17},{2,10},{10... | collective-permute-start | bytes 9437192 | tf_op jit(solution)/shard_map/ppermute | solution.py:456
  287.5 540.2 %reduce-scatter.8.cloned.1.call-start = ((), (), s32[]{:S(2)}) async-start(), calls=%async_computation.7 | async-start | bytes 9437184 | tf_op jit(solution)/shard_map/reduce_scatter | solution.py:716
  562.6 341.7 %reduce-scatter.6.cloned.1.call-start = ((), (), s32[]{:S(2)}) async-start(), calls=%async_computation.6 | async-start | bytes 9437184 | tf_op jit(solution)/shard_map/reduce_scatter | solution.py:716
  645.4 263.9 %reduce-scatter.4.cloned.1.call-start = ((), (), s32[]{:S(2)}) async-start(), calls=%async_computation.5 | async-start | bytes 9437184 | tf_op jit(solution)/shard_map/reduce_scatter | solution.py:716
  677.7 729.6 %all-gather.17.cloned.1.call-start = ((), (), s32[]{:S(2)}) async-start(), calls=%async_computation.10 | async-start | bytes 9437184 | tf_op jit(solution)/shard_map/all_gather | solution.py:719
  771.1 52.8 %collective-permute-start.28 = (bf16[512,2048]{1,0:T(8,128)(2,1)S(1)}, bf16[512,2048]{1,0:T(8,128)(2,1)}, u32[]{:S(2)}, u32[]{:S(2)}) collective-permute-start(bf16[512,2048]{1,0:T(8,128)(2,1)S(1)} %get-tuple-element.71), channel_id=1, source_target_pairs={{0,1},{1,0},{8,9},{9,8},{16,17},{17,16},{24,25},{25,24},{2,3},{3,2... | collective-permute-start | bytes 6291464 | tf_op jit(solution)/shard_map/ppermute | solution.py:456
  817.2 78.6 %collective-permute-start.40 = (bf16[256,2048]{1,0:T(8,128)(2,1)}, bf16[256,2048]{1,0:T(8,128)(2,1)}, u32[]{:S(2)}, u32[]{:S(2)}) collective-permute-start(bf16[256,2048]{1,0:T(8,128)(2,1)} %slice.353), channel_id=1, source_target_pairs={{0,2},{2,0},{4,6},{6,4},{1,3},{3,1},{5,7},{7,5},{8,10},{10,8},{12,... | collective-permute-start | bytes 3145736 | tf_op jit(solution)/shard_map/ppermute | solution.py:456
  822.5 75.0 %collective-permute-start.42 = (bf16[256,2048]{1,0:T(8,128)(2,1)}, bf16[256,2048]{1,0:T(8,128)(2,1)S(1)}, u32[]{:S(2)}, u32[]{:S(2)}) collective-permute-start(bf16[256,2048]{1,0:T(8,128)(2,1)} %slice.352), channel_id=1, source_target_pairs={{0,4},{2,6},{4,0},{6,2},{1,5},{3,7},{5,1},{7,3},{8,12},{10,14},{12... | collective-permute-start | bytes 3145736 | tf_op jit(solution)/shard_map/ppermute | solution.py:456
  827.8 591.2 %all-gather.15.cloned.1.call-start = ((), (), s32[]{:S(2)}) async-start(), calls=%async_computation.9 | async-start | bytes 9437184 | tf_op jit(solution)/shard_map/all_gather | solution.py:719
  845.2 47.1 %collective-permute-start.37 = (bf16[256,2048]{1,0:T(8,128)(2,1)}, bf16[256,2048]{1,0:T(8,128)(2,1)}, u32[]{:S(2)}, u32[]{:S(2)}) collective-permute-start(bf16[256,2048]{1,0:T(8,128)(2,1)} %pad_maximum_fusion.35), channel_id=1, source_target_pairs={{0,2},{2,0},{4,6},{6,4},{1,3},{3,1},{5,7},{7,5},{8,10},{10,8},{12,... | collective-permute-start | bytes 3145736 | tf_op jit(solution)/shard_map/ppermute | solution.py:456
  953.2 64.8 %collective-permute-start.48 = (bf16[256,2048]{1,0:T(8,128)(2,1)}, bf16[256,2048]{1,0:T(8,128)(2,1)}, u32[]{:S(2)}, u32[]{:S(2)}) collective-permute-start(bf16[256,2048]{1,0:T(8,128)(2,1)} %get-tuple-element.178), channel_id=1, source_target_pairs={{0,0},{16,1},{8,8},{24,9},{1,16},{17,17},{9,24},{25,25},{2,2},{18,... | collective-permute-start | bytes 3145736 | tf_op jit(solution)/shard_map/ppermute | solution.py:563
  963.4 113.9 %collective-permute-start.49 = (bf16[256,2048]{1,0:T(8,128)(2,1)}, bf16[256,2048]{1,0:T(8,128)(2,1)}, u32[]{:S(2)}, u32[]{:S(2)}) collective-permute-start(bf16[256,2048]{1,0:T(8,128)(2,1)} %get-tuple-element.177), channel_id=1, source_target_pairs={{8,0},{24,1},{0,8},{16,9},{9,16},{25,17},{1,24},{17,25},{10,2},{26... | collective-permute-start | bytes 3145736 | tf_op jit(solution)/shard_map/ppermute | solution.py:563
  963.9 466.9 %all-gather.13.cloned.1.call-start = ((), (), s32[]{:S(2)}) async-start(), calls=%async_computation.8 | async-start | bytes 9437184 | tf_op jit(solution)/shard_map/all_gather | solution.py:719
  973.6 105.4 %collective-permute-start.43 = (bf16[512,3072]{1,0:T(8,128)(2,1)}, bf16[512,3072]{1,0:T(8,128)(2,1)}, u32[]{:S(2)}, u32[]{:S(2)}) collective-permute-start(bf16[512,3072]{1,0:T(8,128)(2,1)} %pad_maximum_fusion.12), channel_id=1, source_target_pairs={{0,4},{2,6},{4,0},{6,2},{1,5},{3,7},{5,1},{7,3},{8,12},{10,14},{12... | collective-permute-start | bytes 9437192 | tf_op jit(solution)/shard_map/ppermute | solution.py:456
  975.6 107.5 %collective-permute-start.45 = (bf16[512,3072]{1,0:T(8,128)(2,1)}, bf16[512,3072]{1,0:T(8,128)(2,1)}, u32[]{:S(2)}, u32[]{:S(2)}) collective-permute-start(bf16[512,3072]{1,0:T(8,128)(2,1)} %pad_maximum_fusion.13), channel_id=1, source_target_pairs={{0,2},{2,0},{4,6},{6,4},{1,3},{3,1},{5,7},{7,5},{8,10},{10,8},{12,... | collective-permute-start | bytes 9437192 | tf_op jit(solution)/shard_map/ppermute | solution.py:456
  995.3 93.8 %collective-permute-start.47 = (bf16[512,2048]{1,0:T(8,128)(2,1)S(1)}, bf16[512,2048]{1,0:T(8,128)(2,1)S(1)}, u32[]{:S(2)}, u32[]{:S(2)}) collective-permute-start(bf16[512,2048]{1,0:T(8,128)(2,1)S(1)} %constant_dynamic-slice_fusion.1), channel_id=1, source_target_pairs={{0,1},{1,0},{8,9},{9,8},{16,17},{17,16},{24,25},{25,24},{2,3},{3,2... | collective-permute-start | bytes 6291464 | tf_op jit(solution)/shard_map/ppermute | solution.py:456
  1168.9 67.7 %collective-permute-start.56 = (bf16[128,4096]{1,0:T(8,128)(2,1)}, bf16[128,4096]{1,0:T(8,128)(2,1)}, u32[]{:S(2)}, u32[]{:S(2)}) collective-permute-start(bf16[128,4096]{1,0:T(8,128)(2,1)} %get-tuple-element.141), channel_id=1, source_target_pairs={{16,8},{24,16},{17,9},{25,17},{18,10},{26,18},{19,11},{27,19},{20,... | collective-permute-start | bytes 3145736 | tf_op jit(solution)/shard_map/ppermute | solution.py:423
  1174.6 82.3 %collective-permute-start.54 = (bf16[128,4096]{1,0:T(8,128)(2,1)}, bf16[128,4096]{1,0:T(8,128)(2,1)}, u32[]{:S(2)}, u32[]{:S(2)}) collective-permute-start(bf16[128,4096]{1,0:T(8,128)(2,1)} %get-tuple-element.140), channel_id=1, source_target_pairs={{0,8},{8,16},{16,24},{1,9},{9,17},{17,25},{2,10},{10,18},{18,26},{... | collective-permute-start | bytes 3145736 | tf_op jit(solution)/shard_map/ppermute | solution.py:422
  1340.8 101.7 %collective-permute-start.69 = (bf16[512,4096]{1,0:T(8,128)(2,1)}, bf16[512,4096]{1,0:T(8,128)(2,1)}, u32[]{:S(2)}, u32[]{:S(2)}) collective-permute-start(bf16[512,4096]{1,0:T(8,128)(2,1)} %select_dynamic-update-slice_fusion), channel_id=1, source_target_pairs={{0,1},{1,0},{8,9},{9,8},{16,17},{17,16},{24,25},{25,24},{2,3},{3,2... | collective-permute-start | bytes 12582920 | tf_op jit(solution)/shard_map/ppermute | solution.py:456
  1348.8 50.0 %collective-permute-start.51 = (bf16[256,2048]{1,0:T(8,128)(2,1)S(1)}, bf16[256,2048]{1,0:T(8,128)(2,1)S(1)}, u32[]{:S(2)}, u32[]{:S(2)}) collective-permute-start(bf16[256,2048]{1,0:T(8,128)(2,1)S(1)} %get-tuple-element.173), channel_id=1, source_target_pairs={{8,0},{24,1},{0,8},{16,9},{9,16},{25,17},{1,24},{17,25},{10,2},{26... | collective-permute-start | bytes 3145736 | tf_op jit(solution)/shard_map/ppermute | solution.py:563
  (111 other events, 3098.7 us)
Sparse Core Ops, SparseCore 0:
  209.8 77.6 all-gather.8
  289.4 87.8 all-gather.10
  562.7 93.3 reduce-scatter.7
  658.2 88.1 reduce-scatter.5
  748.6 88.0 reduce-scatter.3
  838.2 79.1 all-gather.16
  964.0 111.5 all-gather.14
  1136.2 106.7 all-gather.12

commit v4 on v3

--- a/solution.py
+++ b/solution.py
@@ -761,9 +761,7 @@
     )
     layer_output = give_back(layer_rows.astype(bf16))
     wqkv_own = scatter_in_order(wqkv_term, f, "fsdp", shards).astype(bf16)
-    wqkv_own, first_grad, layer_output = together(
-        wqkv_own, team_scatter(against(lin_grad, wqkv, bf16)), layer_output
-    )
+    wqkv_own, first_grad = together(wqkv_own, team_scatter(against(lin_grad, wqkv, bf16)))
     down_grad = members_gather(down_piece).reshape(part, features).astype(f32)
     gate_grad_w = members_gather(gate_spread).reshape(rows, hidden).astype(f32)
     up_grad_w = members_gather(up_spread).reshape(rows, hidden).astype(f32)
@@ -795,7 +793,9 @@
         for bit in bit_orders(size)[0]:
             gain_terms = gain_terms + swap(gain_terms, axis, size, bit)
     packed, gain_terms = together(packed.astype(bf16), gain_terms)
-    packed = line_gather(packed, "seq", lengths, stride)
+    packed, gate_grad_w, up_grad_w, down_grad = together(
+        line_gather(packed, "seq", lengths, stride), gate_grad_w, up_grad_w, down_grad
+    )
 
     def unpack(value):
         out = value[:, 3 * width :].reshape(line, team, wo_rows, width)

time: 1480 us -> 1460 us (0.986)
  waiting for transfers between devices: 642 us -> 616 us
    ppermute x3, waiting for transfers between devices: 57.8 us -> 14.2 us  [line_scatter(): lax.ppermute(down, axis, line_pairs(size, stride, last - s, last, -1))]
    ppermute x4, waiting for transfers between devices: 122 us -> 79.8 us  [give_back(): lax.ppermute(lax.dynamic_index_in_dim(blocks, lax.rem(local_seq + batch -...]
    ppermute x3, waiting for transfers between devices: 49.6 us -> 86.4 us  [line_scatter(): up = lax.ppermute(up, axis, line_pairs(size, stride, 0, s, 1))]
    ppermute x49, waiting for transfers between devices: 280 us -> 315 us  [swap(): return lax.ppermute(value, axis, [(i, i ^ distance) for i in range(size)])]
  transfers between devices with their start and end apart: 78 -> 78, of which waited for: 36 -> 37; matrix products, arithmetic and copies ran while one was open for 33% -> 33% of each run, Pallas kernels for 6% -> 6%
where the time goes in v4:
time: 1460 us; the launch traced here: 1450 us
  waiting for transfers between devices  616 us (42%)
  matrix products  298 us (20%)
  other arithmetic  176 us (12%)
  local copies, waits for them, and re-layouts  141 us (10%)
  starting transfers between devices  111 us (8%)
  Pallas kernels  95.3 us (7%)
  between operations  15.7 us (1%)
    ppermute x49, waiting for transfers between devices, swap(): return lax.ppermute(value, axis, [(i, i ^ distance) for i in range(size)])  315 us
    dot_general x5, matrix products, matmul(): return jnp.dot(left_op, right_op, preferred_element_type=f32).astype(out)  102 us
    dot_general x5, matrix products, outer_sum(): lax.dot_general(left_op, right_op, (((0,), (0,)), ((), ())), preferred_el...  98.9 us
    dot_general x5, matrix products, against(): lax.dot_general(left_op, right_op, (((1,), (1,)), ((), ())), preferred_el...  97 us
    ppermute x3, waiting for transfers between devices, line_scatter(): up = lax.ppermute(up, axis, line_pairs(size, stride, 0, s, 1))  86.4 us
    ppermute x4, waiting for transfers between devices, give_back(): lax.ppermute(lax.dynamic_index_in_dim(blocks, lax.rem(local_seq + batch -...  79.8 us
    ppermute x4, waiting for transfers between devices, take_sequence(): lax.ppermute(lax.dynamic_index_in_dim(value, lax.rem(z + k, batch), 0, Fa...  62.1 us
    ppermute x49, starting transfers between devices, swap(): return lax.ppermute(value, axis, [(i, i ^ distance) for i in range(size)])  56.8 us
  transfers between devices with their start and end apart: 78, of which 37 were waited for; matrix products, arithmetic and copies ran while one was open for 33% of the time, Pallas kernels for 6%

profile of v4, /device:TPU:9, one launch (start us, length us, event | category | flops | bytes accessed | tf_op | source)
XLA Modules:
  0.0 1452.9 jit_solution(1346517880075242402)
XLA Ops:
  44.0 39.5 %collective-permute-done.1 = bf16[256,2048]{1,0:T(8,128)(2,1)} collective-permute-done((bf16[256,2048]{1,0:T(8,128)(2,1)}, bf16[256,2048]{1,0:T(8,128)(2,1)}, u32[]{:S(2)}, u32[]{:S(2)}) %collective-permute-start.1) | collective-permute-done | bytes 1048608 | tf_op jit(solution)/shard_map/ppermute | solution.py:548
  136.0 16.1 %collective-permute-done.8 = bf16[512,3072]{1,0:T(8,128)(2,1)} collective-permute-done((bf16[512,3072]{1,0:T(8,128)(2,1)}, bf16[512,3072]{1,0:T(8,128)(2,1)}, u32[]{:S(2)}, u32[]{:S(2)}) %collective-permute-start.8) | collective-permute-done | bytes 3145760 | tf_op jit(solution)/shard_map/ppermute | solution.py:456
  161.4 37.0 %collective-permute-done.10 = bf16[512,3072]{1,0:T(8,128)(2,1)S(1)} collective-permute-done((bf16[512,3072]{1,0:T(8,128)(2,1)S(1)}, bf16[512,3072]{1,0:T(8,128)(2,1)S(1)}, u32[]{:S(2)}, u32[]{:S(2)}) %collective-permute-start.10) | collective-permute-done | bytes 3145760 | tf_op jit(solution)/shard_map/ppermute | solution.py:456
  210.2 19.0 %fusion.16.lin_ref = f32[1024,3072]{1,0:T(8,128)} fusion(bf16[2048,3072]{1,0:T(8,128)(2,1)} %slice_dynamic-update-slice_fusion, bf16[512,2048]{1,0:T(8,128)(2,1)} %get-tuple-element.173, bf16[512,2048]{1,0:T(8,128)(2,1)} %get-tuple-element.172), kind=kOutput, calls=%fused_computation.81 | convolution fusion | flops 12893290496 | bytes 29360128 | tf_op jit(solution)/shard_map/dot_general | solution.py:27
  229.3 35.6 %attend_forward.1 = (bf16[1024,1024]{1,0:T(8,128)(2,1)}, bf16[1024,3072]{1,0:T(8,128)(2,1)}, f32[8,4,512]{2,1,0:T(4,128)}) custom-call(s32[1]{0:T(128)} %collective-permute-done.6.start_ref, f32[1024,3072]{1,0:T(8,128)} %fusion.16.lin_ref, f32[1024,128]{1,0:T(8,128)} %get-tuple-element.221.cos_ref, f32[1024,128]{1,0:T(8,128)} %get-tuple-element.222.sin_ref), custom_call_target="tpu_custom_call" | custom-call | flops 8589934592 | bytes 20971520 | tf_op jit(solution)/shard_map/attend_forward/pallas_call | solution.py:232
  271.0 16.5 %all-gather.9.cloned.1.call-done = bf16[1024,2048]{1,0:T(8,128)(2,1)} async-done(((bf16[256,2048]{1,0:T(8,128)(2,1)}), bf16[1024,2048]{1,0:T(8,128)(2,1)}) %all-gather.9.cloned.1.call-update) | async-done | bytes 4194320 | tf_op jit(solution)/shard_map/all_gather | solution.py:625
  297.6 42.9 %collective-permute-done.21 = bf16[3,2,256,1024]{3,2,1,0:T(8,128)(2,1)} collective-permute-done((bf16[3,2,256,1024]{3,2,1,0:T(8,128)(2,1)}, bf16[3,2,256,1024]{3,2,1,0:T(8,128)(2,1)}, u32[]{:S(2)}, u32[]{:S(2)}) %collective-permute-start.21) | collective-permute-done | bytes 3145760 | tf_op jit(solution)/shard_map/ppermute | solution.py:456
  378.3 23.0 %collective-permute-done.17 = bf16[256,2048]{1,0:T(8,128)(2,1)S(1)} collective-permute-done((bf16[256,2048]{1,0:T(8,128)(2,1)}, bf16[256,2048]{1,0:T(8,128)(2,1)S(1)}, u32[]{:S(2)}, u32[]{:S(2)}) %collective-permute-start.17) | collective-permute-done | bytes 1048608 | tf_op jit(solution)/shard_map/ppermute | solution.py:456
  417.3 31.4 %collective-permute-done.18 = bf16[512,2048]{1,0:T(8,128)(2,1)S(1)} collective-permute-done((bf16[512,2048]{1,0:T(8,128)(2,1)S(1)}, bf16[512,2048]{1,0:T(8,128)(2,1)S(1)}, u32[]{:S(2)}, u32[]{:S(2)}) %collective-permute-start.18) | collective-permute-done | bytes 2097184 | tf_op jit(solution)/shard_map/ppermute | solution.py:456
  456.9 24.7 %fusion.44 = f32[2048,2048]{1,0:T(8,128)} fusion(bf16[2048,2048]{1,0:T(8,128)(2,1)} %all-gather.11.cloned.1.call-done, bf16[2048,2048]{1,0:T(8,128)(2,1)} %param.23), kind=kOutput, calls=%fused_computation.277 | convolution fusion | flops 17179869184 | bytes 33554432 | tf_op jit(solution)/shard_map/dot_general | solution.py:37
  481.6 21.6 %fusion.1 = f32[2048,2048]{1,0:T(8,128)} fusion(bf16[2048,2048]{1,0:T(8,128)(2,1)} %slice_dynamic-update-slice_fusion.4, bf16[2048,1024]{1,0:T(8,128)(2,1)S(1)} %copy-done.31, bf16[2048,1024]{1,0:T(8,128)(2,1)S(1)} %copy-done.30), kind=kOutput, calls=%fused_computation.28 | convolution fusion | flops 17196646400 | bytes 33554432 | tf_op jit(solution)/shard_map/dot_general | solution.py:27
  503.2 35.5 %multiply_convert_fusion = (bf16[2048,2048]{1,0:T(8,128)(2,1)}, bf16[2048,2048]{1,0:T(8,128)(2,1)}, bf16[2048,2048]{1,0:T(8,128)(2,1)}) fusion(f32[2048,2048]{1,0:T(8,128)} %fusion.1, f32[2048,2048]{1,0:T(8,128)} %fusion.44, bf16[2048,2048]{1,0:T(8,128)(2,1)} %slice_dynamic-update-slice_fusion.4, bf16[2048,1024]{1,0:T(8,128)(2,1)} %get-tuple-element.137, ...), kind=kOutput, calls=%fused_computation.1 | convolution fusion | flops 17259560960 | bytes 75497472 | tf_op jit(solution)/shard_map/dot_general | solution.py:27
  538.7 23.9 %convolution_convert_fusion.4 = bf16[2048,2048]{1,0:T(8,128)(2,1)} fusion(bf16[2048,2048]{1,0:T(8,128)(2,1)} %get-tuple-element.73, bf16[2048,2048]{1,0:T(8,128)(2,1)} %all-gather.11.cloned.1.call-done), kind=kOutput, calls=%fused_computation.25 | convolution fusion | flops 17184063488 | bytes 25165824 | tf_op jit(solution)/shard_map/dot_general | solution.py:31
  562.7 24.6 %fusion.2 = f32[2048,2048]{1,0:T(8,128)} fusion(bf16[2048,2048]{1,0:T(8,128)(2,1)} %get-tuple-element.79, bf16[2048,1024]{1,0:T(8,128)(2,1)} %get-tuple-element.137, bf16[2048,1024]{1,0:T(8,128)(2,1)} %get-tuple-element.136), kind=kOutput, calls=%fused_computation.29 | convolution fusion | flops 17196646400 | bytes 33554432 | tf_op jit(solution)/shard_map/dot_general | solution.py:37
  587.3 25.7 %add_convert_fusion = bf16[2048,2048]{1,0:T(8,128)(2,1)} fusion(f32[2048,2048]{1,0:T(8,128)} %fusion.2, bf16[2048,2048]{1,0:T(8,128)(2,1)} %get-tuple-element.77, bf16[2048,1024]{1,0:T(8,128)(2,1)} %get-tuple-element.139, bf16[2048,1024]{1,0:T(8,128)(2,1)} %get-tuple-element.138), kind=kOutput, calls=%fused_computation | convolution fusion | flops 17205035008 | bytes 41943040 | tf_op jit(solution)/shard_map/dot_general | solution.py:37
  612.9 24.0 %convolution_convert_fusion.2 = bf16[2048,2048]{1,0:T(8,128)(2,1)} fusion(bf16[2048,2048]{1,0:T(8,128)(2,1)} %slice_dynamic-update-slice_fusion.4, bf16[2048,2048]{1,0:T(8,128)(2,1)} %get-tuple-element.77), kind=kOutput, calls=%fused_computation.23 | convolution fusion | flops 17184063488 | bytes 25165824 | tf_op jit(solution)/shard_map/dot_general | solution.py:31
  645.4 23.8 %convolution_convert_fusion.1 = bf16[2048,2048]{1,0:T(8,128)(2,1)} fusion(bf16[2048,2048]{1,0:T(8,128)(2,1)} %slice_dynamic-update-slice_fusion.4, bf16[2048,2048]{1,0:T(8,128)(2,1)} %get-tuple-element.79), kind=kOutput, calls=%fused_computation.22 | convolution fusion | flops 17184063488 | bytes 25165824 | tf_op jit(solution)/shard_map/dot_general | solution.py:31
  685.5 42.1 %collective-permute-done.24 = bf16[512,2048]{1,0:T(8,128)(2,1)S(1)} collective-permute-done((bf16[512,2048]{1,0:T(8,128)(2,1)S(1)}, bf16[512,2048]{1,0:T(8,128)(2,1)S(1)}, u32[]{:S(2)}, u32[]{:S(2)}) %collective-permute-start.24) | collective-permute-done | bytes 2097184 | tf_op jit(solution)/shard_map/ppermute | solution.py:456
  732.1 21.4 %convolution_convert_fusion.3 = bf16[2048,2048]{1,0:T(8,128)(2,1)} fusion(bf16[2048,2048]{1,0:T(8,128)(2,1)} %get-tuple-element.73, bf16[2048,2048]{1,0:T(8,128)(2,1)S(1)} %bitcast.199), kind=kOutput, calls=%fused_computation.24 | convolution fusion | flops 17184063488 | bytes 25165824 | tf_op jit(solution)/shard_map/dot_general | solution.py:27
  791.8 27.1 %collective-permute-done.39 = bf16[512,2048]{1,0:T(8,128)(2,1)} collective-permute-done((bf16[512,2048]{1,0:T(8,128)(2,1)}, bf16[512,2048]{1,0:T(8,128)(2,1)}, u32[]{:S(2)}, u32[]{:S(2)}) %collective-permute-start.39) | collective-permute-done | bytes 2097184 | tf_op jit(solution)/shard_map/ppermute | solution.py:456
  832.0 43.7 %attend_backward.1 = bf16[1024,3072]{1,0:T(8,128)(2,1)} custom-call(s32[1]{0:T(128)} %collective-permute-done.6.start_ref, bf16[1024,3072]{1,0:T(8,128)(2,1)} %get-tuple-element.56.qkv_ref, bf16[1024,1024]{1,0:T(8,128)(2,1)} %get-tuple-element.60.out_ref, bf16[1024,1024]{1,0:T(8,128)(2,1)} %fusion.17.grad_ref, f32[8,4,512]{2,1,0:T(4,128)} %get-tuple-element.76.lse_ref, ...), custom_call_target="tpu_custom_call" | custom-call | flops 21474836480 | bytes 16777216 | tf_op jit(solution)/shard_map/attend_backward/pallas_call | solution.py:273
  918.1 19.7 %convolution_convert_fusion = bf16[2048,3072]{1,0:T(8,128)(2,1)} fusion(bf16[1024,3072]{1,0:T(8,128)(2,1)} %attend_backward.1, bf16[512,2048]{1,0:T(8,128)(2,1)} %get-tuple-element.173, bf16[512,2048]{1,0:T(8,128)(2,1)S(1)} %copy-done.38), kind=kOutput, calls=%fused_computation.6 | convolution fusion | flops 12899581952 | bytes 23068672 | tf_op jit(solution)/shard_map/dot_general | solution.py:31
  950.9 16.3 %convolution_convert_fusion.5 = bf16[1024,2048]{1,0:T(8,128)(2,1)} fusion(bf16[1024,3072]{1,0:T(8,128)(2,1)} %attend_backward.1, bf16[2048,3072]{1,0:T(8,128)(2,1)S(1)} %bitcast.162), kind=kOutput, calls=%fused_computation.65 | convolution fusion | flops 12886999040 | bytes 23068672 | tf_op jit(solution)/shard_map/dot_general | solution.py:37
  976.4 36.0 %collective-permute-done.45 = bf16[512,3072]{1,0:T(8,128)(2,1)} collective-permute-done((bf16[512,3072]{1,0:T(8,128)(2,1)}, bf16[512,3072]{1,0:T(8,128)(2,1)}, u32[]{:S(2)}, u32[]{:S(2)}) %collective-permute-start.45) | collective-permute-done | bytes 3145760 | tf_op jit(solution)/shard_map/ppermute | solution.py:456
  1027.7 20.9 %collective-permute-done.46 = bf16[256,3072]{1,0:T(8,128)(2,1)S(1)} collective-permute-done((bf16[256,3072]{1,0:T(8,128)(2,1)S(1)}, bf16[256,3072]{1,0:T(8,128)(2,1)S(1)}, u32[]{:S(2)}, u32[]{:S(2)}) %collective-permute-start.46) | collective-permute-done | bytes 1572896 | tf_op jit(solution)/shard_map/ppermute | solution.py:456
  1056.2 45.1 %collective-permute-done.52 = bf16[128,4096]{1,0:T(8,128)(2,1)} collective-permute-done((bf16[128,4096]{1,0:T(8,128)(2,1)}, bf16[128,4096]{1,0:T(8,128)(2,1)}, u32[]{:S(2)}, u32[]{:S(2)}) %collective-permute-start.52) | collective-permute-done | bytes 1048608 | tf_op jit(solution)/shard_map/ppermute | solution.py:422
  1105.8 41.2 %collective-permute-done.53 = bf16[128,4096]{1,0:T(8,128)(2,1)} collective-permute-done((bf16[128,4096]{1,0:T(8,128)(2,1)}, bf16[128,4096]{1,0:T(8,128)(2,1)}, u32[]{:S(2)}, u32[]{:S(2)}) %collective-permute-start.53) | collective-permute-done | bytes 1048608 | tf_op jit(solution)/shard_map/ppermute | solution.py:422
  1160.6 14.2 collective-permute-done.56
  1210.8 15.2 %collective-permute-done.64 = bf16[128,4096]{1,0:T(8,128)(2,1)S(1)} collective-permute-done((bf16[128,4096]{1,0:T(8,128)(2,1)S(1)}, bf16[128,4096]{1,0:T(8,128)(2,1)S(1)}, u32[]{:S(2)}, u32[]{:S(2)}) %collective-permute-start.64) | collective-permute-done | bytes 1048608 | tf_op jit(solution)/shard_map/ppermute | solution.py:440
  1233.3 14.4 collective-permute-done.65
  1349.3 46.2 %collective-permute-done.44 = bf16[256,2048]{1,0:T(8,128)(2,1)} collective-permute-done((bf16[256,2048]{1,0:T(8,128)(2,1)}, bf16[256,2048]{1,0:T(8,128)(2,1)}, u32[]{:S(2)}, u32[]{:S(2)}) %collective-permute-start.44) | collective-permute-done | bytes 1048608 | tf_op jit(solution)/shard_map/ppermute | solution.py:563
  1402.5 15.4 %collective-permute-done.51 = bf16[256,2048]{1,0:T(8,128)(2,1)} collective-permute-done((bf16[256,2048]{1,0:T(8,128)(2,1)S(1)}, bf16[256,2048]{1,0:T(8,128)(2,1)}, u32[]{:S(2)}, u32[]{:S(2)}) %collective-permute-start.51) | collective-permute-done | bytes 1048608 | tf_op jit(solution)/shard_map/ppermute | solution.py:563
  (448 shorter events, 553.5 us)
Async XLA Ops:
  7.2 280.3 %all-gather.9.cloned.1.call-start = ((), (), s32[]{:S(2)}) async-start(), calls=%async_computation.3 | async-start | bytes 5242880 | tf_op jit(solution)/shard_map/all_gather | solution.py:625
  15.3 68.2 %collective-permute-start.1 = (bf16[256,2048]{1,0:T(8,128)(2,1)}, bf16[256,2048]{1,0:T(8,128)(2,1)}, u32[]{:S(2)}, u32[]{:S(2)}) collective-permute-start(bf16[256,2048]{1,0:T(8,128)(2,1)} %get-tuple-element.190), channel_id=1, source_target_pairs={{0,8},{1,24},{8,0},{9,16},{16,9},{17,25},{24,1},{25,17},{2,10},{3,... | collective-permute-start | bytes 3145736 | tf_op jit(solution)/shard_map/ppermute | solution.py:548
  16.9 77.8 %collective-permute-start.11 = (bf16[256,2048]{1,0:T(8,128)(2,1)}, bf16[256,2048]{1,0:T(8,128)(2,1)}, u32[]{:S(2)}, u32[]{:S(2)}) collective-permute-start(bf16[256,2048]{1,0:T(8,128)(2,1)} %get-tuple-element.195), channel_id=1, source_target_pairs={{0,0},{1,16},{8,8},{9,24},{16,1},{17,17},{24,9},{25,25},{2,2},{3,1... | collective-permute-start | bytes 3145736 | tf_op jit(solution)/shard_map/ppermute | solution.py:548
  21.3 84.8 %collective-permute-start.12 = (bf16[256,2048]{1,0:T(8,128)(2,1)}, bf16[256,2048]{1,0:T(8,128)(2,1)}, u32[]{:S(2)}, u32[]{:S(2)}) collective-permute-start(bf16[256,2048]{1,0:T(8,128)(2,1)} %get-tuple-element.194), channel_id=1, source_target_pairs={{0,8},{1,24},{8,0},{9,16},{16,9},{17,25},{24,1},{25,17},{2,10},{3,... | collective-permute-start | bytes 3145736 | tf_op jit(solution)/shard_map/ppermute | solution.py:548
  42.3 68.8 %collective-permute-start.7 = (bf16[256,3072]{1,0:T(8,128)(2,1)}, bf16[256,3072]{1,0:T(8,128)(2,1)S(1)}, u32[]{:S(2)}, u32[]{:S(2)}) collective-permute-start(bf16[256,3072]{1,0:T(8,128)(2,1)} %get-tuple-element.176), channel_id=1, source_target_pairs={{0,2},{2,0},{4,6},{6,4},{1,3},{3,1},{5,7},{7,5},{8,10},{10,8},{12,... | collective-permute-start | bytes 4718600 | tf_op jit(solution)/shard_map/ppermute | solution.py:456
  42.7 84.1 %collective-permute-start.9 = (bf16[256,3072]{1,0:T(8,128)(2,1)}, bf16[256,3072]{1,0:T(8,128)(2,1)}, u32[]{:S(2)}, u32[]{:S(2)}) collective-permute-start(bf16[256,3072]{1,0:T(8,128)(2,1)} %get-tuple-element.174), channel_id=1, source_target_pairs={{0,4},{2,6},{4,0},{6,2},{1,5},{3,7},{5,1},{7,3},{8,12},{10,14},{12... | collective-permute-start | bytes 4718600 | tf_op jit(solution)/shard_map/ppermute | solution.py:456
  116.7 112.5 %collective-permute-start.6 = (s32[1]{0:T(128)}, s32[1]{0:T(128)}, u32[]{:S(2)}, u32[]{:S(2)}) collective-permute-start(s32[1]{0:T(128)} %dynamic_slice.215), channel_id=1, source_target_pairs={{0,0},{1,16},{8,8},{9,24},{16,1},{17,17},{24,9},{25,25},{2,2},{3,1... | collective-permute-start | bytes 20 | tf_op jit(solution)/shard_map/ppermute | solution.py:599
  129.0 69.4 %collective-permute-start.10 = (bf16[512,3072]{1,0:T(8,128)(2,1)S(1)}, bf16[512,3072]{1,0:T(8,128)(2,1)S(1)}, u32[]{:S(2)}, u32[]{:S(2)}) collective-permute-start(bf16[512,3072]{1,0:T(8,128)(2,1)S(1)} %pad_maximum_fusion.10), channel_id=1, source_target_pairs={{0,2},{2,0},{4,6},{6,4},{1,3},{3,1},{5,7},{7,5},{8,10},{10,8},{12,... | collective-permute-start | bytes 9437192 | tf_op jit(solution)/shard_map/ppermute | solution.py:456
  204.9 60.0 %collective-permute-start.15 = (bf16[2,256,1024]{2,1,0:T(8,128)(2,1)}, bf16[2,256,1024]{2,1,0:T(8,128)(2,1)S(1)}, u32[]{:S(2)}, u32[]{:S(2)}) collective-permute-start(bf16[2,256,1024]{2,1,0:T(8,128)(2,1)} %pad_maximum_fusion.33), channel_id=1, source_target_pairs={{0,6},{2,4},{4,2},{6,0},{1,7},{3,5},{5,3},{7,1},{8,14},{10,12},{12... | collective-permute-start | bytes 3145736 | tf_op jit(solution)/shard_map/ppermute | solution.py:456
  207.1 60.3 %collective-permute-start.14 = (bf16[2,256,1024]{2,1,0:T(8,128)(2,1)}, bf16[2,256,1024]{2,1,0:T(8,128)(2,1)S(1)}, u32[]{:S(2)}, u32[]{:S(2)}) collective-permute-start(bf16[2,256,1024]{2,1,0:T(8,128)(2,1)} %pad_maximum_fusion.32), channel_id=1, source_target_pairs={{0,4},{2,6},{4,0},{6,2},{1,5},{3,7},{5,1},{7,3},{8,12},{10,14},{12... | collective-permute-start | bytes 3145736 | tf_op jit(solution)/shard_map/ppermute | solution.py:456
  209.4 58.0 %collective-permute-start.13 = (bf16[2,256,1024]{2,1,0:T(8,128)(2,1)}, bf16[2,256,1024]{2,1,0:T(8,128)(2,1)}, u32[]{:S(2)}, u32[]{:S(2)}) collective-permute-start(bf16[2,256,1024]{2,1,0:T(8,128)(2,1)} %pad_maximum_fusion.31), channel_id=1, source_target_pairs={{0,2},{2,0},{4,6},{6,4},{1,3},{3,1},{5,7},{7,5},{8,10},{10,8},{12,... | collective-permute-start | bytes 3145736 | tf_op jit(solution)/shard_map/ppermute | solution.py:456
  209.7 247.2 %all-gather.11.cloned.1.call-start = ((), (), s32[]{:S(2)}) async-start(), calls=%async_computation.4 | async-start | bytes 10485760 | tf_op jit(solution)/shard_map/all_gather | solution.py:627
  271.0 69.4 %collective-permute-start.21 = (bf16[3,2,256,1024]{3,2,1,0:T(8,128)(2,1)}, bf16[3,2,256,1024]{3,2,1,0:T(8,128)(2,1)}, u32[]{:S(2)}, u32[]{:S(2)}) collective-permute-start(bf16[3,2,256,1024]{3,2,1,0:T(8,128)(2,1)} %pad_maximum_fusion.11), channel_id=1, source_target_pairs={{0,8},{8,0},{16,24},{24,16},{1,9},{9,1},{17,25},{25,17},{2,10},{10... | collective-permute-start | bytes 9437192 | tf_op jit(solution)/shard_map/ppermute | solution.py:456
  287.5 496.4 %reduce-scatter.8.cloned.1.call-start = ((), (), s32[]{:S(2)}) async-start(), calls=%async_computation.7 | async-start | bytes 9437184 | tf_op jit(solution)/shard_map/reduce_scatter | solution.py:716
  562.6 330.0 %reduce-scatter.4.cloned.1.call-start = ((), (), s32[]{:S(2)}) async-start(), calls=%async_computation.5 | async-start | bytes 9437184 | tf_op jit(solution)/shard_map/reduce_scatter | solution.py:716
  645.4 251.9 %reduce-scatter.6.cloned.1.call-start = ((), (), s32[]{:S(2)}) async-start(), calls=%async_computation.6 | async-start | bytes 9437184 | tf_op jit(solution)/shard_map/reduce_scatter | solution.py:716
  677.7 596.6 %all-gather.17.cloned.1.call-start = ((), (), s32[]{:S(2)}) async-start(), calls=%async_computation.10 | async-start | bytes 9437184 | tf_op jit(solution)/shard_map/all_gather | solution.py:719
  771.4 47.5 %collective-permute-start.39 = (bf16[512,2048]{1,0:T(8,128)(2,1)}, bf16[512,2048]{1,0:T(8,128)(2,1)}, u32[]{:S(2)}, u32[]{:S(2)}) collective-permute-start(bf16[512,2048]{1,0:T(8,128)(2,1)} %pad_maximum_fusion.25), channel_id=1, source_target_pairs={{0,4},{2,6},{4,0},{6,2},{1,5},{3,7},{5,1},{7,3},{8,12},{10,14},{12... | collective-permute-start | bytes 6291464 | tf_op jit(solution)/shard_map/ppermute | solution.py:456
  773.8 49.3 %collective-permute-start.41 = (bf16[512,2048]{1,0:T(8,128)(2,1)}, bf16[512,2048]{1,0:T(8,128)(2,1)}, u32[]{:S(2)}, u32[]{:S(2)}) collective-permute-start(bf16[512,2048]{1,0:T(8,128)(2,1)} %pad_maximum_fusion.26), channel_id=1, source_target_pairs={{0,2},{2,0},{4,6},{6,4},{1,3},{3,1},{5,7},{7,5},{8,10},{10,8},{12,... | collective-permute-start | bytes 6291464 | tf_op jit(solution)/shard_map/ppermute | solution.py:456
  784.0 502.1 %all-gather.15.cloned.1.call-start = ((), (), s32[]{:S(2)}) async-start(), calls=%async_computation.9 | async-start | bytes 9437184 | tf_op jit(solution)/shard_map/all_gather | solution.py:719
  822.7 58.0 %collective-permute-start.40 = (bf16[256,2048]{1,0:T(8,128)(2,1)}, bf16[256,2048]{1,0:T(8,128)(2,1)}, u32[]{:S(2)}, u32[]{:S(2)}) collective-permute-start(bf16[256,2048]{1,0:T(8,128)(2,1)} %slice.351), channel_id=1, source_target_pairs={{0,2},{2,0},{4,6},{6,4},{1,3},{3,1},{5,7},{7,5},{8,10},{10,8},{12,... | collective-permute-start | bytes 3145736 | tf_op jit(solution)/shard_map/ppermute | solution.py:456
  827.0 55.8 %collective-permute-start.42 = (bf16[256,2048]{1,0:T(8,128)(2,1)}, bf16[256,2048]{1,0:T(8,128)(2,1)S(1)}, u32[]{:S(2)}, u32[]{:S(2)}) collective-permute-start(bf16[256,2048]{1,0:T(8,128)(2,1)} %slice.350), channel_id=1, source_target_pairs={{0,4},{2,6},{4,0},{6,2},{1,5},{3,7},{5,1},{7,3},{8,12},{10,14},{12... | collective-permute-start | bytes 3145736 | tf_op jit(solution)/shard_map/ppermute | solution.py:456
  937.8 360.0 %all-gather.13.cloned.1.call-start = ((), (), s32[]{:S(2)}) async-start(), calls=%async_computation.8 | async-start | bytes 9437184 | tf_op jit(solution)/shard_map/all_gather | solution.py:719
  947.6 64.8 %collective-permute-start.45 = (bf16[512,3072]{1,0:T(8,128)(2,1)}, bf16[512,3072]{1,0:T(8,128)(2,1)}, u32[]{:S(2)}, u32[]{:S(2)}) collective-permute-start(bf16[512,3072]{1,0:T(8,128)(2,1)} %pad_maximum_fusion.12), channel_id=1, source_target_pairs={{0,4},{2,6},{4,0},{6,2},{1,5},{3,7},{5,1},{7,3},{8,12},{10,14},{12... | collective-permute-start | bytes 9437192 | tf_op jit(solution)/shard_map/ppermute | solution.py:456
  950.0 67.1 %collective-permute-start.47 = (bf16[512,3072]{1,0:T(8,128)(2,1)}, bf16[512,3072]{1,0:T(8,128)(2,1)}, u32[]{:S(2)}, u32[]{:S(2)}) collective-permute-start(bf16[512,3072]{1,0:T(8,128)(2,1)} %pad_maximum_fusion.13), channel_id=1, source_target_pairs={{0,2},{2,0},{4,6},{6,4},{1,3},{3,1},{5,7},{7,5},{8,10},{10,8},{12,... | collective-permute-start | bytes 9437192 | tf_op jit(solution)/shard_map/ppermute | solution.py:456
  970.5 51.0 %collective-permute-start.49 = (bf16[512,2048]{1,0:T(8,128)(2,1)}, bf16[512,2048]{1,0:T(8,128)(2,1)}, u32[]{:S(2)}, u32[]{:S(2)}) collective-permute-start(bf16[512,2048]{1,0:T(8,128)(2,1)} %constant_dynamic-slice_fusion.1), channel_id=1, source_target_pairs={{0,1},{1,0},{8,9},{9,8},{16,17},{17,16},{24,25},{25,24},{2,3},{3,2... | collective-permute-start | bytes 6291464 | tf_op jit(solution)/shard_map/ppermute | solution.py:456
  1053.3 48.1 %collective-permute-start.52 = (bf16[128,4096]{1,0:T(8,128)(2,1)}, bf16[128,4096]{1,0:T(8,128)(2,1)}, u32[]{:S(2)}, u32[]{:S(2)}) collective-permute-start(bf16[128,4096]{1,0:T(8,128)(2,1)} %get-tuple-element.148), channel_id=1, source_target_pairs={{0,8},{1,9},{2,10},{3,11},{4,12},{5,13},{6,14},{7,15}} | collective-permute-start | bytes 3145736 | tf_op jit(solution)/shard_map/ppermute | solution.py:422
  1054.6 51.2 %collective-permute-start.55 = (bf16[128,4096]{1,0:T(8,128)(2,1)}, bf16[128,4096]{1,0:T(8,128)(2,1)}, u32[]{:S(2)}, u32[]{:S(2)}) collective-permute-start(bf16[128,4096]{1,0:T(8,128)(2,1)} %get-tuple-element.149), channel_id=1, source_target_pairs={{24,16},{25,17},{26,18},{27,19},{28,20},{29,21},{30,22},{31,23}} | collective-permute-start | bytes 3145736 | tf_op jit(solution)/shard_map/ppermute | solution.py:423
  1309.7 118.0 %collective-permute-start.69 = (bf16[512,4096]{1,0:T(8,128)(2,1)}, bf16[512,4096]{1,0:T(8,128)(2,1)}, u32[]{:S(2)}, u32[]{:S(2)}) collective-permute-start(bf16[512,4096]{1,0:T(8,128)(2,1)} %select_dynamic-update-slice_fusion), channel_id=1, source_target_pairs={{0,1},{1,0},{8,9},{9,8},{16,17},{17,16},{24,25},{25,24},{2,3},{3,2... | collective-permute-start | bytes 12582920 | tf_op jit(solution)/shard_map/ppermute | solution.py:456
  1323.0 72.5 %collective-permute-start.44 = (bf16[256,2048]{1,0:T(8,128)(2,1)}, bf16[256,2048]{1,0:T(8,128)(2,1)}, u32[]{:S(2)}, u32[]{:S(2)}) collective-permute-start(bf16[256,2048]{1,0:T(8,128)(2,1)} %get-tuple-element.183), channel_id=1, source_target_pairs={{8,0},{24,1},{0,8},{16,9},{9,16},{25,17},{1,24},{17,25},{10,2},{26... | collective-permute-start | bytes 3145736 | tf_op jit(solution)/shard_map/ppermute | solution.py:563
  1332.4 70.1 %collective-permute-start.50 = (bf16[256,2048]{1,0:T(8,128)(2,1)}, bf16[256,2048]{1,0:T(8,128)(2,1)S(1)}, u32[]{:S(2)}, u32[]{:S(2)}) collective-permute-start(bf16[256,2048]{1,0:T(8,128)(2,1)} %get-tuple-element.180), channel_id=1, source_target_pairs={{0,0},{16,1},{8,8},{24,9},{1,16},{17,17},{9,24},{25,25},{2,2},{18,... | collective-permute-start | bytes 3145736 | tf_op jit(solution)/shard_map/ppermute | solution.py:563
  1335.2 82.7 %collective-permute-start.51 = (bf16[256,2048]{1,0:T(8,128)(2,1)S(1)}, bf16[256,2048]{1,0:T(8,128)(2,1)}, u32[]{:S(2)}, u32[]{:S(2)}) collective-permute-start(bf16[256,2048]{1,0:T(8,128)(2,1)S(1)} %get-tuple-element.179), channel_id=1, source_target_pairs={{8,0},{24,1},{0,8},{16,9},{9,16},{25,17},{1,24},{17,25},{10,2},{26... | collective-permute-start | bytes 3145736 | tf_op jit(solution)/shard_map/ppermute | solution.py:563
  (111 other events, 2844.4 us)
Sparse Core Ops, SparseCore 0:
  209.8 77.6 all-gather.8
  289.4 87.8 all-gather.10
  562.7 93.2 reduce-scatter.7
  658.2 88.1 reduce-scatter.3
  748.5 88.0 reduce-scatter.5
  838.1 79.1 all-gather.16
  937.9 86.4 all-gather.14
  1026.0 118.4 all-gather.12
